TPU v7x, 32 devices: a whole 2x2x4 slice. The times are simulated.
32 devices in a mesh: rep: 8 (over z, y), shard: 4 (over x, core).
Axes of the slice: x: 2, y: 2, z: 4, core: 2. Of those that a mesh axis runs over, the one named last changes fastest.
Arguments:
- tokens: bfloat16 [4096, 1024], P(('rep', 'shard')), may hold values from -6 to 6
- segments: int32 [32, 128], P(('rep', 'shard')), may hold values from 0 to 1, never falling along the last dimension, each value on 1 to 96 neighbouring positions
- out_cot: bfloat16 [4096, 1024], P(('rep', 'shard')), may hold values from -6 to 6
- step_count: int32 [1], replicated, may hold values from 1 to 8
- w_qkv: float32 [1024, 4096], P(('rep', 'shard')), may hold values from -0.1875 to 0.1875
- w_out: float32 [2048, 1024], P(('rep', 'shard')), may hold values from -0.5 to 0.5
- w_gate_up: float32 [1024, 6144], P(('rep', 'shard')), may hold values from -0.1875 to 0.1875
- w_down: float32 [3072, 1024], P(('rep', 'shard')), may hold values from -0.109375 to 0.109375
- norm_gains: float32 [2304], P(('rep', 'shard')), may hold values from 0.5 to 1.5
- mean_qkv: float32 [1024, 4096], P(('rep', 'shard')), may hold values from -0.0625 to 0.0625
- mean_out: float32 [2048, 1024], P(('rep', 'shard')), may hold values from -0.0625 to 0.0625
- mean_gate_up: float32 [1024, 6144], P(('rep', 'shard')), may hold values from -0.0625 to 0.0625
- mean_down: float32 [3072, 1024], P(('rep', 'shard')), may hold values from -0.0625 to 0.0625
- mean_gains: float32 [2304], P(('rep', 'shard')), may hold values from -0.0625 to 0.0625
- square_qkv: float32 [1024, 4096], P(('rep', 'shard')), may hold values from 2.4414062e-06 to 0.00024414062
- square_out: float32 [2048, 1024], P(('rep', 'shard')), may hold values from 2.4414062e-06 to 0.00024414062
- square_gate_up: float32 [1024, 6144], P(('rep', 'shard')), may hold values from 2.4414062e-06 to 0.00024414062
- square_down: float32 [3072, 1024], P(('rep', 'shard')), may hold values from 2.4414062e-06 to 0.00024414062
- square_gains: float32 [2304], P(('rep', 'shard')), may hold values from 2.4414062e-06 to 0.00024414062
Outputs:
- layer_out: bfloat16 [4096, 1024], P(('rep', 'shard'))
- input_grad: float32 [4096, 1024], P(('rep', 'shard'))
- grad_qkv: float32 [1024, 4096], P(('rep', 'shard'))
- grad_out: float32 [2048, 1024], P(('rep', 'shard'))
- grad_gate_up: float32 [1024, 6144], P(('rep', 'shard'))
- grad_down: float32 [3072, 1024], P(('rep', 'shard'))
- grad_gains: float32 [2304], P(('rep', 'shard'))
- new_qkv: float32 [1024, 4096], P(('rep', 'shard'))
- new_out: float32 [2048, 1024], P(('rep', 'shard'))
- new_gate_up: float32 [1024, 6144], P(('rep', 'shard'))
- new_down: float32 [3072, 1024], P(('rep', 'shard'))
- new_gains: float32 [2304], P(('rep', 'shard'))
- new_mean_qkv: float32 [1024, 4096], P(('rep', 'shard'))
- new_mean_out: float32 [2048, 1024], P(('rep', 'shard'))
- new_mean_gate_up: float32 [1024, 6144], P(('rep', 'shard'))
- new_mean_down: float32 [3072, 1024], P(('rep', 'shard'))
- new_mean_gains: float32 [2304], P(('rep', 'shard'))
- new_square_qkv: float32 [1024, 4096], P(('rep', 'shard'))
- new_square_out: float32 [2048, 1024], P(('rep', 'shard'))
- new_square_gate_up: float32 [1024, 6144], P(('rep', 'shard'))
- new_square_down: float32 [3072, 1024], P(('rep', 'shard'))
- new_square_gains: float32 [2304], P(('rep', 'shard'))
Inputs may be any that keep to these rules, and one draw needn't show every extreme that they name: `segments`: segment ids never fall along a row, and each row's longest document has at most 96 positions.
All inputs are finite; a program needn't handle non-finite values.
Results may differ from a plain program's by a relative error of at most 0.013.
The roundings to bfloat16 on the way count: a program that leaves them out, or rounds other values in their place, can miss the bound.
Values may be sent and summed in bfloat16 or wider, within the bound.
No kernel may reach another device: no remote copies, remote signals or barrier semaphores. Data moves between devices by JAX's collectives and lax.ppermute only.
A program may use at most 256 MiB of HBM per device.

v0:
```python
import math

import jax
import jax.numpy as jnp
from jax import lax
from jax.sharding import PartitionSpec as P

D = 1024
QUERY_HEADS = 16
KEY_VALUE_HEADS = 8
HEAD_SIZE = 128
FF = 3072


NORM_EPS = 1e-06
ROPE_BASE = 1000000.0
LEARN_RATE = 0.02
BETA_ONE = 0.9
BETA_TWO = 0.95
ADAM_EPS = 1e-08
DECAY_RATE = 0.1


def batched(pattern, left, right):
    return jnp.einsum(pattern, left, right, preferred_element_type=jnp.float32)


def rms_forward(signal, gain):
    inverse = lax.rsqrt(jnp.mean(signal * signal, axis=-1, keepdims=True) + NORM_EPS)
    return (signal * inverse * gain, inverse)


def rms_backward(signal, inverse, gain, upstream):
    scaled = upstream * gain
    inner = jnp.mean(scaled * signal, axis=-1, keepdims=True)
    d_signal = inverse * (scaled - signal * inverse * inverse * inner)
    d_gain = jnp.sum((upstream * signal * inverse).reshape(-1, signal.shape[-1]), axis=0)
    return (d_signal, d_gain)


def rope_tables(length_per_row, width):
    positions = jnp.arange(length_per_row).astype(jnp.float32)
    freqs = jnp.exp(-math.log(ROPE_BASE) * 2.0 * jnp.arange(width // 2).astype(jnp.float32) / width)
    angles = positions[:, None] * freqs[None, :]
    return (jnp.cos(angles)[:, None, :], jnp.sin(angles)[:, None, :])


def apply_rotation(signal, cosine_table, sine_table):
    half_width = signal.shape[-1] // 2
    front_half = signal[..., :half_width]
    back_half = signal[..., half_width:]
    return jnp.concatenate(
        [
            front_half * cosine_table - back_half * sine_table,
            back_half * cosine_table + front_half * sine_table,
        ],
        axis=-1,
    )


def unrotate(upstream, cosine_table, sine_table):
    half_width = upstream.shape[-1] // 2
    front_half = upstream[..., :half_width]
    back_half = upstream[..., half_width:]
    return jnp.concatenate(
        [
            front_half * cosine_table + back_half * sine_table,
            back_half * cosine_table - front_half * sine_table,
        ],
        axis=-1,
    )


def attention_mask(segment_rows):
    length_per_row = segment_rows.shape[1]
    rows_idx = jnp.arange(length_per_row)[:, None]
    cols_idx = jnp.arange(length_per_row)[None, :]
    causal = (cols_idx <= rows_idx)[None, :, :]
    return causal & (segment_rows[:, :, None] == segment_rows[:, None, :])


def scores_of(rotated_query, k_rot, allowed):
    scores = batched("rikgd,rjkd->rkgij", rotated_query, k_rot)
    return jnp.where(allowed[:, None, None, :, :], scores, -1e30)


def forward_pass(tokens_rows, segment_rows, qkv_bf, output_half, gate_up_bf, down_bf, gain_all):
    total_rows = tokens_rows.shape[0]
    length_per_row = tokens_rows.shape[1]
    flat = total_rows * length_per_row
    head_group = QUERY_HEADS // KEY_VALUE_HEADS
    query_width = QUERY_HEADS * HEAD_SIZE
    key_width = KEY_VALUE_HEADS * HEAD_SIZE
    x_float = tokens_rows.astype(jnp.float32)
    normed_float, inv_attn = rms_forward(x_float, gain_all[:D])
    normed = normed_float.astype(jnp.bfloat16).reshape(flat, D)
    projected_rows = jnp.dot(normed, qkv_bf, preferred_element_type=jnp.float32).reshape(
        total_rows, length_per_row, -1
    )
    queries = projected_rows[..., :query_width].reshape(
        total_rows, length_per_row, QUERY_HEADS, HEAD_SIZE
    )
    unnormed_keys = projected_rows[..., query_width : query_width + key_width].reshape(
        total_rows, length_per_row, KEY_VALUE_HEADS, HEAD_SIZE
    )
    unnormed_values = projected_rows[..., query_width + key_width :].reshape(
        total_rows, length_per_row, KEY_VALUE_HEADS, HEAD_SIZE
    )
    normalized_query, inv_query = rms_forward(queries, gain_all[2 * D : 2 * D + HEAD_SIZE])
    key_normed, inv_key = rms_forward(unnormed_keys, gain_all[2 * D + HEAD_SIZE :])
    cosine_table, sine_table = rope_tables(length_per_row, HEAD_SIZE)
    rotated_query = (
        (apply_rotation(normalized_query, cosine_table, sine_table) * (1.0 / math.sqrt(HEAD_SIZE)))
        .astype(jnp.bfloat16)
        .reshape(total_rows, length_per_row, KEY_VALUE_HEADS, head_group, HEAD_SIZE)
    )
    k_rot = apply_rotation(key_normed, cosine_table, sine_table).astype(jnp.bfloat16)
    v_bf = unnormed_values.astype(jnp.bfloat16)
    allowed = attention_mask(segment_rows)
    scores = scores_of(rotated_query, k_rot, allowed)
    peak = jnp.max(scores, axis=-1, keepdims=True)
    log_total = peak + jnp.log(jnp.sum(jnp.exp(scores - peak), axis=-1, keepdims=True))
    probs_bf = jnp.exp(scores - log_total).astype(jnp.bfloat16)
    attended = batched("rkgij,rjkd->rikgd", probs_bf, v_bf)
    attended_bf = attended.astype(jnp.bfloat16).reshape(flat, query_width)
    x_mid = x_float + jnp.dot(attended_bf, output_half, preferred_element_type=jnp.float32).reshape(
        total_rows, length_per_row, D
    )
    mid_float, inv_mlp = rms_forward(x_mid, gain_all[D : 2 * D])
    mid_normed = mid_float.astype(jnp.bfloat16).reshape(flat, D)
    gated = jnp.dot(mid_normed, gate_up_bf, preferred_element_type=jnp.float32)
    gate_pre = gated[:, :FF]
    up_pre = gated[:, FF:]
    hidden = (jax.nn.silu(gate_pre) * up_pre).astype(jnp.bfloat16)
    layer_rows = (
        x_mid
        + jnp.dot(hidden, down_bf, preferred_element_type=jnp.float32).reshape(
            total_rows, length_per_row, D
        )
    ).astype(jnp.bfloat16)
    saved = {
        "x_float": x_float,
        "inv_attn": inv_attn,
        "normed": normed,
        "queries": queries,
        "keys_raw": unnormed_keys,
        "inv_query": inv_query,
        "inv_key": inv_key,
        "q_rot": rotated_query,
        "k_rot": k_rot,
        "v_bf": v_bf,
        "allowed": allowed,
        "log_total": log_total,
        "attended": attended,
        "attended_bf": attended_bf,
        "x_mid": x_mid,
        "inv_mlp": inv_mlp,
        "mid_normed": mid_normed,
        "gate_pre": gate_pre,
        "up_pre": up_pre,
        "hidden": hidden,
    }
    return (layer_rows, saved)


def ffn_backward(saved, cot_rows, gate_up_bf, down_bf, gain_all):
    total_rows = cot_rows.shape[0]
    length_per_row = cot_rows.shape[1]
    cot_flat = cot_rows.reshape(total_rows * length_per_row, D)
    gate_pre = saved["gate_pre"]
    grad_down = jnp.dot(saved["hidden"].T, cot_flat, preferred_element_type=jnp.float32)
    d_hidden = jnp.dot(cot_flat, down_bf.T, preferred_element_type=jnp.float32)
    sig_gate = jax.nn.sigmoid(gate_pre)
    d_gate = d_hidden * saved["up_pre"] * sig_gate * (1.0 + gate_pre * (1.0 - sig_gate))
    d_upper = d_hidden * gate_pre * sig_gate
    d_gated = jnp.concatenate([d_gate, d_upper], axis=1).astype(jnp.bfloat16)
    grad_gate_up = jnp.dot(saved["mid_normed"].T, d_gated, preferred_element_type=jnp.float32)
    d_mid_norm = jnp.dot(d_gated, gate_up_bf.T, preferred_element_type=jnp.float32).reshape(
        total_rows, length_per_row, D
    )
    d_mid_part, d_mlp_gain = rms_backward(
        saved["x_mid"], saved["inv_mlp"], gain_all[D : 2 * D], d_mid_norm
    )
    return (grad_gate_up, grad_down, cot_rows.astype(jnp.float32) + d_mid_part, d_mlp_gain)


def attn_backward(saved, d_mid, qkv_bf, output_half, gain_all):
    total_rows = d_mid.shape[0]
    length_per_row = d_mid.shape[1]
    flat = total_rows * length_per_row
    head_group = QUERY_HEADS // KEY_VALUE_HEADS
    query_width = QUERY_HEADS * HEAD_SIZE
    key_width = KEY_VALUE_HEADS * HEAD_SIZE
    middle_gradient_half = d_mid.astype(jnp.bfloat16).reshape(flat, D)
    grad_out = jnp.dot(
        saved["attended_bf"].T, middle_gradient_half, preferred_element_type=jnp.float32
    )
    attention_gradient = (
        jnp.dot(middle_gradient_half, output_half.T, preferred_element_type=jnp.float32)
        .astype(jnp.bfloat16)
        .reshape(total_rows, length_per_row, KEY_VALUE_HEADS, head_group, HEAD_SIZE)
    )
    delta = jnp.sum(attention_gradient.astype(jnp.float32) * saved["attended"], axis=-1)
    delta = jnp.transpose(delta, (0, 2, 3, 1))[..., None]
    scores = scores_of(saved["q_rot"], saved["k_rot"], saved["allowed"])
    probs = jnp.exp(scores - saved["log_total"])
    probs_bf = probs.astype(jnp.bfloat16)
    d_probs = batched("rikgd,rjkd->rkgij", attention_gradient, saved["v_bf"])
    d_scores = (probs * (d_probs - delta)).astype(jnp.bfloat16)
    d_values = batched("rkgij,rikgd->rjkd", probs_bf, attention_gradient)
    d_qrot = batched("rkgij,rjkd->rikgd", d_scores, saved["k_rot"]).reshape(
        total_rows, length_per_row, QUERY_HEADS, HEAD_SIZE
    )
    d_krot = batched("rkgij,rikgd->rjkd", d_scores, saved["q_rot"])
    cosine_table, sine_table = rope_tables(length_per_row, HEAD_SIZE)
    d_queries, d_query_gain = rms_backward(
        saved["queries"],
        saved["inv_query"],
        gain_all[2 * D : 2 * D + HEAD_SIZE],
        unrotate(d_qrot * (1.0 / math.sqrt(HEAD_SIZE)), cosine_table, sine_table),
    )
    d_keys, d_key_gain = rms_backward(
        saved["keys_raw"],
        saved["inv_key"],
        gain_all[2 * D + HEAD_SIZE :],
        unrotate(d_krot, cosine_table, sine_table),
    )
    d_projected = jnp.concatenate(
        [
            d_queries.reshape(flat, query_width),
            d_keys.reshape(flat, key_width),
            d_values.reshape(flat, key_width),
        ],
        axis=1,
    ).astype(jnp.bfloat16)
    grad_qkv = jnp.dot(saved["normed"].T, d_projected, preferred_element_type=jnp.float32)
    d_normed = jnp.dot(d_projected, qkv_bf.T, preferred_element_type=jnp.float32).reshape(
        total_rows, length_per_row, D
    )
    d_input_part, d_attn_gain = rms_backward(
        saved["x_float"], saved["inv_attn"], gain_all[:D], d_normed
    )
    return (grad_qkv, grad_out, d_attn_gain, d_query_gain, d_key_gain, d_mid + d_input_part)


def adamw(weight, grad_sum, mean_old, square_old, step_float, token_total, decay):
    gradient = grad_sum / token_total
    mean_new = BETA_ONE * mean_old + (1.0 - BETA_ONE) * gradient
    square_new = BETA_TWO * square_old + (1.0 - BETA_TWO) * gradient * gradient
    fix_one = 1.0 - jnp.power(BETA_ONE, step_float)
    fix_two = 1.0 - jnp.power(BETA_TWO, step_float)
    change = mean_new / fix_one / (jnp.sqrt(square_new / fix_two) + ADAM_EPS) + decay * weight
    return (weight - LEARN_RATE * change, mean_new, square_new)


def body(
    tokens,
    segments,
    out_cot,
    step_count,
    w_qkv,
    w_out,
    w_gate_up,
    w_down,
    norm_gains,
    mean_qkv,
    mean_out,
    mean_gate_up,
    mean_down,
    mean_gains,
    square_qkv,
    square_out,
    square_gate_up,
    square_down,
    square_gains,
):
    length_per_row = tokens.shape[0]
    qkv_part = w_qkv.astype(jnp.bfloat16)
    out_part = w_out.astype(jnp.bfloat16)
    gate_up_part = w_gate_up.astype(jnp.bfloat16)
    down_part = w_down.astype(jnp.bfloat16)
    gains_part = norm_gains.astype(jnp.bfloat16)
    whole = (
        lax.all_gather(qkv_part, ("rep", "shard"), axis=0, tiled=True),
        lax.all_gather(out_part, ("rep", "shard"), axis=0, tiled=True),
        lax.all_gather(gate_up_part, ("rep", "shard"), axis=0, tiled=True),
        lax.all_gather(down_part, ("rep", "shard"), axis=0, tiled=True),
        lax.all_gather(gains_part, ("rep", "shard"), axis=0, tiled=True),
    )
    gain_all = whole[4].astype(jnp.float32)
    layer_rows, saved = forward_pass(
        tokens.reshape(1, length_per_row, D),
        segments,
        whole[0],
        whole[1],
        whole[2],
        whole[3],
        gain_all,
    )
    grad_gate_up, grad_down, d_mid, d_mlp_gain = ffn_backward(
        saved, out_cot.reshape(1, length_per_row, D), whole[2], whole[3], gain_all
    )
    grad_qkv, grad_out, d_attn_gain, d_query_gain, d_key_gain, input_rows = attn_backward(
        saved, d_mid, whole[0], whole[1], gain_all
    )
    grad_gains = jnp.concatenate([d_attn_gain, d_mlp_gain, d_query_gain, d_key_gain])
    sum_qkv, sum_out, sum_gate_up, sum_down, sum_gains = (
        lax.psum_scatter(grad_qkv, ("rep", "shard"), scatter_dimension=0, tiled=True),
        lax.psum_scatter(grad_out, ("rep", "shard"), scatter_dimension=0, tiled=True),
        lax.psum_scatter(grad_gate_up, ("rep", "shard"), scatter_dimension=0, tiled=True),
        lax.psum_scatter(grad_down, ("rep", "shard"), scatter_dimension=0, tiled=True),
        lax.psum_scatter(grad_gains, ("rep", "shard"), scatter_dimension=0, tiled=True),
    )
    token_total = float(length_per_row * lax.axis_size(("rep", "shard")))
    step_float = step_count[0].astype(jnp.float32)
    new_qkv, new_mean_qkv, new_square_qkv = adamw(
        w_qkv, sum_qkv, mean_qkv, square_qkv, step_float, token_total, DECAY_RATE
    )
    new_out, new_mean_out, new_square_out = adamw(
        w_out, sum_out, mean_out, square_out, step_float, token_total, DECAY_RATE
    )
    new_gate_up, new_mean_gate_up, new_square_gate_up = adamw(
        w_gate_up, sum_gate_up, mean_gate_up, square_gate_up, step_float, token_total, DECAY_RATE
    )
    new_down, new_mean_down, new_square_down = adamw(
        w_down, sum_down, mean_down, square_down, step_float, token_total, DECAY_RATE
    )
    new_gains, new_mean_gains, new_square_gains = adamw(
        norm_gains, sum_gains, mean_gains, square_gains, step_float, token_total, 0.0
    )
    layer_out = layer_rows.reshape(length_per_row, D)
    input_grad = input_rows.reshape(length_per_row, D)
    return (
        layer_out,
        input_grad,
        sum_qkv,
        sum_out,
        sum_gate_up,
        sum_down,
        sum_gains,
        new_qkv,
        new_out,
        new_gate_up,
        new_down,
        new_gains,
        new_mean_qkv,
        new_mean_out,
        new_mean_gate_up,
        new_mean_down,
        new_mean_gains,
        new_square_qkv,
        new_square_out,
        new_square_gate_up,
        new_square_down,
        new_square_gains,
    )


def solution(mesh):
    return jax.shard_map(
        body,
        mesh=mesh,
        in_specs=(
            P(("rep", "shard"), None),
            P(("rep", "shard"), None),
            P(("rep", "shard"), None),
            P(),
            P(("rep", "shard"), None),
            P(("rep", "shard"), None),
            P(("rep", "shard"), None),
            P(("rep", "shard"), None),
            P(("rep", "shard")),
            P(("rep", "shard"), None),
            P(("rep", "shard"), None),
            P(("rep", "shard"), None),
            P(("rep", "shard"), None),
            P(("rep", "shard")),
            P(("rep", "shard"), None),
            P(("rep", "shard"), None),
            P(("rep", "shard"), None),
            P(("rep", "shard"), None),
            P(("rep", "shard")),
        ),
        out_specs=(
            P(("rep", "shard"), None),
            P(("rep", "shard"), None),
            P(("rep", "shard"), None),
            P(("rep", "shard"), None),
            P(("rep", "shard"), None),
            P(("rep", "shard"), None),
            P(("rep", "shard")),
            P(("rep", "shard"), None),
            P(("rep", "shard"), None),
            P(("rep", "shard"), None),
            P(("rep", "shard"), None),
            P(("rep", "shard")),
            P(("rep", "shard"), None),
            P(("rep", "shard"), None),
            P(("rep", "shard"), None),
            P(("rep", "shard"), None),
            P(("rep", "shard")),
            P(("rep", "shard"), None),
            P(("rep", "shard"), None),
            P(("rep", "shard"), None),
            P(("rep", "shard"), None),
            P(("rep", "shard")),
        ),
        check_vma=False,
    )
```

profile of v0, /device:TPU:0, one launch (start us, length us, event | category | flops | bytes accessed | tf_op | source)
XLA Modules:
  0.0 1096.2 jit_solution(7142288678782446879)
XLA Ops:
  7.3 1.8 convert_element_type.179
  9.2 1.6 convert_element_type.186
  10.9 1.9 convert_element_type.188
  14.0 42.6 %all-reduce = bf16[2304]{0:T(1024)(128)(2,1)S(1)} all-reduce(bf16[2304]{0:T(1024)(128)(2,1)S(1)} %dynamic-update-slice), channel_id=1, replica_groups=mesh['rep'=8,'shard'=4] {'rep','shard'}, use_global_device_ids=true, to_apply=%add | all-reduce | flops 2304 | bytes 9216
  57.2 34.2 %all-gather.5.cloned.1.call-done = bf16[1024,4096]{1,0:T(8,128)(2,1)} async-done(((bf16[32,4096]{1,0:T(8,128)(2,1)}), bf16[1024,4096]{1,0:T(8,128)(2,1)}) %all-gather.5.cloned.1.call-update) | async-done | bytes 8388624 | tf_op jit(solution)/shard_map/all_gather | solution.py:284
  91.4 4.7 convolution_bitcast_fusion
  96.1 1.4 fusion.63
  99.5 1.3 copy.138
  100.8 1.3 copy.139
  103.6 2.0 fusion.14
  107.5 1.3 fusion.69
  108.8 46.4 %all-gather.7.cloned.1.call-done = bf16[2048,1024]{1,0:T(8,128)(2,1)} async-done(((bf16[64,1024]{1,0:T(8,128)(2,1)}), bf16[2048,1024]{1,0:T(8,128)(2,1)}) %all-gather.7.cloned.1.call-update) | async-done | bytes 4194320 | tf_op jit(solution)/shard_map/all_gather | solution.py:285
  155.2 3.0 multiply_reduce_fusion.3
  158.3 94.4 %all-gather.9.cloned.1.call-done = bf16[1024,6144]{1,0:T(8,128)(2,1)} async-done(((bf16[32,6144]{1,0:T(8,128)(2,1)}), bf16[1024,6144]{1,0:T(8,128)(2,1)}) %all-gather.9.cloned.1.call-update) | async-done | bytes 12582928 | tf_op jit(solution)/shard_map/all_gather | solution.py:286
  252.7 8.1 fusion.62
  260.7 63.0 %all-gather.11.cloned.1.call-done = bf16[3072,1024]{1,0:T(8,128)(2,1)} async-done(((bf16[96,1024]{1,0:T(8,128)(2,1)}), bf16[3072,1024]{1,0:T(8,128)(2,1)}) %all-gather.11.cloned.1.call-update) | async-done | bytes 6291472 | tf_op jit(solution)/shard_map/all_gather | solution.py:287
  323.7 7.8 multiply_convert_fusion.1
  331.5 7.6 multiply_reduce_fusion.1
  339.1 1.5 multiply_add_fusion.7
  340.6 5.5 fusion.50
  347.3 6.4 fusion.70
  355.2 10.5 fusion.17
  367.7 3.8 convolution_convert_fusion
  371.5 1.2 copy.144
  373.0 1.9 multiply_reduce_fusion
  374.9 1.3 fusion.4
  378.6 2.5 copy.181
  381.1 2.4 copy.182
  383.5 1.3 convolution_bitcast_fusion.4
  388.8 2.2 fusion.6
  390.9 1.8 copy.180
  392.8 1.8 multiply_add_fusion
  397.8 1.5 fusion.10
  400.1 8.2 fusion.41
  410.3 2.5 reshape.750
  412.8 2.0 copy_bitcast_fusion
  414.7 1.4 fusion.40
  417.0 6.5 fusion.35
  423.5 40.8 %all-reduce.1 = f32[2304]{0:T(1024)S(1)} all-reduce(f32[2304]{0:T(1024)S(1)} %pad_maximum_fusion.8), channel_id=6, replica_groups=mesh['rep'=8,'shard'=4] {'rep','shard'}, use_global_device_ids=true, to_apply=%region_19.20.clone | all-reduce | flops 2304 | bytes 18432
  466.0 4.6 fusion.5
  470.6 24.5 %reduce-scatter.7.cloned.1.call-done = f32[64,1024]{1,0:T(8,128)} async-done(((f32[2048,1024]{1,0:T(8,128)}), f32[64,1024]{1,0:T(8,128)}) %reduce-scatter.7.cloned.1.call-update) | async-done | bytes 262160 | tf_op jit(solution)/shard_map/reduce_scatter | solution.py:309
  495.1 2.0 multiply_subtract_fusion.6
  497.1 155.2 %reduce-scatter.11.cloned.1.call-done = f32[96,1024]{1,0:T(8,128)} async-done(((f32[3072,1024]{1,0:T(8,128)}), f32[96,1024]{1,0:T(8,128)}) %reduce-scatter.11.cloned.1.call-update) | async-done | bytes 393232 | tf_op jit(solution)/shard_map/reduce_scatter | solution.py:311
  652.3 2.4 multiply_subtract_fusion.5
  654.7 246.5 %reduce-scatter.9.cloned.1.call-done = f32[32,6144]{1,0:T(8,128)} async-done(((f32[1024,6144]{1,0:T(8,128)}), f32[32,6144]{1,0:T(8,128)}) %reduce-scatter.9.cloned.1.call-update) | async-done | bytes 786448 | tf_op jit(solution)/shard_map/reduce_scatter | solution.py:310
  901.3 3.1 multiply_subtract_fusion.2
  904.4 182.2 %reduce-scatter.5.cloned.1.call-done = f32[32,4096]{1,0:T(8,128)} async-done(((f32[1024,4096]{1,0:T(8,128)}), f32[32,4096]{1,0:T(8,128)}) %reduce-scatter.5.cloned.1.call-update) | async-done | bytes 524304 | tf_op jit(solution)/shard_map/reduce_scatter | solution.py:308
  1086.6 2.6 multiply_subtract_fusion.3
  (199 shorter events, 25.8 us)
Async XLA Ops:
  7.2 5.7 copy-start.37
  7.2 6.5 copy-start.59
  7.2 49.4 %copy-start.11 = (bf16[128,1024]{1,0:T(8,128)(2,1)S(1)}, bf16[128,1024]{1,0:T(8,128)(2,1)}, u32[]{:S(2)}) copy-start(bf16[128,1024]{1,0:T(8,128)(2,1)} %param.19) | copy-start | bytes 786436
  7.2 49.6 %copy-start.58 = (s32[1,128]{1,0:T(1,128)S(1)}, s32[1,128]{1,0:T(1,128)}, u32[]{:S(2)}) copy-start(s32[1,128]{1,0:T(1,128)} %param.20) | copy-start | bytes 1540
  7.2 84.2 %all-gather.5.cloned.1.call-start = ((), (), s32[]{:S(2)}) async-start(), calls=%async_computation.4 | async-start | bytes 8650752 | tf_op jit(solution)/shard_map/all_gather | solution.py:284
  9.1 146.1 %all-gather.7.cloned.1.call-start = ((), (), s32[]{:S(2)}) async-start(), calls=%async_computation.5 | async-start | bytes 4325376 | tf_op jit(solution)/shard_map/all_gather | solution.py:285
  10.8 241.8 %all-gather.9.cloned.1.call-start = ((), (), s32[]{:S(2)}) async-start(), calls=%async_computation.6 | async-start | bytes 12976128 | tf_op jit(solution)/shard_map/all_gather | solution.py:286
  12.8 310.9 %all-gather.11.cloned.1.call-start = ((), (), s32[]{:S(2)}) async-start(), calls=%async_computation.7 | async-start | bytes 6488064 | tf_op jit(solution)/shard_map/all_gather | solution.py:287
  13.6 481.5 %reduce-scatter.7.cloned.1.call-start = ((), (), s32[]{:S(2)}) async-start(), calls=%async_computation.9 | async-start | bytes 8650752 | tf_op jit(solution)/shard_map/reduce_scatter | solution.py:309
  56.8 309.0 %copy-start.57 = (f32[128]{0:T(128)}, f32[128]{0:T(128)S(1)}, u32[]{:S(2)}) copy-start(f32[128]{0:T(128)S(1)} %get-tuple-element.66) | copy-start | bytes 1540
  56.8 309.6 %copy-start.55 = (f32[128]{0:T(128)}, f32[128]{0:T(128)S(1)}, u32[]{:S(2)}) copy-start(f32[128]{0:T(128)S(1)} %get-tuple-element.67) | copy-start | bytes 1540
  96.1 7.4 copy-start.7
  103.1 2.7 copy-start.18
  103.6 3.1 copy-start.27
  108.8 151.9 %copy-start.12 = (bf16[1,128,8,2,128]{1,4,3,2,0:T(8,128)(2,1)}, bf16[1,128,8,2,128]{1,4,3,2,0:T(8,128)(2,1)S(1)}, u32[]{:S(2)}) copy-start(bf16[1,128,8,2,128]{1,4,3,2,0:T(8,128)(2,1)S(1)} %get-tuple-element.72) | copy-start | bytes 1572868
  158.2 102.5 %copy-start.3 = (f32[128,1024]{1,0:T(8,128)}, f32[128,1024]{1,0:T(8,128)S(1)}, u32[]{:S(2)}) copy-start(f32[128,1024]{1,0:T(8,128)S(1)} %get-tuple-element.75) | copy-start | bytes 1572868
  323.7 7.8 copy-start
  346.1 306.2 %reduce-scatter.11.cloned.1.call-start = ((), (), s32[]{:S(2)}) async-start(), calls=%async_computation.11 | async-start | bytes 12976128 | tf_op jit(solution)/shard_map/reduce_scatter | solution.py:311
  353.7 547.6 %reduce-scatter.9.cloned.1.call-start = ((), (), s32[]{:S(2)}) async-start(), calls=%async_computation.10 | async-start | bytes 25952256 | tf_op jit(solution)/shard_map/reduce_scatter | solution.py:310
  365.8 720.9 %reduce-scatter.5.cloned.1.call-start = ((), (), s32[]{:S(2)}) async-start(), calls=%async_computation.8 | async-start | bytes 17301504 | tf_op jit(solution)/shard_map/reduce_scatter | solution.py:308
  371.5 3.4 copy-start.2
  373.0 4.5 copy-start.17
  373.0 4.0 copy-start.29
  373.0 4.0 copy-start.31
  377.5 6.0 copy-start.14
  378.6 7.3 copy-start.19
  388.8 5.8 copy-start.6
  390.9 3.6 copy-start.56
  394.5 2.6 copy-start.9
  395.3 2.5 copy-start.52
  397.4 2.7 copy-start.42
  410.3 5.8 copy-start.10
  412.7 3.4 copy-start.21
  412.7 4.2 copy-start.33
  412.7 4.2 copy-start.41
  412.7 4.2 copy-start.43
  417.0 6.5 copy-start.54
  417.0 47.4 %copy-start.60 = (f32[72]{0:T(128)S(1)}, f32[72]{0:T(128)}, u32[]{:S(2)}) copy-start(f32[72]{0:T(128)} %param.27) | copy-start | bytes 868
  417.0 47.4 %copy-start.61 = (f32[72]{0:T(128)S(1)}, f32[72]{0:T(128)}, u32[]{:S(2)}) copy-start(f32[72]{0:T(128)} %param.37) | copy-start | bytes 868
  417.0 47.3 %copy-start.62 = (f32[72]{0:T(128)S(1)}, f32[72]{0:T(128)}, u32[]{:S(2)}) copy-start(f32[72]{0:T(128)} %param.32) | copy-start | bytes 868
  417.0 49.0 %copy-start.23 = (bf16[128,3072]{1,0:T(8,128)(2,1)S(1)}, bf16[128,3072]{1,0:T(8,128)(2,1)}, u32[]{:S(2)}) copy-start(bf16[128,3072]{1,0:T(8,128)(2,1)} %get-tuple-element.48) | copy-start | bytes 2359300
  466.0 29.1 %copy-start.44 = (f32[64,1024]{1,0:T(8,128)S(1)}, f32[64,1024]{1,0:T(8,128)}, u32[]{:S(2)}) copy-start(f32[64,1024]{1,0:T(8,128)} %param.24) | copy-start | bytes 786436
  466.0 29.1 %copy-start.50 = (f32[64,1024]{1,0:T(8,128)S(1)}, f32[64,1024]{1,0:T(8,128)}, u32[]{:S(2)}) copy-start(f32[64,1024]{1,0:T(8,128)} %param.34) | copy-start | bytes 786436
  466.0 186.4 %copy-start.38 = (f32[96,1024]{1,0:T(8,128)S(1)}, f32[96,1024]{1,0:T(8,128)}, u32[]{:S(2)}) copy-start(f32[96,1024]{1,0:T(8,128)} %param.26) | copy-start | bytes 1179652
  470.6 430.7 %copy-start.26 = (f32[32,6144]{1,0:T(8,128)S(1)}, f32[32,6144]{1,0:T(8,128)}, u32[]{:S(2)}) copy-start(f32[32,6144]{1,0:T(8,128)} %param.25) | copy-start | bytes 2359300
  470.6 430.7 %copy-start.47 = (f32[32,6144]{1,0:T(8,128)S(1)}, f32[32,6144]{1,0:T(8,128)}, u32[]{:S(2)}) copy-start(f32[32,6144]{1,0:T(8,128)} %param.35) | copy-start | bytes 2359300
  654.7 431.9 %copy-start.34 = (f32[32,4096]{1,0:T(8,128)S(1)}, f32[32,4096]{1,0:T(8,128)}, u32[]{:S(2)}) copy-start(f32[32,4096]{1,0:T(8,128)} %param.23) | copy-start | bytes 1572868
  654.7 431.9 %copy-start.49 = (f32[32,4096]{1,0:T(8,128)S(1)}, f32[32,4096]{1,0:T(8,128)}, u32[]{:S(2)}) copy-start(f32[32,4096]{1,0:T(8,128)} %param.33) | copy-start | bytes 1572868
  (23 other events, 30.1 us)
Sparse Core Ops, SparseCore 0:
  11.5 79.8 all-gather.4
  94.9 60.3 all-gather.6
  158.7 93.9 all-gather.8
  255.9 67.7 all-gather.10
  346.2 148.7 reduce-scatter.6
  501.5 150.7 reduce-scatter.10
  659.3 241.9 reduce-scatter.8
  904.2 182.4 reduce-scatter.4
where the time goes:
time: 1110 us; the launch traced here: 1100 us
  waiting for transfers between devices  847 us (76%)
  matrix products  83.6 us (8%)
  blocking collectives  83.4 us (8%)
  other arithmetic  33.5 us (3%)
  local copies, waits for them, and re-layouts  32.9 us (3%)
  between operations  15.9 us (1%)
    reduce_scatter x1, waiting for transfers between devices, body(): lax.psum_scatter(grad_gate_up, ('rep', 'shard'), scatter_dimension=0, til...  247 us
    reduce_scatter x1, waiting for transfers between devices, body(): lax.psum_scatter(grad_qkv, ('rep', 'shard'), scatter_dimension=0, tiled=T...  182 us
    reduce_scatter x1, waiting for transfers between devices, body(): lax.psum_scatter(grad_down, ('rep', 'shard'), scatter_dimension=0, tiled=...  155 us
    all_gather x1, waiting for transfers between devices, body(): lax.all_gather(gate_up_part, ('rep', 'shard'), axis=0, tiled=True)  94.4 us
    unnamed x2, blocking collectives  83.4 us
    all_gather x1, waiting for transfers between devices, body(): lax.all_gather(down_part, ('rep', 'shard'), axis=0, tiled=True)  63 us
    all_gather x1, waiting for transfers between devices, body(): lax.all_gather(out_part, ('rep', 'shard'), axis=0, tiled=True)  46.4 us
    all_gather x1, waiting for transfers between devices, body(): lax.all_gather(qkv_part, ('rep', 'shard'), axis=0, tiled=True)  34.2 us
  transfers between devices with their start and end apart: 8, of which 8 were waited for; matrix products, arithmetic and copies ran while one was open for 11% of the time, Pallas kernels for 0%

commit v1 on v0

v1 whole, which is shorter than its diff:
```python
import math

import jax
import jax.numpy as jnp
from jax import lax
from jax.sharding import PartitionSpec as P

D = 1024
QUERY_HEADS = 16
KEY_VALUE_HEADS = 8
HEAD_SIZE = 128
FF = 3072


NORM_EPS = 1e-06
ROPE_BASE = 1000000.0
LEARN_RATE = 0.02
BETA_ONE = 0.9
BETA_TWO = 0.95
ADAM_EPS = 1e-08
DECAY_RATE = 0.1


def batched(pattern, left, right):
    return jnp.einsum(pattern, left, right, preferred_element_type=jnp.float32)


def rms_forward(signal, gain):
    inverse = lax.rsqrt(jnp.mean(signal * signal, axis=-1, keepdims=True) + NORM_EPS)
    return (signal * inverse * gain, inverse)


def rms_backward(signal, inverse, gain, upstream):
    scaled = upstream * gain
    inner = jnp.mean(scaled * signal, axis=-1, keepdims=True)
    d_signal = inverse * (scaled - signal * inverse * inverse * inner)
    d_gain = jnp.sum((upstream * signal * inverse).reshape(-1, signal.shape[-1]), axis=0)
    return (d_signal, d_gain)


def rope_tables(length_per_row, width):
    positions = jnp.arange(length_per_row).astype(jnp.float32)
    freqs = jnp.exp(-math.log(ROPE_BASE) * 2.0 * jnp.arange(width // 2).astype(jnp.float32) / width)
    angles = positions[:, None] * freqs[None, :]
    return (jnp.cos(angles)[:, None, :], jnp.sin(angles)[:, None, :])


def apply_rotation(signal, cosine_table, sine_table):
    half_width = signal.shape[-1] // 2
    front_half = signal[..., :half_width]
    back_half = signal[..., half_width:]
    return jnp.concatenate(
        [
            front_half * cosine_table - back_half * sine_table,
            back_half * cosine_table + front_half * sine_table,
        ],
        axis=-1,
    )


def unrotate(upstream, cosine_table, sine_table):
    half_width = upstream.shape[-1] // 2
    front_half = upstream[..., :half_width]
    back_half = upstream[..., half_width:]
    return jnp.concatenate(
        [
            front_half * cosine_table + back_half * sine_table,
            back_half * cosine_table - front_half * sine_table,
        ],
        axis=-1,
    )


def attention_mask(segment_rows):
    length_per_row = segment_rows.shape[1]
    rows_idx = jnp.arange(length_per_row)[:, None]
    cols_idx = jnp.arange(length_per_row)[None, :]
    causal = (cols_idx <= rows_idx)[None, :, :]
    return causal & (segment_rows[:, :, None] == segment_rows[:, None, :])


def scores_of(rotated_query, k_rot, allowed):
    scores = batched("rikgd,rjkd->rkgij", rotated_query, k_rot)
    return jnp.where(allowed[:, None, None, :, :], scores, -1e30)


def xor_perm(axis_size, bit):
    return [(i, i ^ bit) for i in range(axis_size)]


def group_gather(part):
    far = lax.ppermute(part, "shard", xor_perm(4, 2))
    pair = jnp.stack([part, far])
    near = lax.ppermute(pair, "shard", xor_perm(4, 1))
    return jnp.stack([part, near[0], far, near[1]])


def group_sum(partial):
    near = lax.ppermute(
        jnp.stack([partial[3], partial[1]]).astype(jnp.bfloat16), "shard", xor_perm(4, 1)
    )
    outgoing = (partial[2] + near[0].astype(jnp.float32)).astype(jnp.bfloat16)
    far = lax.ppermute(outgoing, "shard", xor_perm(4, 2))
    return partial[0] + near[1].astype(jnp.float32) + far.astype(jnp.float32)


def after(value, *earlier):
    return lax.optimization_barrier((value,) + earlier)[0]


RING = [(2 * z + y, 2 * ((z + 1) % 4) + y) for z in range(4) for y in range(2)]


def in_order(blocks, z, rows):
    row = jnp.concatenate([blocks[3], blocks[2], blocks[1], blocks[0], blocks[3], blocks[2], blocks[1]])
    return lax.dynamic_slice_in_dim(row, (3 - z) * rows, 4 * rows, axis=0)


def gather_rep(long, wide, ahead=()):
    if lax.axis_size("rep") != 8:
        return tuple(lax.all_gather(x, "rep", axis=0, tiled=True) for x in (long, wide)) + ((),)
    place = lax.axis_index("rep")
    z, even = place // 2, place % 2 == 0
    rows, columns = long.shape
    width = wide.shape[0]
    longs = [after(long, *ahead[:1])] if ahead else [long]
    wide_in = after(wide, *ahead[:1]) if ahead else wide
    longs.append(lax.ppermute(longs[-1], "rep", RING))
    other = lax.ppermute(wide_in, "rep", xor_perm(8, 1))
    wides = [jnp.where(even, jnp.concatenate([wide, other]), jnp.concatenate([other, wide]))]
    for k in range(3):
        if k:
            longs.append(lax.ppermute(longs[-1], "rep", RING))
        wides.append(lax.ppermute(wides[-1], "rep", RING))
    mine = in_order(longs, z, rows)
    other = lax.ppermute(mine, "rep", xor_perm(8, 1))
    mine, other = mine.reshape(4, rows, columns), other.reshape(4, rows, columns)
    both = jnp.stack([jnp.where(even, mine, other), jnp.where(even, other, mine)], axis=1)
    return both.reshape(8 * rows, columns), in_order(wides, z, 2 * width), (longs[1], longs[2], longs[3])


def as_bf(value):
    return value.astype(jnp.bfloat16)


def ring_sum(held, z):
    def entry(back):
        return lax.dynamic_index_in_dim(held, (z + 4 - back) % 4, axis=0, keepdims=False)

    got = lax.ppermute(as_bf(entry(1)), "rep", RING)
    for back in (2, 3):
        got = lax.ppermute(as_bf(entry(back) + got.astype(jnp.float32)), "rep", RING)
    return entry(0) + got.astype(jnp.float32)


def sum_pair_first(partial):
    if lax.axis_size("rep") != 8:
        return lax.psum_scatter(partial, "rep", scatter_dimension=0, tiled=True)
    rows, columns = partial.shape[0] // 8, partial.shape[1]
    place = lax.axis_index("rep")
    z, y = place // 2, place % 2
    blocks = partial.reshape(4, 2, rows, columns)
    outgoing = lax.dynamic_index_in_dim(blocks, 1 - y, axis=1, keepdims=False)
    kept = lax.dynamic_index_in_dim(blocks, y, axis=1, keepdims=False)
    got = lax.ppermute(as_bf(outgoing), "rep", xor_perm(8, 1))
    return ring_sum(kept + got.astype(jnp.float32), z)


def sum_ring_first(partial):
    if lax.axis_size("rep") != 8:
        return lax.psum_scatter(partial, "rep", scatter_dimension=0, tiled=True)
    rows, columns = partial.shape[0] // 8, partial.shape[1]
    place = lax.axis_index("rep")
    z, y = place // 2, place % 2
    pair = ring_sum(partial.reshape(4, 2, rows, columns), z)
    outgoing = lax.dynamic_index_in_dim(pair, 1 - y, axis=0, keepdims=False)
    kept = lax.dynamic_index_in_dim(pair, y, axis=0, keepdims=False)
    return kept + lax.ppermute(as_bf(outgoing), "rep", xor_perm(8, 1)).astype(jnp.float32)


def columns_of(array, widths, index):
    start, parts = 0, []
    for width in widths:
        parts.append(
            lax.dynamic_slice_in_dim(array, start + index * (width // 4), width // 4, axis=1)
        )
        start += width
    return jnp.concatenate(parts, axis=1)


def trade(pieces, mine):
    far = lax.ppermute(jnp.stack([pieces(2), pieces(3)]), "shard", xor_perm(4, 2))
    near = lax.ppermute(jnp.stack([pieces(1), far[1]]), "shard", xor_perm(4, 1))
    return [pieces(0), near[0], far[0], near[1]]


def split_columns(array, widths):
    rows = array.shape[0]
    mine = lax.axis_index("shard")
    result = jnp.zeros((4 * rows, sum(widths) // 4), array.dtype)
    for k, piece in enumerate(trade(lambda k: columns_of(array, widths, mine ^ k), mine)):
        result = lax.dynamic_update_slice_in_dim(result, piece, (mine ^ k) * rows, axis=0)
    return result


def join_columns(array, widths):
    rows = array.shape[0] // 4
    mine = lax.axis_index("shard")
    result = jnp.zeros((rows, sum(widths)), jnp.float32)
    own = lax.dynamic_slice_in_dim(array, mine * rows, rows, axis=0)
    array = as_bf(array)
    got = trade(lambda k: lax.dynamic_slice_in_dim(array, (mine ^ k) * rows, rows, axis=0), mine)
    for k, piece in enumerate([own] + got[1:]):
        piece = piece.astype(jnp.float32)
        start, taken = 0, 0
        for width in widths:
            result = lax.dynamic_update_slice(
                result,
                piece[:, taken : taken + width // 4],
                (0, start + (mine ^ k) * (width // 4)),
            )
            start += width
            taken += width // 4
    return result


def turned(inverse):
    rep, shard = lax.axis_size("rep"), lax.axis_size("shard")
    pairs = [(b, (b % rep) * shard + b // rep) for b in range(rep * shard)]
    return [(b, a) for a, b in pairs] if inverse else pairs


def by_shard(parts, mine):
    swapped = jnp.where(mine % 2 == 0, parts, parts[jnp.array([1, 0, 3, 2])])
    return jnp.where(mine // 2 == 0, swapped, jnp.concatenate([swapped[2:], swapped[:2]]))


def sum_gains(partial):
    rep = lax.axis_size("rep")
    if rep != 8:
        return lax.psum(partial, ("rep", "shard"))
    for axis, size, bit in (("shard", 4, 1), ("shard", 4, 2), ("rep", 8, 1), ("rep", 8, 2), ("rep", 8, 4)):
        partial = partial + lax.ppermute(partial, axis, xor_perm(size, bit))
    return partial


QKV_WIDTHS = (QUERY_HEADS * HEAD_SIZE, KEY_VALUE_HEADS * HEAD_SIZE, KEY_VALUE_HEADS * HEAD_SIZE)
GATE_UP_WIDTHS = (FF, FF)


def dot(left, right):
    return jnp.dot(left, right, preferred_element_type=jnp.float32)


def attention_forward(projected, segment_rows, query_gain, key_gain):
    total_rows, length = segment_rows.shape
    heads, kv_heads = QUERY_HEADS // 4, KEY_VALUE_HEADS // 4
    group = heads // kv_heads
    wide, narrow = heads * HEAD_SIZE, kv_heads * HEAD_SIZE
    rows = projected.reshape(total_rows, length, -1)
    queries = rows[..., :wide].reshape(total_rows, length, heads, HEAD_SIZE)
    keys = rows[..., wide : wide + narrow].reshape(total_rows, length, kv_heads, HEAD_SIZE)
    values = rows[..., wide + narrow :].reshape(total_rows, length, kv_heads, HEAD_SIZE)
    normalized, inv_query = rms_forward(queries, query_gain)
    key_normed, inv_key = rms_forward(keys, key_gain)
    cosine, sine = rope_tables(length, HEAD_SIZE)
    q_rot = (
        (apply_rotation(normalized, cosine, sine) * (1.0 / math.sqrt(HEAD_SIZE)))
        .astype(jnp.bfloat16)
        .reshape(total_rows, length, kv_heads, group, HEAD_SIZE)
    )
    k_rot = apply_rotation(key_normed, cosine, sine).astype(jnp.bfloat16)
    v_bf = values.astype(jnp.bfloat16)
    scores = scores_of(q_rot, k_rot, attention_mask(segment_rows))
    peak = jnp.max(scores, axis=-1, keepdims=True)
    log_total = peak + jnp.log(jnp.sum(jnp.exp(scores - peak), axis=-1, keepdims=True))
    probs = jnp.exp(scores - log_total)
    attended = batched("rkgij,rjkd->rikgd", probs.astype(jnp.bfloat16), v_bf)
    saved = (queries, keys, inv_query, inv_key, q_rot, k_rot, v_bf, probs, attended)
    return attended.astype(jnp.bfloat16).reshape(total_rows * length, wide), saved


def attention_backward(saved, d_att, query_gain, key_gain):
    queries, keys, inv_query, inv_key, q_rot, k_rot, v_bf, probs, attended = saved
    total_rows, length = q_rot.shape[:2]
    d_att = d_att.reshape(q_rot.shape)
    delta = jnp.sum(d_att.astype(jnp.float32) * attended, axis=-1)
    delta = jnp.transpose(delta, (0, 2, 3, 1))[..., None]
    d_probs = batched("rikgd,rjkd->rkgij", d_att, v_bf)
    d_scores = (probs * (d_probs - delta)).astype(jnp.bfloat16)
    d_values = batched("rkgij,rikgd->rjkd", probs.astype(jnp.bfloat16), d_att)
    d_qrot = batched("rkgij,rjkd->rikgd", d_scores, k_rot).reshape(queries.shape)
    d_krot = batched("rkgij,rikgd->rjkd", d_scores, q_rot)
    cosine, sine = rope_tables(length, HEAD_SIZE)
    d_queries, d_query_gain = rms_backward(
        queries, inv_query, query_gain, unrotate(d_qrot * (1.0 / math.sqrt(HEAD_SIZE)), cosine, sine)
    )
    d_keys, d_key_gain = rms_backward(keys, inv_key, key_gain, unrotate(d_krot, cosine, sine))
    flat = total_rows * length
    d_projected = jnp.concatenate(
        [d_queries.reshape(flat, -1), d_keys.reshape(flat, -1), d_values.reshape(flat, -1)], axis=1
    ).astype(jnp.bfloat16)
    return d_projected, d_query_gain, d_key_gain


def adamw(weight, grad_sum, mean_old, square_old, step_float, token_total, decay):
    gradient = grad_sum / token_total
    mean_new = BETA_ONE * mean_old + (1.0 - BETA_ONE) * gradient
    square_new = BETA_TWO * square_old + (1.0 - BETA_TWO) * gradient * gradient
    fix_one = 1.0 - jnp.power(BETA_ONE, step_float)
    fix_two = 1.0 - jnp.power(BETA_TWO, step_float)
    change = mean_new / fix_one / (jnp.sqrt(square_new / fix_two) + ADAM_EPS) + decay * weight
    return (weight - LEARN_RATE * change, mean_new, square_new)


def body(
    tokens,
    segments,
    out_cot,
    step_count,
    w_qkv,
    w_out,
    w_gate_up,
    w_down,
    norm_gains,
    mean_qkv,
    mean_out,
    mean_gate_up,
    mean_down,
    mean_gains,
    square_qkv,
    square_out,
    square_gate_up,
    square_down,
    square_gains,
):
    length = tokens.shape[0]
    bf = jnp.bfloat16
    both = ("rep", "shard")
    mine = lax.axis_index("shard")
    own = norm_gains.shape[0]
    extra = jnp.zeros((16, D), bf)
    extra = lax.dynamic_update_slice(extra, norm_gains.astype(bf)[None], (0, 0))
    extra = lax.dynamic_update_slice(extra, segments.astype(bf), (1, 0))
    group = group_gather(jnp.concatenate([tokens, extra]))
    token_group = group[:, :length].reshape(4 * length, D)
    segment_group = group[:, length + 1, :length]
    gain_row = by_shard(group[:, length, :own], mine).reshape(1, 4 * own)
    split = split_columns(
        jnp.concatenate([w_qkv, w_gate_up], axis=1).astype(bf), QKV_WIDTHS + GATE_UP_WIDTHS
    )
    narrow = sum(QKV_WIDTHS) // 4
    block = jnp.concatenate([split[:, :narrow], jnp.zeros((16, narrow), bf)])
    block = lax.dynamic_update_slice(block, gain_row, (4 * w_qkv.shape[0], 0))
    turn = lax.ppermute(jnp.concatenate([w_out, w_down]).astype(bf), both, turned(False))
    qkv, output, steps = gather_rep(block, turn[: w_out.shape[0]])
    gate_up, down, _ = gather_rep(split[:, narrow:], turn[w_out.shape[0] :], steps)
    qkv = qkv.reshape(-1, 4 * w_qkv.shape[0] + 16, narrow)
    gains = qkv[:, 4 * w_qkv.shape[0], : 4 * own].reshape(-1).astype(jnp.float32)
    qkv = qkv[:, : 4 * w_qkv.shape[0]].reshape(D, narrow)
    cot_group = group_gather(after(out_cot, steps[0]) if steps else out_cot).reshape(4 * length, D)
    attn_gain, mlp_gain = gains[:D], gains[D : 2 * D]
    query_gain, key_gain = gains[2 * D : 2 * D + HEAD_SIZE], gains[2 * D + HEAD_SIZE :]

    x_float = tokens.astype(jnp.float32)
    normed = rms_forward(token_group.astype(jnp.float32), attn_gain)[0].astype(bf)
    inv_attn = rms_forward(x_float, attn_gain)[1]
    attended_bf, saved = attention_forward(dot(normed, qkv), segment_group, query_gain, key_gain)
    x_mid = x_float + group_sum(dot(attended_bf, output).reshape(4, length, D))
    mid_float, inv_mlp = rms_forward(x_mid, mlp_gain)
    mid_normed = group_gather(mid_float.astype(bf)).reshape(4 * length, D)
    gated = dot(mid_normed, gate_up)
    half = gated.shape[1] // 2
    gate_pre, up_pre = gated[:, :half], gated[:, half:]
    hidden = (jax.nn.silu(gate_pre) * up_pre).astype(bf)
    layer_out = (x_mid + group_sum(dot(hidden, down).reshape(4, length, D))).astype(bf)

    sum_down = lax.ppermute(
        sum_ring_first(dot(hidden.T, cot_group)).astype(bf), both, turned(True)
    ).astype(jnp.float32)
    d_hidden = dot(cot_group, down.T)
    sig = jax.nn.sigmoid(gate_pre)
    d_gated = jnp.concatenate(
        [d_hidden * up_pre * sig * (1.0 + gate_pre * (1.0 - sig)), d_hidden * gate_pre * sig], axis=1
    ).astype(bf)
    d_mid_norm = group_sum(dot(d_gated, gate_up.T).reshape(4, length, D))
    d_mid_part, d_mlp_gain = rms_backward(x_mid, inv_mlp, mlp_gain, d_mid_norm)
    d_mid = out_cot.astype(jnp.float32) + d_mid_part
    sum_gate_up = join_columns(sum_pair_first(dot(mid_normed.T, d_gated)), GATE_UP_WIDTHS)
    d_mid_bf = group_gather(d_mid.astype(bf)).reshape(4 * length, D)
    sum_out = lax.ppermute(
        sum_pair_first(dot(attended_bf.T, d_mid_bf)).astype(bf), both, turned(True)
    ).astype(jnp.float32)
    d_att = dot(d_mid_bf, output.T).astype(bf)
    d_projected, d_query_gain, d_key_gain = attention_backward(saved, d_att, query_gain, key_gain)
    cut = d_projected.shape[1] // 2
    grad_qkv = dot(normed.T, d_projected)
    sum_qkv = join_columns(
        jnp.concatenate([sum_pair_first(grad_qkv[:, :cut]), sum_ring_first(grad_qkv[:, cut:])], axis=1),
        QKV_WIDTHS,
    )
    d_normed = group_sum(dot(d_projected, qkv.T).reshape(4, length, D))
    d_input_part, d_attn_gain = rms_backward(x_float, inv_attn, attn_gain, d_normed)
    input_grad = d_mid + d_input_part
    gain_grads = sum_gains(
        jnp.concatenate([d_attn_gain, d_mlp_gain, d_query_gain, d_key_gain]).reshape(-1, 128)
    ).reshape(-1)
    place = lax.axis_index("rep") * 4 + lax.axis_index("shard")
    sum_gain = lax.dynamic_slice_in_dim(gain_grads, place * own, own)

    token_total = float(length * lax.axis_size(both))
    step_float = step_count[0].astype(jnp.float32)
    new_qkv, new_mean_qkv, new_square_qkv = adamw(
        w_qkv, sum_qkv, mean_qkv, square_qkv, step_float, token_total, DECAY_RATE
    )
    new_out, new_mean_out, new_square_out = adamw(
        w_out, sum_out, mean_out, square_out, step_float, token_total, DECAY_RATE
    )
    new_gate_up, new_mean_gate_up, new_square_gate_up = adamw(
        w_gate_up, sum_gate_up, mean_gate_up, square_gate_up, step_float, token_total, DECAY_RATE
    )
    new_down, new_mean_down, new_square_down = adamw(
        w_down, sum_down, mean_down, square_down, step_float, token_total, DECAY_RATE
    )
    new_gains, new_mean_gains, new_square_gains = adamw(
        norm_gains, sum_gain, mean_gains, square_gains, step_float, token_total, 0.0
    )
    return (
        layer_out,
        input_grad,
        sum_qkv,
        sum_out,
        sum_gate_up,
        sum_down,
        sum_gain,
        new_qkv,
        new_out,
        new_gate_up,
        new_down,
        new_gains,
        new_mean_qkv,
        new_mean_out,
        new_mean_gate_up,
        new_mean_down,
        new_mean_gains,
        new_square_qkv,
        new_square_out,
        new_square_gate_up,
        new_square_down,
        new_square_gains,
    )


def solution(mesh):
    return jax.shard_map(
        body,
        mesh=mesh,
        in_specs=(
            P(("rep", "shard"), None),
            P(("rep", "shard"), None),
            P(("rep", "shard"), None),
            P(),
            P(("rep", "shard"), None),
            P(("rep", "shard"), None),
            P(("rep", "shard"), None),
            P(("rep", "shard"), None),
            P(("rep", "shard")),
            P(("rep", "shard"), None),
            P(("rep", "shard"), None),
            P(("rep", "shard"), None),
            P(("rep", "shard"), None),
            P(("rep", "shard")),
            P(("rep", "shard"), None),
            P(("rep", "shard"), None),
            P(("rep", "shard"), None),
            P(("rep", "shard"), None),
            P(("rep", "shard")),
        ),
        out_specs=(
            P(("rep", "shard"), None),
            P(("rep", "shard"), None),
            P(("rep", "shard"), None),
            P(("rep", "shard"), None),
            P(("rep", "shard"), None),
            P(("rep", "shard"), None),
            P(("rep", "shard")),
            P(("rep", "shard"), None),
            P(("rep", "shard"), None),
            P(("rep", "shard"), None),
            P(("rep", "shard"), None),
            P(("rep", "shard")),
            P(("rep", "shard"), None),
            P(("rep", "shard"), None),
            P(("rep", "shard"), None),
            P(("rep", "shard"), None),
            P(("rep", "shard")),
            P(("rep", "shard"), None),
            P(("rep", "shard"), None),
            P(("rep", "shard"), None),
            P(("rep", "shard"), None),
            P(("rep", "shard")),
        ),
        check_vma=False,
    )
```

time: 1110 us -> 413 us (0.37)
  waiting for transfers between devices: 847 us -> 205 us
  blocking collectives: 83.4 us -> 0 us
  matrix products: 83.6 us -> 26.5 us
  starting transfers between devices: 0.33 us -> 45.8 us
  local copies, waits for them, and re-layouts: 32.9 us -> 68 us
  other arithmetic: 33.5 us -> 55.6 us
    reduce_scatter x4 -> x0, waiting for transfers between devices: 608 us -> none  [the longest x1 247 us: body(): lax.psum_scatter(grad_gate_up, ('rep', 'shard'), scatter_dimension=0, til...]
    all_gather x4 -> x0, waiting for transfers between devices: 238 us -> none  [the longest x1 94.4 us: body(): lax.all_gather(gate_up_part, ('rep', 'shard'), axis=0, tiled=True)]
    ppermute x0 -> x66, waiting for transfers between devices: none -> 205 us  [the longest x6 41.4 us: gather_rep(): longs.append(lax.ppermute(longs[-1], 'rep', RING))]
    unnamed x2 -> x0, blocking collectives: 83.4 us -> none
    dot_general x12, matrix products: 76.7 us -> 21.2 us  [dot(): return jnp.dot(left, right, preferred_element_type=jnp.float32)]
    ppermute x0 -> x66, starting transfers between devices: none -> 45.8 us  [the longest x3 5.95 us: trade(): lax.ppermute(jnp.stack([pieces(2), pieces(3)]), 'shard', xor_perm(4, 2))]
    unnamed x134 -> x237, local copies, waits for them, and re-layouts: 13.2 us -> 22.4 us
  transfers between devices with their start and end apart: 8 -> 66, of which waited for: 8 -> 32; matrix products, arithmetic and copies ran while one was open for 11% -> 31% of each run, Pallas kernels for 0% -> 0%
where the time goes in v1:
time: 413 us; the launch traced here: 406 us
  waiting for transfers between devices  205 us (50%)
  local copies, waits for them, and re-layouts  68 us (16%)
  other arithmetic  55.6 us (13%)
  starting transfers between devices  45.8 us (11%)
  matrix products  26.5 us (6%)
  between operations  5.15 us (1%)
    ppermute x6, waiting for transfers between devices, gather_rep(): longs.append(lax.ppermute(longs[-1], 'rep', RING))  41.4 us
    ppermute x6, waiting for transfers between devices, gather_rep(): wides.append(lax.ppermute(wides[-1], 'rep', RING))  37.5 us
    ppermute x5, waiting for transfers between devices, ring_sum(): got = lax.ppermute(as_bf(entry(1)), 'rep', RING)  36 us
    ppermute x3, waiting for transfers between devices, trade(): lax.ppermute(jnp.stack([pieces(2), pieces(3)]), 'shard', xor_perm(4, 2))  33.2 us
    unnamed x237, local copies, waits for them, and re-layouts  22.4 us
    dot_general x12, matrix products, dot(): return jnp.dot(left, right, preferred_element_type=jnp.float32)  21.2 us
    ppermute x10, waiting for transfers between devices, ring_sum(): lax.ppermute(as_bf(entry(back) + got.astype(jnp.float32)), 'rep', RING)  16.2 us
    ppermute x5, waiting for transfers between devices, sum_gains(): partial = partial + lax.ppermute(partial, axis, xor_perm(size, bit))  13.1 us
  transfers between devices with their start and end apart: 66, of which 32 were waited for; matrix products, arithmetic and copies ran while one was open for 31% of the time, Pallas kernels for 0%

profile of v1, /device:TPU:0, one launch (start us, length us, event | category | flops | bytes accessed | tf_op | source)
XLA Modules:
  0.0 406.3 jit_solution(15238901404270026568)
XLA Ops:
  3.9 3.0 collective-permute-start
  10.9 23.5 %collective-permute-done.2 = bf16[2,32,2560]{2,1,0:T(8,128)(2,1)S(1)} collective-permute-done((bf16[2,32,2560]{2,1,0:T(8,128)(2,1)S(1)}, bf16[2,32,2560]{2,1,0:T(8,128)(2,1)S(1)}, u32[]{:S(2)}, u32[]{:S(2)}) %collective-permute-start.2) | collective-permute-done | bytes 327712 | tf_op jit(solution)/shard_map/ppermute | solution.py:192
  38.2 3.1 collective-permute-done.9
  41.6 10.7 %collective-permute-done.10 = bf16[128,1024]{1,0:T(8,128)(2,1)} collective-permute-done((bf16[128,1024]{1,0:T(8,128)(2,1)S(1)}, bf16[128,1024]{1,0:T(8,128)(2,1)}, u32[]{:S(2)}, u32[]{:S(2)}) %collective-permute-start.10) | collective-permute-done | bytes 262176 | tf_op jit(solution)/shard_map/ppermute | solution.py:134
  56.4 7.1 %collective-permute-done.11 = bf16[128,1024]{1,0:T(8,128)(2,1)} collective-permute-done((bf16[128,1024]{1,0:T(8,128)(2,1)}, bf16[128,1024]{1,0:T(8,128)(2,1)}, u32[]{:S(2)}, u32[]{:S(2)}) %collective-permute-start.11) | collective-permute-done | bytes 262176 | tf_op jit(solution)/shard_map/ppermute | solution.py:134
  64.3 5.4 %collective-permute-done.4 = bf16[144,1024]{1,0:T(8,128)(2,1)S(1)} collective-permute-done((bf16[144,1024]{1,0:T(8,128)(2,1)S(1)}, bf16[144,1024]{1,0:T(8,128)(2,1)S(1)}, u32[]{:S(2)}, u32[]{:S(2)}) %collective-permute-start.4) | collective-permute-done | bytes 294944 | tf_op jit(solution)/shard_map/ppermute | solution.py:128
  71.7 3.7 collective-permute-done.12
  78.4 10.1 %collective-permute-done.5 = bf16[144,1024]{1,0:T(8,128)(2,1)S(1)} collective-permute-done((bf16[144,1024]{1,0:T(8,128)(2,1)S(1)}, bf16[144,1024]{1,0:T(8,128)(2,1)S(1)}, u32[]{:S(2)}, u32[]{:S(2)}) %collective-permute-start.5) | collective-permute-done | bytes 294944 | tf_op jit(solution)/shard_map/ppermute | solution.py:133
  90.6 9.5 %collective-permute-done.6 = bf16[144,1024]{1,0:T(8,128)(2,1)S(1)} collective-permute-done((bf16[144,1024]{1,0:T(8,128)(2,1)S(1)}, bf16[144,1024]{1,0:T(8,128)(2,1)S(1)}, u32[]{:S(2)}, u32[]{:S(2)}) %collective-permute-start.6) | collective-permute-done | bytes 294944 | tf_op jit(solution)/shard_map/ppermute | solution.py:133
  100.3 8.3 %collective-permute-done.22 = bf16[192,1024]{1,0:T(8,128)(2,1)S(1)} collective-permute-done((bf16[192,1024]{1,0:T(8,128)(2,1)S(1)}, bf16[192,1024]{1,0:T(8,128)(2,1)S(1)}, u32[]{:S(2)}, u32[]{:S(2)}) %collective-permute-start.22) | collective-permute-done | bytes 393248 | tf_op jit(solution)/shard_map/ppermute | solution.py:134
  108.7 8.3 %collective-permute-done.18 = bf16[128,1536]{1,0:T(8,128)(2,1)S(1)} collective-permute-done((bf16[128,1536]{1,0:T(8,128)(2,1)S(1)}, bf16[128,1536]{1,0:T(8,128)(2,1)S(1)}, u32[]{:S(2)}, u32[]{:S(2)}) %collective-permute-start.18) | collective-permute-done | bytes 393248 | tf_op jit(solution)/shard_map/ppermute | solution.py:133
  119.6 5.9 %collective-permute-done.23 = bf16[192,1024]{1,0:T(8,128)(2,1)S(1)} collective-permute-done((bf16[192,1024]{1,0:T(8,128)(2,1)S(1)}, bf16[192,1024]{1,0:T(8,128)(2,1)S(1)}, u32[]{:S(2)}, u32[]{:S(2)}) %collective-permute-start.23) | collective-permute-done | bytes 393248 | tf_op jit(solution)/shard_map/ppermute | solution.py:134
  125.9 8.0 %collective-permute-done.19 = bf16[128,1536]{1,0:T(8,128)(2,1)S(1)} collective-permute-done((bf16[128,1536]{1,0:T(8,128)(2,1)S(1)}, bf16[128,1536]{1,0:T(8,128)(2,1)S(1)}, u32[]{:S(2)}, u32[]{:S(2)}) %collective-permute-start.19) | collective-permute-done | bytes 393248 | tf_op jit(solution)/shard_map/ppermute | solution.py:133
  140.3 4.9 %collective-permute-done.7 = bf16[576,1024]{1,0:T(8,128)(2,1)S(1)} collective-permute-done((bf16[576,1024]{1,0:T(8,128)(2,1)S(1)}, bf16[576,1024]{1,0:T(8,128)(2,1)S(1)}, u32[]{:S(2)}, u32[]{:S(2)}) %collective-permute-start.7) | collective-permute-done | bytes 1179680 | tf_op jit(solution)/shard_map/ppermute | solution.py:136
  159.6 2.2 copy.264
  161.7 2.0 reshape.517
  163.8 2.1 fusion.144
  173.7 5.2 %collective-permute-done.14 = bf16[128,1024]{1,0:T(8,128)(2,1)S(1)} collective-permute-done((bf16[128,1024]{1,0:T(8,128)(2,1)S(1)}, bf16[128,1024]{1,0:T(8,128)(2,1)S(1)}, u32[]{:S(2)}, u32[]{:S(2)}) %collective-permute-start.14) | collective-permute-done | bytes 262176 | tf_op jit(solution)/shard_map/ppermute | solution.py:103
  189.0 2.1 copy.284
  193.3 2.5 broadcast_select_fusion.1
  201.3 2.3 fusion.146
  205.0 3.1 fusion.145
  209.0 2.3 copy.286
  211.3 2.5 fusion.150
  216.8 2.3 copy.285
  221.7 9.3 %collective-permute-done.56 = bf16[2,96,1024]{2,1,0:T(8,128)(2,1)} collective-permute-done((bf16[2,96,1024]{2,1,0:T(8,128)(2,1)}, bf16[2,96,1024]{2,1,0:T(8,128)(2,1)}, u32[]{:S(2)}, u32[]{:S(2)}) %collective-permute-start.56) | collective-permute-done | bytes 393248 | tf_op jit(solution)/shard_map/ppermute | solution.py:150
  236.8 4.8 %collective-permute-done.26 = bf16[128,1024]{1,0:T(8,128)(2,1)S(1)} collective-permute-done((bf16[128,1024]{1,0:T(8,128)(2,1)S(1)}, bf16[128,1024]{1,0:T(8,128)(2,1)S(1)}, u32[]{:S(2)}, u32[]{:S(2)}) %collective-permute-start.26) | collective-permute-done | bytes 262176 | tf_op jit(solution)/shard_map/ppermute | solution.py:103
  241.7 2.4 fusion.130
  247.3 4.0 collective-permute-done.31
  251.5 5.7 %collective-permute-done.58 = bf16[2,96,1024]{2,1,0:T(8,128)(2,1)S(1)} collective-permute-done((bf16[2,96,1024]{2,1,0:T(8,128)(2,1)S(1)}, bf16[2,96,1024]{2,1,0:T(8,128)(2,1)S(1)}, u32[]{:S(2)}, u32[]{:S(2)}) %collective-permute-start.58) | collective-permute-done | bytes 393248 | tf_op jit(solution)/shard_map/ppermute | solution.py:152
  260.8 4.4 %collective-permute-done.59 = bf16[96,1024]{1,0:T(8,128)(2,1)S(1)} collective-permute-done((bf16[96,1024]{1,0:T(8,128)(2,1)S(1)}, bf16[96,1024]{1,0:T(8,128)(2,1)S(1)}, u32[]{:S(2)}, u32[]{:S(2)}) %collective-permute-start.59) | collective-permute-done | bytes 196640 | tf_op jit(solution)/shard_map/ppermute | solution.py:178
  265.9 3.2 collective-permute-start.60
  287.0 2.4 copy.315
  290.3 2.2 copy.276
  315.5 2.2 multiply_subtract_fusion.5
  317.6 7.7 %collective-permute-done.39 = bf16[2,128,512]{2,1,0:T(8,128)(2,1)S(1)} collective-permute-done((bf16[2,128,512]{2,1,0:T(8,128)(2,1)S(1)}, bf16[2,128,512]{2,1,0:T(8,128)(2,1)S(1)}, u32[]{:S(2)}, u32[]{:S(2)}) %collective-permute-start.39) | collective-permute-done | bytes 262176 | tf_op jit(solution)/shard_map/ppermute | solution.py:150
  328.9 7.5 %collective-permute-done.40 = bf16[2,128,512]{2,1,0:T(8,128)(2,1)S(1)} collective-permute-done((bf16[2,128,512]{2,1,0:T(8,128)(2,1)S(1)}, bf16[2,128,512]{2,1,0:T(8,128)(2,1)S(1)}, u32[]{:S(2)}, u32[]{:S(2)}) %collective-permute-start.40) | collective-permute-done | bytes 262176 | tf_op jit(solution)/shard_map/ppermute | solution.py:152
  336.9 10.8 %collective-permute-done.46 = bf16[64,1024]{1,0:T(8,128)(2,1)S(1)} collective-permute-done((bf16[64,1024]{1,0:T(8,128)(2,1)S(1)}, bf16[64,1024]{1,0:T(8,128)(2,1)S(1)}, u32[]{:S(2)}, u32[]{:S(2)}) %collective-permute-start.46) | collective-permute-done | bytes 131104 | tf_op jit(solution)/shard_map/ppermute | solution.py:150
  347.8 8.2 %collective-permute-done.36 = bf16[128,512]{1,0:T(8,128)(2,1)S(1)} collective-permute-done((bf16[128,512]{1,0:T(8,128)(2,1)S(1)}, bf16[128,512]{1,0:T(8,128)(2,1)S(1)}, u32[]{:S(2)}, u32[]{:S(2)}) %collective-permute-start.36) | collective-permute-done | bytes 131104 | tf_op jit(solution)/shard_map/ppermute | solution.py:150
  359.4 2.3 collective-permute-done.62
  361.7 2.2 collective-permute-done.37
  365.7 3.6 collective-permute-start.64
  369.3 7.8 %collective-permute-done.64 = f32[18,128]{1,0:T(8,128)S(1)} collective-permute-done((f32[18,128]{1,0:T(8,128)S(1)}, f32[18,128]{1,0:T(8,128)S(1)}, u32[]{:S(2)}, u32[]{:S(2)}) %collective-permute-start.64) | collective-permute-done | bytes 9248 | tf_op jit(solution)/shard_map/ppermute | solution.py:243
  378.8 3.0 collective-permute-done.65
  383.5 3.3 collective-permute-start.43
  386.9 5.8 %collective-permute-done.43 = bf16[2,32,1024]{2,1,0:T(8,128)(2,1)S(1)} collective-permute-done((bf16[2,32,1024]{2,1,0:T(8,128)(2,1)S(1)}, bf16[2,32,1024]{2,1,0:T(8,128)(2,1)S(1)}, u32[]{:S(2)}, u32[]{:S(2)}) %collective-permute-start.43) | collective-permute-done | bytes 131104 | tf_op jit(solution)/shard_map/ppermute | solution.py:192
  394.2 2.5 collective-permute-start.54
  398.4 3.9 collective-permute-done.54
  (573 shorter events, 151.8 us)
Async XLA Ops:
  3.9 32.3 %collective-permute-start = (bf16[144,1024]{1,0:T(8,128)(2,1)}, bf16[144,1024]{1,0:T(8,128)(2,1)S(1)}, u32[]{:S(2)}, u32[]{:S(2)}) collective-permute-start(bf16[144,1024]{1,0:T(8,128)(2,1)} %get-tuple-element.122), channel_id=1, source_target_pairs={{0,2},{1,3},{2,0},{3,1},{4,6},{5,7},{6,4},{7,5},{8,10},{9,11},{10,... | collective-permute-start | bytes 884744 | tf_op jit(solution)/shard_map/ppermute | solution.py:92
  9.2 25.3 %collective-permute-start.2 = (bf16[2,32,2560]{2,1,0:T(8,128)(2,1)S(1)}, bf16[2,32,2560]{2,1,0:T(8,128)(2,1)S(1)}, u32[]{:S(2)}, u32[]{:S(2)}) collective-permute-start(bf16[2,32,2560]{2,1,0:T(8,128)(2,1)S(1)} %pad_maximum_fusion.23), channel_id=1, source_target_pairs={{0,2},{1,3},{2,0},{3,1},{4,6},{5,7},{6,4},{7,5},{8,10},{9,11},{10,... | collective-permute-start | bytes 983048 | tf_op jit(solution)/shard_map/ppermute | solution.py:192
  9.6 25.6 %collective-permute-start.8 = (bf16[160,1024]{1,0:T(8,128)(2,1)S(1)}, bf16[160,1024]{1,0:T(8,128)(2,1)S(1)}, u32[]{:S(2)}, u32[]{:S(2)}) collective-permute-start(bf16[160,1024]{1,0:T(8,128)(2,1)S(1)} %pad_maximum_fusion.25), channel_id=1, source_target_pairs={{0,0},{1,4},{2,8},{3,12},{4,16},{5,20},{6,24},{7,28},{8,1},{9,5},{... | collective-permute-start | bytes 983048 | tf_op jit(solution)/shard_map/ppermute | solution.py:355
  36.3 15.9 %collective-permute-start.1 = (bf16[2,144,1024]{2,1,0:T(8,128)(2,1)S(1)}, bf16[2,144,1024]{2,1,0:T(8,128)(2,1)S(1)}, u32[]{:S(2)}, u32[]{:S(2)}) collective-permute-start(bf16[2,144,1024]{2,1,0:T(8,128)(2,1)S(1)} %pad_maximum_fusion.12), channel_id=1, source_target_pairs={{0,1},{1,0},{2,3},{3,2},{4,5},{5,4},{6,7},{7,6},{8,9},{9,8},{10,11... | collective-permute-start | bytes 1769480 | tf_op jit(solution)/shard_map/ppermute | solution.py:94
  41.3 10.9 %collective-permute-start.10 = (bf16[128,1024]{1,0:T(8,128)(2,1)S(1)}, bf16[128,1024]{1,0:T(8,128)(2,1)}, u32[]{:S(2)}, u32[]{:S(2)}) collective-permute-start(bf16[128,1024]{1,0:T(8,128)(2,1)S(1)} %maximum_select_fusion.1), channel_id=1, source_target_pairs={{0,8},{4,12},{8,16},{12,20},{16,24},{20,28},{24,0},{28,4},{1,9},{5... | collective-permute-start | bytes 786440 | tf_op jit(solution)/shard_map/ppermute | solution.py:134
  52.2 11.3 %collective-permute-start.11 = (bf16[128,1024]{1,0:T(8,128)(2,1)}, bf16[128,1024]{1,0:T(8,128)(2,1)}, u32[]{:S(2)}, u32[]{:S(2)}) collective-permute-start(bf16[128,1024]{1,0:T(8,128)(2,1)} %collective-permute-done.10), channel_id=1, source_target_pairs={{0,8},{4,12},{8,16},{12,20},{16,24},{20,28},{24,0},{28,4},{1,9},{5... | collective-permute-start | bytes 786440 | tf_op jit(solution)/shard_map/ppermute | solution.py:134
  55.5 14.2 %collective-permute-start.4 = (bf16[144,1024]{1,0:T(8,128)(2,1)S(1)}, bf16[144,1024]{1,0:T(8,128)(2,1)S(1)}, u32[]{:S(2)}, u32[]{:S(2)}) collective-permute-start(bf16[144,1024]{1,0:T(8,128)(2,1)S(1)} %dynamic_update_slice.87), channel_id=1, source_target_pairs={{0,8},{4,12},{8,16},{12,20},{16,24},{20,28},{24,0},{28,4},{1,9},{5... | collective-permute-start | bytes 884744 | tf_op jit(solution)/shard_map/ppermute | solution.py:128
  63.5 11.8 %collective-permute-start.12 = (bf16[128,1024]{1,0:T(8,128)(2,1)}, bf16[128,1024]{1,0:T(8,128)(2,1)S(1)}, u32[]{:S(2)}, u32[]{:S(2)}) collective-permute-start(bf16[128,1024]{1,0:T(8,128)(2,1)} %collective-permute-done.11), channel_id=1, source_target_pairs={{0,8},{4,12},{8,16},{12,20},{16,24},{20,28},{24,0},{28,4},{1,9},{5... | collective-permute-start | bytes 786440 | tf_op jit(solution)/shard_map/ppermute | solution.py:134
  69.7 19.8 %collective-permute-start.21 = (bf16[96,1024]{1,0:T(8,128)(2,1)}, bf16[96,1024]{1,0:T(8,128)(2,1)S(1)}, u32[]{:S(2)}, u32[]{:S(2)}) collective-permute-start(bf16[96,1024]{1,0:T(8,128)(2,1)} %slice.460), channel_id=1, source_target_pairs={{0,4},{4,0},{8,12},{12,8},{16,20},{20,16},{24,28},{28,24},{1,5},{5... | collective-permute-start | bytes 589832 | tf_op jit(solution)/shard_map/ppermute | solution.py:129
  71.2 18.7 %collective-permute-start.17 = (bf16[128,1536]{1,0:T(8,128)(2,1)S(1)}, bf16[128,1536]{1,0:T(8,128)(2,1)S(1)}, u32[]{:S(2)}, u32[]{:S(2)}) collective-permute-start(bf16[128,1536]{1,0:T(8,128)(2,1)S(1)} %slice.457), channel_id=1, source_target_pairs={{0,8},{4,12},{8,16},{12,20},{16,24},{20,28},{24,0},{28,4},{1,9},{5... | collective-permute-start | bytes 1179656 | tf_op jit(solution)/shard_map/ppermute | solution.py:128
  71.2 18.5 %collective-permute-start.27 = (bf16[128,1024]{1,0:T(8,128)(2,1)S(1)}, bf16[128,1024]{1,0:T(8,128)(2,1)S(1)}, u32[]{:S(2)}, u32[]{:S(2)}) collective-permute-start(bf16[128,1024]{1,0:T(8,128)(2,1)S(1)} %copy-done.29), channel_id=1, source_target_pairs={{0,2},{1,3},{2,0},{3,1},{4,6},{5,7},{6,4},{7,5},{8,10},{9,11},{10,... | collective-permute-start | bytes 786440 | tf_op jit(solution)/shard_map/ppermute | solution.py:92
  71.7 16.8 %collective-permute-start.5 = (bf16[144,1024]{1,0:T(8,128)(2,1)S(1)}, bf16[144,1024]{1,0:T(8,128)(2,1)S(1)}, u32[]{:S(2)}, u32[]{:S(2)}) collective-permute-start(bf16[144,1024]{1,0:T(8,128)(2,1)S(1)} %collective-permute-done.4), channel_id=1, source_target_pairs={{0,8},{4,12},{8,16},{12,20},{16,24},{20,28},{24,0},{28,4},{1,9},{5... | collective-permute-start | bytes 884744 | tf_op jit(solution)/shard_map/ppermute | solution.py:133
  88.5 11.7 %collective-permute-start.6 = (bf16[144,1024]{1,0:T(8,128)(2,1)S(1)}, bf16[144,1024]{1,0:T(8,128)(2,1)S(1)}, u32[]{:S(2)}, u32[]{:S(2)}) collective-permute-start(bf16[144,1024]{1,0:T(8,128)(2,1)S(1)} %collective-permute-done.5), channel_id=1, source_target_pairs={{0,8},{4,12},{8,16},{12,20},{16,24},{20,28},{24,0},{28,4},{1,9},{5... | collective-permute-start | bytes 884744 | tf_op jit(solution)/shard_map/ppermute | solution.py:133
  89.6 19.0 %collective-permute-start.22 = (bf16[192,1024]{1,0:T(8,128)(2,1)S(1)}, bf16[192,1024]{1,0:T(8,128)(2,1)S(1)}, u32[]{:S(2)}, u32[]{:S(2)}) collective-permute-start(bf16[192,1024]{1,0:T(8,128)(2,1)S(1)} %maximum_select_fusion), channel_id=1, source_target_pairs={{0,8},{4,12},{8,16},{12,20},{16,24},{20,28},{24,0},{28,4},{1,9},{5... | collective-permute-start | bytes 1179656 | tf_op jit(solution)/shard_map/ppermute | solution.py:134
  89.8 28.6 %collective-permute-start.28 = (bf16[2,128,1024]{2,1,0:T(8,128)(2,1)S(1)}, bf16[2,128,1024]{2,1,0:T(8,128)(2,1)S(1)}, u32[]{:S(2)}, u32[]{:S(2)}) collective-permute-start(bf16[2,128,1024]{2,1,0:T(8,128)(2,1)S(1)} %pad_maximum_fusion.16), channel_id=1, source_target_pairs={{0,1},{1,0},{2,3},{3,2},{4,5},{5,4},{6,7},{7,6},{8,9},{9,8},{10,11... | collective-permute-start | bytes 1572872 | tf_op jit(solution)/shard_map/ppermute | solution.py:94
  89.9 27.2 %collective-permute-start.18 = (bf16[128,1536]{1,0:T(8,128)(2,1)S(1)}, bf16[128,1536]{1,0:T(8,128)(2,1)S(1)}, u32[]{:S(2)}, u32[]{:S(2)}) collective-permute-start(bf16[128,1536]{1,0:T(8,128)(2,1)S(1)} %collective-permute-done.17), channel_id=1, source_target_pairs={{0,8},{4,12},{8,16},{12,20},{16,24},{20,28},{24,0},{28,4},{1,9},{5... | collective-permute-start | bytes 1179656 | tf_op jit(solution)/shard_map/ppermute | solution.py:133
  108.6 16.9 %collective-permute-start.23 = (bf16[192,1024]{1,0:T(8,128)(2,1)S(1)}, bf16[192,1024]{1,0:T(8,128)(2,1)S(1)}, u32[]{:S(2)}, u32[]{:S(2)}) collective-permute-start(bf16[192,1024]{1,0:T(8,128)(2,1)S(1)} %collective-permute-done.22), channel_id=1, source_target_pairs={{0,8},{4,12},{8,16},{12,20},{16,24},{20,28},{24,0},{28,4},{1,9},{5... | collective-permute-start | bytes 1179656 | tf_op jit(solution)/shard_map/ppermute | solution.py:134
  117.0 16.9 %collective-permute-start.19 = (bf16[128,1536]{1,0:T(8,128)(2,1)S(1)}, bf16[128,1536]{1,0:T(8,128)(2,1)S(1)}, u32[]{:S(2)}, u32[]{:S(2)}) collective-permute-start(bf16[128,1536]{1,0:T(8,128)(2,1)S(1)} %collective-permute-done.18), channel_id=1, source_target_pairs={{0,8},{4,12},{8,16},{12,20},{16,24},{20,28},{24,0},{28,4},{1,9},{5... | collective-permute-start | bytes 1179656 | tf_op jit(solution)/shard_map/ppermute | solution.py:133
  117.1 28.1 %collective-permute-start.7 = (bf16[576,1024]{1,0:T(8,128)(2,1)S(1)}, bf16[576,1024]{1,0:T(8,128)(2,1)S(1)}, u32[]{:S(2)}, u32[]{:S(2)}) collective-permute-start(bf16[576,1024]{1,0:T(8,128)(2,1)S(1)} %constant_dynamic-slice_fusion.1), channel_id=1, source_target_pairs={{0,4},{4,0},{8,12},{12,8},{16,20},{20,16},{24,28},{28,24},{1,5},{5... | collective-permute-start | bytes 3538952 | tf_op jit(solution)/shard_map/ppermute | solution.py:136
  125.5 13.2 %collective-permute-start.24 = (bf16[192,1024]{1,0:T(8,128)(2,1)S(1)}, bf16[192,1024]{1,0:T(8,128)(2,1)S(1)}, u32[]{:S(2)}, u32[]{:S(2)}) collective-permute-start(bf16[192,1024]{1,0:T(8,128)(2,1)S(1)} %collective-permute-done.23), channel_id=1, source_target_pairs={{0,8},{4,12},{8,16},{12,20},{16,24},{20,28},{24,0},{28,4},{1,9},{5... | collective-permute-start | bytes 1179656 | tf_op jit(solution)/shard_map/ppermute | solution.py:134
  135.6 57.8 %collective-permute-start.20 = (bf16[512,1536]{1,0:T(8,128)(2,1)}, bf16[512,1536]{1,0:T(8,128)(2,1)}, u32[]{:S(2)}, u32[]{:S(2)}) collective-permute-start(bf16[512,1536]{1,0:T(8,128)(2,1)} %constant_dynamic-slice_fusion), channel_id=1, source_target_pairs={{0,4},{4,0},{8,12},{12,8},{16,20},{20,16},{24,28},{28,24},{1,5},{5... | collective-permute-start | bytes 4718600 | tf_op jit(solution)/shard_map/ppermute | solution.py:136
  181.3 11.0 %collective-permute-start.15 = (bf16[128,1024]{1,0:T(8,128)(2,1)}, bf16[128,1024]{1,0:T(8,128)(2,1)}, u32[]{:S(2)}, u32[]{:S(2)}) collective-permute-start(bf16[128,1024]{1,0:T(8,128)(2,1)} %multiply_convert_fusion.5), channel_id=1, source_target_pairs={{0,2},{1,3},{2,0},{3,1},{4,6},{5,7},{6,4},{7,5},{8,10},{9,11},{10,... | collective-permute-start | bytes 786440 | tf_op jit(solution)/shard_map/ppermute | solution.py:92
  204.5 27.9 %collective-permute-start.25 = (bf16[2,128,1024]{2,1,0:T(8,128)(2,1)}, bf16[2,128,1024]{2,1,0:T(8,128)(2,1)}, u32[]{:S(2)}, u32[]{:S(2)}) collective-permute-start(bf16[2,128,1024]{2,1,0:T(8,128)(2,1)} %pad_maximum_fusion.15), channel_id=1, source_target_pairs={{0,1},{1,0},{2,3},{3,2},{4,5},{5,4},{6,7},{7,6},{8,9},{9,8},{10,11... | collective-permute-start | bytes 1572872 | tf_op jit(solution)/shard_map/ppermute | solution.py:99
  209.0 10.1 %collective-permute-start.29 = (bf16[2,128,1024]{2,1,0:T(8,128)(2,1)}, bf16[2,128,1024]{2,1,0:T(8,128)(2,1)}, u32[]{:S(2)}, u32[]{:S(2)}) collective-permute-start(bf16[2,128,1024]{2,1,0:T(8,128)(2,1)} %pad_maximum_fusion.17), channel_id=1, source_target_pairs={{0,1},{1,0},{2,3},{3,2},{4,5},{5,4},{6,7},{7,6},{8,9},{9,8},{10,11... | collective-permute-start | bytes 1572872 | tf_op jit(solution)/shard_map/ppermute | solution.py:99
  216.3 14.8 %collective-permute-start.56 = (bf16[2,96,1024]{2,1,0:T(8,128)(2,1)}, bf16[2,96,1024]{2,1,0:T(8,128)(2,1)}, u32[]{:S(2)}, u32[]{:S(2)}) collective-permute-start(bf16[2,96,1024]{2,1,0:T(8,128)(2,1)} %fusion.69), channel_id=1, source_target_pairs={{0,8},{4,12},{8,16},{12,20},{16,24},{20,28},{24,0},{28,4},{1,9},{5... | collective-permute-start | bytes 1179656 | tf_op jit(solution)/shard_map/ppermute | solution.py:150
  220.4 14.3 %collective-permute-start.30 = (bf16[128,1024]{1,0:T(8,128)(2,1)S(1)}, bf16[128,1024]{1,0:T(8,128)(2,1)S(1)}, u32[]{:S(2)}, u32[]{:S(2)}) collective-permute-start(bf16[128,1024]{1,0:T(8,128)(2,1)S(1)} %fusion.54), channel_id=1, source_target_pairs={{0,2},{1,3},{2,0},{3,1},{4,6},{5,7},{6,4},{7,5},{8,10},{9,11},{10,... | collective-permute-start | bytes 786440 | tf_op jit(solution)/shard_map/ppermute | solution.py:103
  232.4 12.9 %collective-permute-start.57 = (bf16[2,96,1024]{2,1,0:T(8,128)(2,1)S(1)}, bf16[2,96,1024]{2,1,0:T(8,128)(2,1)S(1)}, u32[]{:S(2)}, u32[]{:S(2)}) collective-permute-start(bf16[2,96,1024]{2,1,0:T(8,128)(2,1)S(1)} %fusion.30), channel_id=1, source_target_pairs={{0,8},{4,12},{8,16},{12,20},{16,24},{20,28},{24,0},{28,4},{1,9},{5... | collective-permute-start | bytes 1179656 | tf_op jit(solution)/shard_map/ppermute | solution.py:152
  245.4 11.8 %collective-permute-start.58 = (bf16[2,96,1024]{2,1,0:T(8,128)(2,1)S(1)}, bf16[2,96,1024]{2,1,0:T(8,128)(2,1)S(1)}, u32[]{:S(2)}, u32[]{:S(2)}) collective-permute-start(bf16[2,96,1024]{2,1,0:T(8,128)(2,1)S(1)} %fusion.31), channel_id=1, source_target_pairs={{0,8},{4,12},{8,16},{12,20},{16,24},{20,28},{24,0},{28,4},{1,9},{5... | collective-permute-start | bytes 1179656 | tf_op jit(solution)/shard_map/ppermute | solution.py:152
  251.4 17.7 %collective-permute-start.32 = (bf16[2,128,1024]{2,1,0:T(8,128)(2,1)S(1)}, bf16[2,128,1024]{2,1,0:T(8,128)(2,1)S(1)}, u32[]{:S(2)}, u32[]{:S(2)}) collective-permute-start(bf16[2,128,1024]{2,1,0:T(8,128)(2,1)S(1)} %pad_maximum_fusion.18), channel_id=1, source_target_pairs={{0,1},{1,0},{2,3},{3,2},{4,5},{5,4},{6,7},{7,6},{8,9},{9,8},{10,11... | collective-permute-start | bytes 1572872 | tf_op jit(solution)/shard_map/ppermute | solution.py:94
  259.8 43.8 %collective-permute-start.50 = (bf16[4,128,1536]{2,1,0:T(8,128)(2,1)}, bf16[4,128,1536]{2,1,0:T(8,128)(2,1)}, u32[]{:S(2)}, u32[]{:S(2)}) collective-permute-start(bf16[4,128,1536]{2,1,0:T(8,128)(2,1)} %fusion.2), channel_id=1, source_target_pairs={{0,4},{4,0},{8,12},{12,8},{16,20},{20,16},{24,28},{28,24},{1,5},{5... | collective-permute-start | bytes 4718600 | tf_op jit(solution)/shard_map/ppermute | solution.py:165
  265.9 47.8 %collective-permute-start.60 = (bf16[96,1024]{1,0:T(8,128)(2,1)}, bf16[96,1024]{1,0:T(8,128)(2,1)}, u32[]{:S(2)}, u32[]{:S(2)}) collective-permute-start(bf16[96,1024]{1,0:T(8,128)(2,1)} %fusion.70), channel_id=1, source_target_pairs={{0,0},{4,1},{8,2},{12,3},{16,4},{20,5},{24,6},{28,7},{1,8},{5,9},{... | collective-permute-start | bytes 589832 | tf_op jit(solution)/shard_map/ppermute | solution.py:378
  303.6 22.7 %collective-permute-start.33 = (bf16[2,128,1024]{2,1,0:T(8,128)(2,1)S(1)}, bf16[2,128,1024]{2,1,0:T(8,128)(2,1)S(1)}, u32[]{:S(2)}, u32[]{:S(2)}) collective-permute-start(bf16[2,128,1024]{2,1,0:T(8,128)(2,1)S(1)} %pad_maximum_fusion.20), channel_id=1, source_target_pairs={{0,1},{1,0},{2,3},{3,2},{4,5},{5,4},{6,7},{7,6},{8,9},{9,8},{10,11... | collective-permute-start | bytes 1572872 | tf_op jit(solution)/shard_map/ppermute | solution.py:99
  306.1 19.4 %collective-permute-start.51 = (bf16[128,1536]{1,0:T(8,128)(2,1)S(1)}, bf16[128,1536]{1,0:T(8,128)(2,1)S(1)}, u32[]{:S(2)}, u32[]{:S(2)}) collective-permute-start(bf16[128,1536]{1,0:T(8,128)(2,1)S(1)} %fusion.68), channel_id=1, source_target_pairs={{0,8},{4,12},{8,16},{12,20},{16,24},{20,28},{24,0},{28,4},{1,9},{5... | collective-permute-start | bytes 1179656 | tf_op jit(solution)/shard_map/ppermute | solution.py:150
  308.9 18.3 %collective-permute-start.45 = (bf16[4,64,1024]{2,1,0:T(8,128)(2,1)S(1)}, bf16[4,64,1024]{2,1,0:T(8,128)(2,1)S(1)}, u32[]{:S(2)}, u32[]{:S(2)}) collective-permute-start(bf16[4,64,1024]{2,1,0:T(8,128)(2,1)S(1)} %fusion.48), channel_id=1, source_target_pairs={{0,4},{4,0},{8,12},{12,8},{16,20},{20,16},{24,28},{28,24},{1,5},{5... | collective-permute-start | bytes 1572872 | tf_op jit(solution)/shard_map/ppermute | solution.py:165
  311.2 14.1 %collective-permute-start.39 = (bf16[2,128,512]{2,1,0:T(8,128)(2,1)S(1)}, bf16[2,128,512]{2,1,0:T(8,128)(2,1)S(1)}, u32[]{:S(2)}, u32[]{:S(2)}) collective-permute-start(bf16[2,128,512]{2,1,0:T(8,128)(2,1)S(1)} %fusion.71), channel_id=1, source_target_pairs={{0,8},{4,12},{8,16},{12,20},{16,24},{20,28},{24,0},{28,4},{1,9},{5... | collective-permute-start | bytes 786440 | tf_op jit(solution)/shard_map/ppermute | solution.py:150
  313.7 22.9 %collective-permute-start.35 = (bf16[4,128,512]{2,1,0:T(8,128)(2,1)S(1)}, bf16[4,128,512]{2,1,0:T(8,128)(2,1)S(1)}, u32[]{:S(2)}, u32[]{:S(2)}) collective-permute-start(bf16[4,128,512]{2,1,0:T(8,128)(2,1)S(1)} %fusion.49), channel_id=1, source_target_pairs={{0,4},{4,0},{8,12},{12,8},{16,20},{20,16},{24,28},{28,24},{1,5},{5... | collective-permute-start | bytes 1572872 | tf_op jit(solution)/shard_map/ppermute | solution.py:165
  325.4 11.0 %collective-permute-start.40 = (bf16[2,128,512]{2,1,0:T(8,128)(2,1)S(1)}, bf16[2,128,512]{2,1,0:T(8,128)(2,1)S(1)}, u32[]{:S(2)}, u32[]{:S(2)}) collective-permute-start(bf16[2,128,512]{2,1,0:T(8,128)(2,1)S(1)} %fusion.64), channel_id=1, source_target_pairs={{0,8},{4,12},{8,16},{12,20},{16,24},{20,28},{24,0},{28,4},{1,9},{5... | collective-permute-start | bytes 786440 | tf_op jit(solution)/shard_map/ppermute | solution.py:152
  325.6 30.9 %collective-permute-start.52 = (bf16[128,1536]{1,0:T(8,128)(2,1)S(1)}, bf16[128,1536]{1,0:T(8,128)(2,1)S(1)}, u32[]{:S(2)}, u32[]{:S(2)}) collective-permute-start(bf16[128,1536]{1,0:T(8,128)(2,1)S(1)} %fusion.32), channel_id=1, source_target_pairs={{0,8},{4,12},{8,16},{12,20},{16,24},{20,28},{24,0},{28,4},{1,9},{5... | collective-permute-start | bytes 1179656 | tf_op jit(solution)/shard_map/ppermute | solution.py:152
  326.3 29.8 %collective-permute-start.34 = (bf16[128,1024]{1,0:T(8,128)(2,1)S(1)}, bf16[128,1024]{1,0:T(8,128)(2,1)S(1)}, u32[]{:S(2)}, u32[]{:S(2)}) collective-permute-start(bf16[128,1024]{1,0:T(8,128)(2,1)S(1)} %fusion.52), channel_id=1, source_target_pairs={{0,2},{1,3},{2,0},{3,1},{4,6},{5,7},{6,4},{7,5},{8,10},{9,11},{10,... | collective-permute-start | bytes 786440 | tf_op jit(solution)/shard_map/ppermute | solution.py:103
  327.4 20.3 %collective-permute-start.46 = (bf16[64,1024]{1,0:T(8,128)(2,1)S(1)}, bf16[64,1024]{1,0:T(8,128)(2,1)S(1)}, u32[]{:S(2)}, u32[]{:S(2)}) collective-permute-start(bf16[64,1024]{1,0:T(8,128)(2,1)S(1)} %fusion.87), channel_id=1, source_target_pairs={{0,8},{4,12},{8,16},{12,20},{16,24},{20,28},{24,0},{28,4},{1,9},{5... | collective-permute-start | bytes 393224 | tf_op jit(solution)/shard_map/ppermute | solution.py:150
  336.6 21.2 %collective-permute-start.41 = (bf16[2,128,512]{2,1,0:T(8,128)(2,1)S(1)}, bf16[2,128,512]{2,1,0:T(8,128)(2,1)S(1)}, u32[]{:S(2)}, u32[]{:S(2)}) collective-permute-start(bf16[2,128,512]{2,1,0:T(8,128)(2,1)S(1)} %fusion.65), channel_id=1, source_target_pairs={{0,8},{4,12},{8,16},{12,20},{16,24},{20,28},{24,0},{28,4},{1,9},{5... | collective-permute-start | bytes 786440 | tf_op jit(solution)/shard_map/ppermute | solution.py:152
  336.9 19.1 %collective-permute-start.36 = (bf16[128,512]{1,0:T(8,128)(2,1)S(1)}, bf16[128,512]{1,0:T(8,128)(2,1)S(1)}, u32[]{:S(2)}, u32[]{:S(2)}) collective-permute-start(bf16[128,512]{1,0:T(8,128)(2,1)S(1)} %fusion.85), channel_id=1, source_target_pairs={{0,8},{4,12},{8,16},{12,20},{16,24},{20,28},{24,0},{28,4},{1,9},{5... | collective-permute-start | bytes 393224 | tf_op jit(solution)/shard_map/ppermute | solution.py:150
  356.6 37.4 %collective-permute-start.53 = (bf16[128,1536]{1,0:T(8,128)(2,1)S(1)}, bf16[128,1536]{1,0:T(8,128)(2,1)S(1)}, u32[]{:S(2)}, u32[]{:S(2)}) collective-permute-start(bf16[128,1536]{1,0:T(8,128)(2,1)S(1)} %fusion.33), channel_id=1, source_target_pairs={{0,8},{4,12},{8,16},{12,20},{16,24},{20,28},{24,0},{28,4},{1,9},{5... | collective-permute-start | bytes 1179656 | tf_op jit(solution)/shard_map/ppermute | solution.py:152
  357.5 25.1 %collective-permute-start.48 = (bf16[64,1024]{1,0:T(8,128)(2,1)S(1)}, bf16[64,1024]{1,0:T(8,128)(2,1)S(1)}, u32[]{:S(2)}, u32[]{:S(2)}) collective-permute-start(bf16[64,1024]{1,0:T(8,128)(2,1)S(1)} %fusion.73), channel_id=1, source_target_pairs={{0,8},{4,12},{8,16},{12,20},{16,24},{20,28},{24,0},{28,4},{1,9},{5... | collective-permute-start | bytes 393224 | tf_op jit(solution)/shard_map/ppermute | solution.py:152
  359.3 23.1 %collective-permute-start.42 = (bf16[128,512]{1,0:T(8,128)(2,1)S(1)}, bf16[128,512]{1,0:T(8,128)(2,1)S(1)}, u32[]{:S(2)}, u32[]{:S(2)}) collective-permute-start(bf16[128,512]{1,0:T(8,128)(2,1)S(1)} %fusion.86), channel_id=1, source_target_pairs={{0,4},{4,0},{8,12},{12,8},{16,20},{20,16},{24,28},{28,24},{1,5},{5... | collective-permute-start | bytes 393224 | tf_op jit(solution)/shard_map/ppermute | solution.py:178
  364.0 18.5 %collective-permute-start.38 = (bf16[128,512]{1,0:T(8,128)(2,1)S(1)}, bf16[128,512]{1,0:T(8,128)(2,1)S(1)}, u32[]{:S(2)}, u32[]{:S(2)}) collective-permute-start(bf16[128,512]{1,0:T(8,128)(2,1)S(1)} %fusion.76), channel_id=1, source_target_pairs={{0,8},{4,12},{8,16},{12,20},{16,24},{20,28},{24,0},{28,4},{1,9},{5... | collective-permute-start | bytes 393224 | tf_op jit(solution)/shard_map/ppermute | solution.py:152
  365.7 11.4 %collective-permute-start.64 = (f32[18,128]{1,0:T(8,128)S(1)}, f32[18,128]{1,0:T(8,128)S(1)}, u32[]{:S(2)}, u32[]{:S(2)}) collective-permute-start(f32[18,128]{1,0:T(8,128)S(1)} %add.829), channel_id=1, source_target_pairs={{0,8},{4,12},{8,0},{12,4},{16,24},{20,28},{24,16},{28,20},{1,9},{5... | collective-permute-start | bytes 27656 | tf_op jit(solution)/shard_map/ppermute | solution.py:243
  382.6 10.2 %collective-permute-start.49 = (bf16[64,1024]{1,0:T(8,128)(2,1)S(1)}, bf16[64,1024]{1,0:T(8,128)(2,1)S(1)}, u32[]{:S(2)}, u32[]{:S(2)}) collective-permute-start(bf16[64,1024]{1,0:T(8,128)(2,1)S(1)} %fusion.74), channel_id=1, source_target_pairs={{0,0},{4,1},{8,2},{12,3},{16,4},{20,5},{24,6},{28,7},{1,8},{5,9},{... | collective-permute-start | bytes 393224 | tf_op jit(solution)/shard_map/ppermute | solution.py:391
  (122 other events, 803.2 us)

commit v2 on v1

v2 whole, which is shorter than its diff:
```python
import math

import jax
import jax.numpy as jnp
import numpy as np
from jax import lax
from jax.experimental import pallas as pl
from jax.experimental.pallas import tpu as pltpu
from jax.sharding import PartitionSpec as P

D = 1024
QUERY_HEADS = 16
KEY_VALUE_HEADS = 8
HEAD_SIZE = 128
FF = 3072


NORM_EPS = 1e-06
ROPE_BASE = 1000000.0
LEARN_RATE = 0.02
BETA_ONE = 0.9
BETA_TWO = 0.95
ADAM_EPS = 1e-08
DECAY_RATE = 0.1


def rms_forward(signal, gain):
    inverse = lax.rsqrt(jnp.mean(signal * signal, axis=-1, keepdims=True) + NORM_EPS)
    return (signal * inverse * gain, inverse)


def rms_backward(signal, inverse, gain, upstream):
    scaled = upstream * gain
    inner = jnp.mean(scaled * signal, axis=-1, keepdims=True)
    d_signal = inverse * (scaled - signal * inverse * inverse * inner)
    d_gain = jnp.sum((upstream * signal * inverse).reshape(-1, signal.shape[-1]), axis=0)
    return (d_signal, d_gain)


def xor_perm(axis_size, bit):
    return [(i, i ^ bit) for i in range(axis_size)]


def group_gather(part):
    near = lax.ppermute(part, "shard", xor_perm(4, 1))
    far = lax.ppermute(part, "shard", xor_perm(4, 2))
    return part, near, far, lax.ppermute(far, "shard", xor_perm(4, 1))


def group_sum(send, keep):
    near = lax.ppermute(send, "shard", xor_perm(4, 1))
    far = lax.ppermute(as_bf(keep[1] + near[0].astype(jnp.float32)), "shard", xor_perm(4, 2))
    return keep[0] + near[1].astype(jnp.float32) + far.astype(jnp.float32)


def after(value, *earlier):
    if not earlier:
        return value
    return lax.optimization_barrier((value,) + earlier)[0]


RING = [(2 * z + y, 2 * ((z + 1) % 4) + y) for z in range(4) for y in range(2)]


def in_order(blocks, z, rows):
    row = jnp.concatenate([blocks[3], blocks[2], blocks[1], blocks[0], blocks[3], blocks[2], blocks[1]])
    return lax.dynamic_slice_in_dim(row, (3 - z) * rows, 4 * rows, axis=0)


ORDER = (
    ("q", "z"), ("k", "y"), ("o", "z"), ("u", "y"), ("d", "z"), ("k", "z"), ("q", "z"), ("o", "z"),
    ("k", "z"), ("q", "z"), ("d", "z"), ("o", "z"), ("k", "z"), ("q", "y"), ("d", "z"), ("o", "y"),
    ("g", "z"), ("u", "z"), ("d", "y"), ("g", "z"), ("u", "z"), ("g", "z"), ("u", "z"), ("g", "y"),
)
WINDOW = 6


def gather_rep(blocks):
    if lax.axis_size("rep") != 8:
        return {n: lax.all_gather(x, "rep", axis=0, tiled=True) for n, x in blocks.items()}, {}
    place = lax.axis_index("rep")
    z, even = place // 2, place % 2 == 0
    chain = {name: [block] for name, block in blocks.items()}
    result, steps, named = {}, [], {}
    for index, (name, kind) in enumerate(ORDER):
        held = chain[name]
        rows, columns = blocks[name].shape
        if kind == "z":
            value, pairs = held[-1], RING
        else:
            value = in_order(held, z, rows) if len(held) == 4 else held[0]
            pairs = xor_perm(8, 1)
        if index >= WINDOW:
            value = after(value, *steps[max(0, index - WINDOW - 2) : index - WINDOW + 1])
        got = lax.ppermute(value, "rep", pairs)
        steps.append(got)
        named[name, kind, len(held)] = got
        if kind == "z":
            held.append(got)
            if len(held) == 4 and held[0].shape[0] == 2 * rows:
                result[name] = in_order(held, z, 2 * rows)
        elif len(held) == 4:
            value, got = value.reshape(4, rows, columns), got.reshape(4, rows, columns)
            both = [jnp.where(even, value, got), jnp.where(even, got, value)]
            result[name] = jnp.stack(both, axis=1).reshape(8 * rows, columns)
        else:
            chain[name] = [
                jnp.where(even, jnp.concatenate([value, got]), jnp.concatenate([got, value]))
            ]
    return result, named


def as_bf(value):
    return value.astype(jnp.bfloat16)


class RepSum:
    def __init__(self, partial, ring_first):
        self.count = 0
        self.whole = lax.axis_size("rep") != 8
        if self.whole:
            self.total = lax.psum_scatter(partial, "rep", scatter_dimension=0, tiled=True)
            return
        rows, columns = partial.shape[0] // 8, partial.shape[1]
        place = lax.axis_index("rep")
        self.z, self.y = place // 2, place % 2
        self.kinds = "zzzy" if ring_first else "yzzz"
        self.held = partial.reshape(4, 2, rows, columns)
        self.axis, self.got = 1, None

    def entry(self, back):
        return lax.dynamic_index_in_dim(self.held, (self.z + 4 - back) % 4, axis=0, keepdims=False)

    def step(self, *ahead):
        if self.whole:
            return self.total
        kind = self.kinds[self.count]
        if kind == "z":
            back = self.kinds[: self.count].count("z") + 1
            value = self.entry(back)
            if back > 1:
                value = value + self.got.astype(jnp.float32)
            self.got = lax.ppermute(after(as_bf(value), *ahead), "rep", RING)
            came = self.got
            if back == 3:
                self.held = self.entry(0) + self.got.astype(jnp.float32)
                self.axis = 0
        else:
            value = lax.dynamic_index_in_dim(self.held, 1 - self.y, axis=self.axis, keepdims=False)
            came = lax.ppermute(after(as_bf(value), *ahead), "rep", xor_perm(8, 1))
            kept = lax.dynamic_index_in_dim(self.held, self.y, axis=self.axis, keepdims=False)
            self.held = kept + came.astype(jnp.float32)
        self.count += 1
        self.total = self.held
        return came


def columns_of(array, widths, index):
    start, parts = 0, []
    for width in widths:
        parts.append(
            lax.dynamic_slice_in_dim(array, start + index * (width // 4), width // 4, axis=1)
        )
        start += width
    return jnp.concatenate(parts, axis=1)


def trade(pieces):
    return [pieces(0)] + [lax.ppermute(pieces(k), "shard", xor_perm(4, k)) for k in (1, 2, 3)]


def arrange(parts, mine):
    odd, high = mine % 2 == 1, mine // 2 == 1
    a, b, c, d = parts
    a, b, c, d = (
        jnp.where(odd, b, a),
        jnp.where(odd, a, b),
        jnp.where(odd, d, c),
        jnp.where(odd, c, d),
    )
    return [jnp.where(high, c, a), jnp.where(high, d, b), jnp.where(high, a, c), jnp.where(high, b, d)]


def split_columns(array, widths, extra=None, ahead=()):
    mine = lax.axis_index("shard")

    def pieces(k):
        piece = columns_of(array, widths, mine ^ k)
        if extra is not None:
            piece = jnp.concatenate([piece, extra], axis=1)
        return after(piece, *ahead) if k else piece

    parts = trade(pieces)
    return jnp.concatenate(arrange(parts, mine)), parts[3]


def join_columns(array, widths, gains=None):
    rows = array.shape[0] // 4
    mine = lax.axis_index("shard")

    def pieces(k):
        piece = lax.dynamic_slice_in_dim(array, (mine ^ k) * rows, rows, axis=0)
        if gains is not None:
            row = lax.dynamic_slice_in_dim(gains, mine ^ k, 1, axis=0)
            row = jnp.pad(row, ((0, 15), (0, piece.shape[1] - row.shape[1])))
            piece = jnp.concatenate([piece, row])
        return as_bf(piece) if k else piece

    parts = [piece.astype(jnp.float32) for piece in trade(pieces)]
    columns, start = [], 0
    ordered = arrange([part[:rows] for part in parts], mine)
    for width in widths:
        columns += [part[:, start : start + width // 4] for part in ordered]
        start += width // 4
    joined = jnp.concatenate(columns, axis=1)
    if gains is None:
        return joined
    return joined, sum(part[rows, : gains.shape[1]] for part in parts)


def turned(inverse):
    rep, shard = lax.axis_size("rep"), lax.axis_size("shard")
    pairs = [(b, (b % rep) * shard + b // rep) for b in range(rep * shard)]
    return [(b, a) for a, b in pairs] if inverse else pairs


QKV_WIDTHS = (QUERY_HEADS * HEAD_SIZE, KEY_VALUE_HEADS * HEAD_SIZE, KEY_VALUE_HEADS * HEAD_SIZE)
GATE_UP_WIDTHS = (FF, FF)


def dot(left, right):
    return jnp.dot(left, right, preferred_element_type=jnp.float32)


def dot_t(left, right):
    return lax.dot_general(left, right, (((1,), (1,)), ((), ())), preferred_element_type=jnp.float32)


def t_dot(left, right):
    return lax.dot_general(left, right, (((0,), (0,)), ((), ())), preferred_element_type=jnp.float32)


def inverse_rms(signal):
    return lax.rsqrt(jnp.mean(signal * signal, axis=-1, keepdims=True) + NORM_EPS)


def turn_tables(length):
    half = HEAD_SIZE // 2
    freqs = np.exp(-math.log(ROPE_BASE) * 2.0 * np.arange(half) / HEAD_SIZE).astype(np.float32)
    angles = (np.arange(length, dtype=np.float32)[:, None] * freqs[None, :]).astype(np.float64)
    cosine, sine = np.cos(angles), np.sin(angles)
    return (
        jnp.asarray(np.concatenate([cosine, cosine], 1), jnp.float32),
        jnp.asarray(np.concatenate([-sine, sine], 1), jnp.float32),
    )


def swap_halves(signal):
    return pltpu.roll(signal, HEAD_SIZE // 2, 1)


def allowed_pairs(segment_row):
    length = segment_row.shape[1]
    across = jnp.broadcast_to(segment_row, (length, length))
    rows = lax.broadcasted_iota(jnp.int32, (length, length), 0)
    columns = lax.broadcasted_iota(jnp.int32, (length, length), 1)
    return (columns <= rows) & (across == across.T)


KV_LOCAL = KEY_VALUE_HEADS // 4
GROUP = QUERY_HEADS // KEY_VALUE_HEADS
SCALE = 1.0 / math.sqrt(HEAD_SIZE)


def head_columns(head):
    return slice(head * HEAD_SIZE, (head + 1) * HEAD_SIZE)


def rotate_key(kv_ref, rows, head, gain, cosine, sine):
    keys = kv_ref[rows, head_columns(head)]
    inverse = inverse_rms(keys)
    normed = keys * inverse * gain
    k_rot = as_bf(normed * cosine + swap_halves(normed) * sine)
    return keys, inverse, k_rot, as_bf(kv_ref[rows, head_columns(KV_LOCAL + head)])


def rotate_query(q_ref, rows, head, gain, cosine, sine):
    queries = q_ref[rows, head_columns(head)]
    inverse = inverse_rms(queries)
    normed = queries * inverse * gain
    return queries, inverse, as_bf((normed * cosine + swap_halves(normed) * sine) * SCALE)


def probabilities(q_rot, k_rot, allowed):
    scores = jnp.where(allowed, dot_t(q_rot, k_rot), -1e30)
    peak = jnp.max(scores, axis=-1, keepdims=True)
    log_total = peak + jnp.log(jnp.sum(jnp.exp(scores - peak), axis=-1, keepdims=True))
    return jnp.exp(scores - log_total)


def block_rows(index, length):
    return pl.ds(pl.multiple_of(index * length, length), length)


def emit_partial(partial, send_ref, keep_ref):
    length = send_ref.shape[1]
    keep_ref[0] = partial[:length]
    keep_ref[1] = partial[2 * length : 3 * length]
    send_ref[0] = as_bf(partial[3 * length :])
    send_ref[1] = as_bf(partial[length : 2 * length])


def attention_kernel(
    tok0, tok1, tok2, tok3, seg_ref, gain_ref, cos_ref, sin_ref, wq_ref, wk_ref, wo_ref,
    normed_ref, q_ref, kv_ref, att_ref, send_ref, keep_ref,
):
    length = send_ref.shape[1]
    attn_gain = gain_ref[:, :D]
    query_gain = gain_ref[:, 2 * D : 2 * D + HEAD_SIZE]
    key_gain = gain_ref[:, 2 * D + HEAD_SIZE :]
    for k, ref in enumerate((tok0, tok1, tok2, tok3)):
        tokens = ref[:length].astype(jnp.float32)
        normed_ref[k * length : (k + 1) * length] = as_bf(tokens * inverse_rms(tokens) * attn_gain)
    q_ref[...] = dot(normed_ref[...], wq_ref[...])
    kv_ref[...] = dot(normed_ref[...], wk_ref[:, : kv_ref.shape[1]])

    def one_row(row, carry):
        rows = block_rows(row, length)
        cosine, sine = cos_ref[...], sin_ref[...]
        allowed = allowed_pairs(seg_ref[pl.ds(row, 1), :])
        for c in range(KV_LOCAL):
            _, _, k_rot, v_bf = rotate_key(kv_ref, rows, c, key_gain, cosine, sine)
            for head in range(c * GROUP, (c + 1) * GROUP):
                _, _, q_rot = rotate_query(q_ref, rows, head, query_gain, cosine, sine)
                probs = as_bf(probabilities(q_rot, k_rot, allowed))
                att_ref[rows, head_columns(head)] = as_bf(dot(probs, v_bf))
        return carry

    lax.fori_loop(0, 4, one_row, 0)
    emit_partial(dot(att_ref[...], wo_ref[...]), send_ref, keep_ref)


def attention_back_kernel(
    dmid_ref, tok0, tok1, tok2, tok3, seg_ref, gain_ref, cos_ref, sin_ref, q_ref, kv_ref, wq_ref, wk_ref,
    wo_ref, dq_ref, dkv_ref, dgain_ref, dattn_ref, send_ref, keep_ref, datt_ref,
):
    length = send_ref.shape[1]
    query_gain = gain_ref[:, 2 * D : 2 * D + HEAD_SIZE]
    key_gain = gain_ref[:, 2 * D + HEAD_SIZE :]
    datt_ref[...] = as_bf(dot_t(dmid_ref[...], wo_ref[...]))

    def one_row(row, carry):
        d_query_gain, d_key_gain = carry
        rows = block_rows(row, length)
        cosine, sine = cos_ref[...], sin_ref[...]
        allowed = allowed_pairs(seg_ref[pl.ds(row, 1), :])
        for c in range(KV_LOCAL):
            keys, inv_key, k_rot, v_bf = rotate_key(kv_ref, rows, c, key_gain, cosine, sine)
            d_values = jnp.zeros((length, HEAD_SIZE), jnp.float32)
            d_krot = jnp.zeros((length, HEAD_SIZE), jnp.float32)
            for head in range(c * GROUP, (c + 1) * GROUP):
                queries, inv_query, q_rot = rotate_query(q_ref, rows, head, query_gain, cosine, sine)
                probs = probabilities(q_rot, k_rot, allowed)
                probs_bf = as_bf(probs)
                d_att = datt_ref[rows, head_columns(head)]
                attended = dot(probs_bf, v_bf)
                delta = jnp.sum(d_att.astype(jnp.float32) * attended, axis=-1, keepdims=True)
                d_scores = as_bf(probs * (dot_t(d_att, v_bf) - delta))
                d_values = d_values + t_dot(probs_bf, d_att)
                d_krot = d_krot + t_dot(d_scores, q_rot)
                upstream = dot(d_scores, k_rot) * SCALE
                upstream = upstream * cosine - swap_halves(upstream) * sine
                d_queries, d_gain = rms_backward(queries, inv_query, query_gain, upstream)
                dq_ref[rows, head_columns(head)] = as_bf(d_queries)
                d_query_gain = d_query_gain + d_gain[None]
            upstream = d_krot * cosine - swap_halves(d_krot) * sine
            d_keys, d_gain = rms_backward(keys, inv_key, key_gain, upstream)
            dkv_ref[rows, head_columns(c)] = as_bf(d_keys)
            dkv_ref[rows, head_columns(KV_LOCAL + c)] = as_bf(d_values)
            d_key_gain = d_key_gain + d_gain[None]
        return d_query_gain, d_key_gain

    zero = jnp.zeros((1, HEAD_SIZE), jnp.float32)
    d_query_gain, d_key_gain = lax.fori_loop(0, 4, one_row, (zero, zero))
    dgain_ref[0:1] = d_query_gain
    dgain_ref[1:2] = d_key_gain
    partial = dot_t(dq_ref[...], wq_ref[...]) + dot_t(dkv_ref[...], wk_ref[:, : kv_ref.shape[1]])
    emit_partial(partial, send_ref, keep_ref)
    d_attn_gain = jnp.zeros((1, D), jnp.float32)
    for k, ref in enumerate((tok0, tok1, tok2, tok3)):
        tokens = ref[:length].astype(jnp.float32)
        scaled = tokens * inverse_rms(tokens)
        part = partial[k * length : (k + 1) * length] * scaled
        d_attn_gain = d_attn_gain + jnp.sum(part, axis=0, keepdims=True)
    dattn_ref[...] = d_attn_gain


def ffn_kernel(
    mn0, mn1, mn2, mn3, cot0, cot1, cot2, cot3, gate_ref, up_ref, down_ref,
    mn_ref, cot_ref, hid_ref, dgate_ref, dup_ref, send_ref, keep_ref,
):
    length = send_ref.shape[1]
    for k, (mn, cot) in enumerate(zip((mn0, mn1, mn2, mn3), (cot0, cot1, cot2, cot3))):
        mn_ref[k * length : (k + 1) * length] = mn[...]
        cot_ref[k * length : (k + 1) * length] = cot[...]

    def half(index, carry):
        rows = block_rows(index, 2 * length)
        gate_pre = dot(mn_ref[rows], gate_ref[...])
        up_pre = dot(mn_ref[rows], up_ref[...])
        d_hidden = dot_t(cot_ref[rows], down_ref[...])
        sig = jax.nn.sigmoid(gate_pre)
        hid_ref[rows] = as_bf(gate_pre * sig * up_pre)
        dgate_ref[rows] = as_bf(d_hidden * up_pre * sig * (1.0 + gate_pre * (1.0 - sig)))
        dup_ref[rows] = as_bf(d_hidden * gate_pre * sig)
        return carry

    lax.fori_loop(0, 2, half, 0)
    emit_partial(
        dot_t(dgate_ref[...], gate_ref[...]) + dot_t(dup_ref[...], up_ref[...]), send_ref, keep_ref
    )


def run_kernel(kernel, outputs, *inputs, scratch=()):
    whole = pl.BlockSpec(memory_space=pltpu.VMEM)
    return pl.pallas_call(
        kernel,
        out_shape=[jax.ShapeDtypeStruct(shape, dtype) for shape, dtype in outputs],
        in_specs=[whole] * len(inputs),
        out_specs=[whole] * len(outputs),
        scratch_shapes=scratch,
        compiler_params=pltpu.CompilerParams(vmem_limit_bytes=48 * 1024 * 1024),
    )(*inputs)


def adamw(weight, grad_sum, mean_old, square_old, step_float, token_total, decay):
    gradient = grad_sum / token_total
    mean_new = BETA_ONE * mean_old + (1.0 - BETA_ONE) * gradient
    square_new = BETA_TWO * square_old + (1.0 - BETA_TWO) * gradient * gradient
    fix_one = 1.0 - jnp.power(BETA_ONE, step_float)
    fix_two = 1.0 - jnp.power(BETA_TWO, step_float)
    change = mean_new / fix_one / (jnp.sqrt(square_new / fix_two) + ADAM_EPS) + decay * weight
    return (weight - LEARN_RATE * change, mean_new, square_new)


def body(
    tokens,
    segments,
    out_cot,
    step_count,
    w_qkv,
    w_out,
    w_gate_up,
    w_down,
    norm_gains,
    mean_qkv,
    mean_out,
    mean_gate_up,
    mean_down,
    mean_gains,
    square_qkv,
    square_out,
    square_gate_up,
    square_down,
    square_gains,
):
    length = tokens.shape[0]
    bf = jnp.bfloat16
    both = ("rep", "shard")
    mine = lax.axis_index("shard")
    own = norm_gains.shape[0]
    extra = jnp.pad(norm_gains.astype(bf)[None], ((0, w_qkv.shape[0] - 1), (0, 128 - own)))
    split, first = split_columns(w_qkv.astype(bf), QKV_WIDTHS, extra)
    turned_out = lax.ppermute(w_out.astype(bf), both, turned(False))
    split_ff, _ = split_columns(w_gate_up.astype(bf), GATE_UP_WIDTHS, ahead=(first,))
    turned_down = lax.ppermute(after(w_down.astype(bf), first), both, turned(False))
    wide, half = QUERY_HEADS * HEAD_SIZE // 4, FF // 4
    whole, steps = gather_rep(
        {
            "q": split[:, :wide],
            "k": split[:, wide:],
            "o": turned_out,
            "g": split_ff[:, :half],
            "u": split_ff[:, half:],
            "d": turned_down,
        }
    )
    w_query, output, gate, up, down = (whole[n] for n in "qogud")
    w_keys = whole["k"]
    gains = w_keys.reshape(-1, w_qkv.shape[0], w_keys.shape[1])
    gains = gains[:, 0, w_keys.shape[1] - 128 : w_keys.shape[1] - 128 + own]
    gains = gains.reshape(1, -1).astype(jnp.float32)
    marks = lax.dynamic_update_slice(jnp.zeros((16, D), bf), segments.astype(bf), (0, 0))
    group = jnp.concatenate([tokens, marks])
    def seen(*events):
        return tuple(steps[event] for event in events if event in steps)

    group = group_gather(after(group, *seen(("q", "z", 1))))
    segment_group = jnp.concatenate([part[length : length + 1, :length] for part in group])
    segment_group = segment_group.astype(jnp.float32)
    attn_gain, mlp_gain = gains[0, :D], gains[0, D : 2 * D]
    cosine, sine = turn_tables(length)
    flat, kv_width = 4 * length, w_keys.shape[1] - 128
    sent = [((2, length, D), bf), ((2, length, D), jnp.float32)]

    x_float = tokens.astype(jnp.float32)
    inv_attn = rms_forward(x_float, attn_gain)[1]
    normed, queries, keys_values, attended_bf, *partial = run_kernel(
        attention_kernel,
        [((flat, D), bf), ((flat, wide), jnp.float32), ((flat, kv_width), jnp.float32), ((flat, wide), bf)]
        + sent,
        *group, segment_group, gains, cosine, sine, w_query, w_keys, output,
    )
    send = after(partial[0], *seen(("g", "z", 2), ("u", "z", 1)))
    cot_group = group_gather(after(out_cot, send))
    x_mid = x_float + group_sum(send, partial[1])
    mid_float, inv_mlp = rms_forward(x_mid, mlp_gain)
    mid_normed, cot_all, hidden, d_gate, d_up, *partial = run_kernel(
        ffn_kernel,
        [((flat, D), bf), ((flat, D), bf)] + [((flat, half), bf)] * 3 + sent,
        *group_gather(after(mid_float.astype(bf), *seen(("g", "z", 3), ("u", "z", 2)))),
        *cot_group, gate, up, down,
    )
    rep_down = RepSum(dot(hidden.T, cot_all), True)
    rep_up = RepSum(dot(mid_normed.T, d_up), True)
    rep_gate = RepSum(dot(mid_normed.T, d_gate), False)
    first = rep_down.step(), rep_gate.step(), rep_up.step()
    d_mid_norm = group_sum(*partial)
    d_mid_part, d_mlp_gain = rms_backward(x_mid, inv_mlp, mlp_gain, d_mid_norm)
    d_mid = out_cot.astype(jnp.float32) + d_mid_part
    second = rep_down.step(), rep_up.step()
    d_mid_bf = jnp.concatenate(group_gather(d_mid.astype(bf)))
    rep_out = RepSum(dot(attended_bf.T, d_mid_bf), False)
    rep_down.step(d_mid_bf), rep_up.step(d_mid_bf), rep_gate.step(d_mid_bf), rep_out.step()
    d_query, d_keys, d_head_gains, d_attn_gain, *partial = run_kernel(
        attention_back_kernel,
        [((flat, wide), bf), ((flat, kv_width), bf), ((2, HEAD_SIZE), jnp.float32), ((1, D), jnp.float32)]
        + sent,
        after(d_mid_bf, first[1], *second),
        *group, segment_group, gains, cosine, sine, queries, keys_values, w_query, w_keys, output,
        scratch=[pltpu.VMEM((flat, wide), bf)],
    )

    gain_grads = jnp.concatenate([d_attn_gain[0], d_mlp_gain, d_head_gains.reshape(-1)])
    gain_grads = gain_grads.reshape(-1, 1, 4 * own)
    gain_grads = jnp.pad(gain_grads, ((0, 0), (0, 15), (0, kv_width - 4 * own)))
    grad_keys = dot(normed.T, d_keys).reshape(gain_grads.shape[0], -1, kv_width)
    rep_keys = RepSum(jnp.concatenate([grad_keys, gain_grads], axis=1).reshape(-1, kv_width), True)
    rep_query = RepSum(dot(normed.T, d_query), False)
    begun = rep_keys.step(), rep_query.step()
    for _ in range(3):
        rep_keys.step(), rep_query.step()
    for ready in (rep_gate, rep_gate, rep_out, rep_up, rep_down, rep_out, rep_out):
        ready.step(begun[0])
    sum_keys, sum_query = rep_keys.total, rep_query.total
    group_rows = grad_keys.shape[1]
    sum_qkv, sum_gain = join_columns(
        jnp.concatenate([sum_query, sum_keys[:group_rows]], axis=1),
        QKV_WIDTHS,
        sum_keys[group_rows, : 4 * own].reshape(4, own),
    )
    d_normed = group_sum(*partial)
    input_grad = d_mid + rms_backward(x_float, inv_attn, attn_gain, d_normed)[0]
    partial = dot(hidden, down).reshape(4, length, D)
    send = after(as_bf(jnp.stack([partial[3], partial[1]])), begun[0])
    layer_out = (x_mid + group_sum(send, (partial[0], partial[2]))).astype(bf)
    sum_gate_up = join_columns(jnp.concatenate([rep_gate.total, rep_up.total], axis=1), GATE_UP_WIDTHS)
    sum_down = lax.ppermute(as_bf(rep_down.total), both, turned(True)).astype(jnp.float32)
    sum_out = lax.ppermute(as_bf(rep_out.total), both, turned(True)).astype(jnp.float32)

    token_total = float(length * lax.axis_size(both))
    step_float = step_count[0].astype(jnp.float32)
    new_qkv, new_mean_qkv, new_square_qkv = adamw(
        w_qkv, sum_qkv, mean_qkv, square_qkv, step_float, token_total, DECAY_RATE
    )
    new_out, new_mean_out, new_square_out = adamw(
        w_out, sum_out, mean_out, square_out, step_float, token_total, DECAY_RATE
    )
    new_gate_up, new_mean_gate_up, new_square_gate_up = adamw(
        w_gate_up, sum_gate_up, mean_gate_up, square_gate_up, step_float, token_total, DECAY_RATE
    )
    new_down, new_mean_down, new_square_down = adamw(
        w_down, sum_down, mean_down, square_down, step_float, token_total, DECAY_RATE
    )
    new_gains, new_mean_gains, new_square_gains = adamw(
        norm_gains, sum_gain, mean_gains, square_gains, step_float, token_total, 0.0
    )
    return (
        layer_out,
        input_grad,
        sum_qkv,
        sum_out,
        sum_gate_up,
        sum_down,
        sum_gain,
        new_qkv,
        new_out,
        new_gate_up,
        new_down,
        new_gains,
        new_mean_qkv,
        new_mean_out,
        new_mean_gate_up,
        new_mean_down,
        new_mean_gains,
        new_square_qkv,
        new_square_out,
        new_square_gate_up,
        new_square_down,
        new_square_gains,
    )


def solution(mesh):
    return jax.shard_map(
        body,
        mesh=mesh,
        in_specs=(
            P(("rep", "shard"), None),
            P(("rep", "shard"), None),
            P(("rep", "shard"), None),
            P(),
            P(("rep", "shard"), None),
            P(("rep", "shard"), None),
            P(("rep", "shard"), None),
            P(("rep", "shard"), None),
            P(("rep", "shard")),
            P(("rep", "shard"), None),
            P(("rep", "shard"), None),
            P(("rep", "shard"), None),
            P(("rep", "shard"), None),
            P(("rep", "shard")),
            P(("rep", "shard"), None),
            P(("rep", "shard"), None),
            P(("rep", "shard"), None),
            P(("rep", "shard"), None),
            P(("rep", "shard")),
        ),
        out_specs=(
            P(("rep", "shard"), None),
            P(("rep", "shard"), None),
            P(("rep", "shard"), None),
            P(("rep", "shard"), None),
            P(("rep", "shard"), None),
            P(("rep", "shard"), None),
            P(("rep", "shard")),
            P(("rep", "shard"), None),
            P(("rep", "shard"), None),
            P(("rep", "shard"), None),
            P(("rep", "shard"), None),
            P(("rep", "shard")),
            P(("rep", "shard"), None),
            P(("rep", "shard"), None),
            P(("rep", "shard"), None),
            P(("rep", "shard"), None),
            P(("rep", "shard")),
            P(("rep", "shard"), None),
            P(("rep", "shard"), None),
            P(("rep", "shard"), None),
            P(("rep", "shard"), None),
            P(("rep", "shard")),
        ),
        check_vma=False,
    )
```

time: 413 us -> 328 us (0.79); the launches traced: 406 us -> 326 us
  waiting for transfers between devices: 205 us -> 144 us
  local copies, waits for them, and re-layouts: 68 us -> 23.8 us
  Pallas kernels: 0 us -> 36.7 us
  starting transfers between devices: 45.8 us -> 78.3 us
  other arithmetic: 55.6 us -> 31.1 us
  matrix products: 26.5 us -> 8.69 us
    ppermute x62 -> x80, waiting for transfers between devices: 201 us -> 138 us  [the longest x24 57.3 us: gather_rep(): got = lax.ppermute(value, 'rep', pairs)]
    pallas_call x0 -> x3, Pallas kernels: none -> 36.7 us  [run_kernel(): pl.pallas_call(kernel, out_shape=[jax.ShapeDtypeStruct(shape, dtype) for...]
    ppermute x62 -> x80, starting transfers between devices: 40.3 us -> 72 us  [the longest x24 24.3 us: gather_rep(): got = lax.ppermute(value, 'rep', pairs)]
    dot_general x12 -> x7, matrix products: 21.2 us -> 8.69 us  [dot(): return jnp.dot(left, right, preferred_element_type=jnp.float32)]
    unnamed x237 -> x166, local copies, waits for them, and re-layouts: 22.4 us -> 12.9 us
    reshape x7 -> x1, local copies, waits for them, and re-layouts: 9.54 us -> 0.09 us  [body(): gain_grads = gain_grads.reshape(-1, 1, 4 * own)]
    another operation x29 -> x6, other arithmetic: 12 us -> 3.46 us  [the longest x4 2.59 us: gather_rep(): result[name] = jnp.stack(both, axis=1).reshape(8 * rows, columns)]
    dot_general x3 -> x0, local copies, waits for them, and re-layouts: 6.65 us -> none  [dot(): return jnp.dot(left, right, preferred_element_type=jnp.float32)]
  transfers between devices with their start and end apart: 66 -> 84, of which waited for: 32 -> 38; matrix products, arithmetic and copies ran while one was open for 31% -> 16% of each run, Pallas kernels for 0% -> 9%
where the time goes in v2:
time: 328 us; the launch traced here: 326 us
  waiting for transfers between devices  144 us (44%)
  starting transfers between devices  78.3 us (24%)
  Pallas kernels  36.7 us (11%)
  other arithmetic  31.1 us (9%)
  local copies, waits for them, and re-layouts  23.8 us (7%)
  matrix products  8.69 us (3%)
  between operations  3.49 us (1%)
    ppermute x24, waiting for transfers between devices, gather_rep(): got = lax.ppermute(value, 'rep', pairs)  57.3 us
    ppermute x18, waiting for transfers between devices, step(): self.got = lax.ppermute(after(as_bf(value), *ahead), 'rep', RING)  55.6 us
    pallas_call x3, Pallas kernels, run_kernel(): pl.pallas_call(kernel, out_shape=[jax.ShapeDtypeStruct(shape, dtype) for...  36.7 us
    ppermute x24, starting transfers between devices, gather_rep(): got = lax.ppermute(value, 'rep', pairs)  24.3 us
    ppermute x12, waiting for transfers between devices, trade(): lax.ppermute(pieces(k), 'shard', xor_perm(4, k))  17.9 us
    unnamed x166, local copies, waits for them, and re-layouts  12.9 us
    ppermute x12, starting transfers between devices, trade(): lax.ppermute(pieces(k), 'shard', xor_perm(4, k))  12.5 us
    ppermute x18, starting transfers between devices, step(): self.got = lax.ppermute(after(as_bf(value), *ahead), 'rep', RING)  12.3 us
  transfers between devices with their start and end apart: 84, of which 38 were waited for; matrix products, arithmetic and copies ran while one was open for 16% of the time, Pallas kernels for 9%

profile of v2, /device:TPU:0, one launch (start us, length us, event | category | flops | bytes accessed | tf_op | source)
XLA Modules:
  0.0 325.8 jit_solution(8789202470269508892)
XLA Ops:
  4.4 4.4 %collective-permute-start.2 = (bf16[32,1152]{1,0:T(8,128)(2,1)S(1)}, bf16[32,1152]{1,0:T(8,128)(2,1)S(1)}, u32[]{:S(2)}, u32[]{:S(2)}) collective-permute-start(bf16[32,1152]{1,0:T(8,128)(2,1)S(1)} %get-tuple-element.222), channel_id=1, source_target_pairs={{0,1},{1,0},{2,3},{3,2},{4,5},{5,4},{6,7},{7,6},{8,9},{9,8},{10,11... | collective-permute-start | bytes 221192 | tf_op jit(solution)/shard_map/ppermute | solution.py:169
  8.8 2.2 collective-permute-start
  11.6 5.2 %collective-permute-done = bf16[32,1152]{1,0:T(8,128)(2,1)S(1)} collective-permute-done((bf16[32,1152]{1,0:T(8,128)(2,1)S(1)}, bf16[32,1152]{1,0:T(8,128)(2,1)S(1)}, u32[]{:S(2)}, u32[]{:S(2)}) %collective-permute-start) | collective-permute-done | bytes 73760 | tf_op jit(solution)/shard_map/ppermute | solution.py:169
  18.7 2.5 collective-permute-start.17
  21.3 3.5 %collective-permute-done.17 = bf16[32,1536]{1,0:T(8,128)(2,1)S(1)} collective-permute-done((bf16[32,1536]{1,0:T(8,128)(2,1)S(1)}, bf16[32,1536]{1,0:T(8,128)(2,1)S(1)}, u32[]{:S(2)}, u32[]{:S(2)}) %collective-permute-start.17) | collective-permute-done | bytes 98336 | tf_op jit(solution)/shard_map/ppermute | solution.py:169
  27.3 3.0 collective-permute-start.19
  30.6 2.7 collective-permute-start.14
  33.3 2.8 collective-permute-start.5
  37.5 2.3 collective-permute-start.4
  39.8 7.5 %collective-permute-start.13 = (bf16[96,1024]{1,0:T(8,128)(2,1)S(1)}, bf16[96,1024]{1,0:T(8,128)(2,1)S(1)}, u32[]{:S(2)}, u32[]{:S(2)}) collective-permute-start(bf16[96,1024]{1,0:T(8,128)(2,1)S(1)} %collective-permute-done.12), channel_id=1, source_target_pairs={{0,8},{4,12},{8,16},{12,20},{16,24},{20,28},{24,0},{28,4},{1,9},{5... | collective-permute-start | bytes 589832 | tf_op jit(solution)/shard_map/ppermute | solution.py:95
  47.6 5.0 %collective-permute-done.13 = bf16[96,1024]{1,0:T(8,128)(2,1)S(1)} collective-permute-done((bf16[96,1024]{1,0:T(8,128)(2,1)S(1)}, bf16[96,1024]{1,0:T(8,128)(2,1)S(1)}, u32[]{:S(2)}, u32[]{:S(2)}) %collective-permute-start.13) | collective-permute-done | bytes 196640 | tf_op jit(solution)/shard_map/ppermute | solution.py:95
  52.6 2.5 collective-permute-start.21
  55.5 2.9 collective-permute-start.6
  58.4 6.9 %collective-permute-done.21 = bf16[64,1024]{1,0:T(8,128)(2,1)S(1)} collective-permute-done((bf16[64,1024]{1,0:T(8,128)(2,1)S(1)}, bf16[64,1024]{1,0:T(8,128)(2,1)S(1)}, u32[]{:S(2)}, u32[]{:S(2)}) %collective-permute-start.21) | collective-permute-done | bytes 131104 | tf_op jit(solution)/shard_map/ppermute | solution.py:95
  65.3 2.4 collective-permute-start.23
  69.5 2.8 collective-permute-done.23
  72.3 2.4 collective-permute-start.28
  75.0 5.3 %collective-permute-done.11 = bf16[256,640]{1,0:T(8,128)(2,1)S(1)} collective-permute-done((bf16[256,640]{1,0:T(8,128)(2,1)S(1)}, bf16[256,640]{1,0:T(8,128)(2,1)S(1)}, u32[]{:S(2)}, u32[]{:S(2)}) %collective-permute-start.11) | collective-permute-done | bytes 327712 | tf_op jit(solution)/shard_map/ppermute | solution.py:95
  82.7 21.4 %collective-permute-done.31 = bf16[96,1024]{1,0:T(8,128)(2,1)S(1)} collective-permute-done((bf16[96,1024]{1,0:T(8,128)(2,1)S(1)}, bf16[96,1024]{1,0:T(8,128)(2,1)S(1)}, u32[]{:S(2)}, u32[]{:S(2)}) %collective-permute-start.31) | collective-permute-done | bytes 196640 | tf_op jit(solution)/shard_map/ppermute | solution.py:95
  109.8 6.5 %collective-permute-done.27 = bf16[128,768]{1,0:T(8,128)(2,1)} collective-permute-done((bf16[128,768]{1,0:T(8,128)(2,1)}, bf16[128,768]{1,0:T(8,128)(2,1)}, u32[]{:S(2)}, u32[]{:S(2)}) %collective-permute-start.27) | collective-permute-done | bytes 196640 | tf_op jit(solution)/shard_map/ppermute | solution.py:95
  118.4 12.1 %shard_map.372 = (bf16[512,1024]{1,0:T(8,128)(2,1)S(1)}, f32[512,512]{1,0:T(8,128)S(1)}, f32[512,512]{1,0:T(8,128)S(1)}, bf16[512,512]{1,0:T(8,128)(2,1)S(1)}, b...) custom-call(bf16[144,1024]{1,0:T(8,128)(2,1)S(1)} %fusion.38.tok0, ...), custom_call_target="tpu_custom_call" | custom-call | tf_op jit(solution)/shard_map/pallas_call | solution.py:426
  135.3 2.9 collective-permute-done.38.cot2
  138.2 6.6 %collective-permute-done.41 = bf16[256,768]{1,0:T(8,128)(2,1)S(1)} collective-permute-done((bf16[256,768]{1,0:T(8,128)(2,1)}, bf16[256,768]{1,0:T(8,128)(2,1)S(1)}, u32[]{:S(2)}, u32[]{:S(2)}) %collective-permute-start.41) | collective-permute-done | bytes 393248 | tf_op jit(solution)/shard_map/ppermute | solution.py:95
  144.8 1.9 collective-permute-start.30
  153.2 1.8 collective-permute-start.35
  157.6 2.9 collective-permute-done.35.mn2
  162.1 8.5 %shard_map.373 = (bf16[512,1024]{1,0:T(8,128)(2,1)S(1)}, bf16[512,1024]{1,0:T(8,128)(2,1)}, bf16[512,768]{1,0:T(8,128)(2,1)S(1)}, bf16[512,768]{1,0:T(8,128)(2,1...) custom-call(bf16[128,1024]{1,0:T(8,128)(2,1)S(1)} %multiply_convert_fusion.mn0, ...), custom_call_target="tpu_custom_call" | custom-call | tf_op jit(solution)/shard_map/pallas_call | solution.py:426
  171.1 2.4 fusion.98
  175.8 2.4 collective-permute-start.48
  181.8 6.6 %collective-permute-done.49 = bf16[2,96,1024]{2,1,0:T(8,128)(2,1)S(1)} collective-permute-done((bf16[2,96,1024]{2,1,0:T(8,128)(2,1)S(1)}, bf16[2,96,1024]{2,1,0:T(8,128)(2,1)S(1)}, u32[]{:S(2)}, u32[]{:S(2)}) %collective-permute-start.49) | collective-permute-done | bytes 393248 | tf_op jit(solution)/shard_map/ppermute | solution.py:143
  188.6 8.3 %collective-permute-done.51 = bf16[2,128,768]{2,1,0:T(8,128)(2,1)S(1)} collective-permute-done((bf16[2,128,768]{2,1,0:T(8,128)(2,1)S(1)}, bf16[2,128,768]{2,1,0:T(8,128)(2,1)S(1)}, u32[]{:S(2)}, u32[]{:S(2)}) %collective-permute-start.51) | collective-permute-done | bytes 393248 | tf_op jit(solution)/shard_map/ppermute | solution.py:143
  200.0 5.2 %collective-permute-done.50 = bf16[2,96,1024]{2,1,0:T(8,128)(2,1)S(1)} collective-permute-done((bf16[2,96,1024]{2,1,0:T(8,128)(2,1)S(1)}, bf16[2,96,1024]{2,1,0:T(8,128)(2,1)S(1)}, u32[]{:S(2)}, u32[]{:S(2)}) %collective-permute-start.50) | collective-permute-done | bytes 393248 | tf_op jit(solution)/shard_map/ppermute | solution.py:143
  206.8 5.9 %collective-permute-done.52 = bf16[2,128,768]{2,1,0:T(8,128)(2,1)S(1)} collective-permute-done((bf16[2,128,768]{2,1,0:T(8,128)(2,1)S(1)}, bf16[2,128,768]{2,1,0:T(8,128)(2,1)S(1)}, u32[]{:S(2)}, u32[]{:S(2)}) %collective-permute-start.52) | collective-permute-done | bytes 393248 | tf_op jit(solution)/shard_map/ppermute | solution.py:143
  215.3 2.3 collective-permute-start.68
  218.0 16.0 %shard_map.374 = (bf16[512,512]{1,0:T(8,128)(2,1)S(1)}, bf16[512,512]{1,0:T(8,128)(2,1)S(1)}, f32[2,128]{1,0:T(2,128)S(1)}, f32[1,1024]{1,0:T(1,128)S(1)}, bf16[...) custom-call(bf16[512,1024]{1,0:T(8,128)(2,1)S(1)} %pad_maximum_fusion.4.dmid_ref, ...), custom_call_target="tpu_custom_call" | custom-call | tf_op jit(solution)/shard_map/pallas_call | solution.py:426
  238.8 4.3 %collective-permute-start.53 = (bf16[2,144,512]{2,1,0:T(8,128)(2,1)S(1)}, bf16[2,144,512]{2,1,0:T(8,128)(2,1)S(1)}, u32[]{:S(2)}, u32[]{:S(2)}) collective-permute-start(bf16[2,144,512]{2,1,0:T(8,128)(2,1)S(1)} %fusion.39), channel_id=1, source_target_pairs={{0,8},{4,12},{8,16},{12,20},{16,24},{20,28},{24,0},{28,4},{1,9},{5... | collective-permute-start | bytes 884744 | tf_op jit(solution)/shard_map/ppermute | solution.py:143
  245.7 9.1 %collective-permute-done.53 = bf16[2,144,512]{2,1,0:T(8,128)(2,1)S(1)} collective-permute-done((bf16[2,144,512]{2,1,0:T(8,128)(2,1)S(1)}, bf16[2,144,512]{2,1,0:T(8,128)(2,1)S(1)}, u32[]{:S(2)}, u32[]{:S(2)}) %collective-permute-start.53) | collective-permute-done | bytes 294944 | tf_op jit(solution)/shard_map/ppermute | solution.py:143
  256.7 2.3 collective-permute-start.62
  260.3 4.6 %collective-permute-done.74 = bf16[128,768]{1,0:T(8,128)(2,1)S(1)} collective-permute-done((bf16[128,768]{1,0:T(8,128)(2,1)S(1)}, bf16[128,768]{1,0:T(8,128)(2,1)S(1)}, u32[]{:S(2)}, u32[]{:S(2)}) %collective-permute-start.74) | collective-permute-done | bytes 196640 | tf_op jit(solution)/shard_map/ppermute | solution.py:143
  268.7 4.0 %collective-permute-done.77 = bf16[128,768]{1,0:T(8,128)(2,1)S(1)} collective-permute-done((bf16[128,768]{1,0:T(8,128)(2,1)S(1)}, bf16[128,768]{1,0:T(8,128)(2,1)S(1)}, u32[]{:S(2)}, u32[]{:S(2)}) %collective-permute-start.77) | collective-permute-done | bytes 196640 | tf_op jit(solution)/shard_map/ppermute | solution.py:150
  273.9 2.6 collective-permute-done.82
  276.6 4.0 %collective-permute-done.69 = bf16[64,1024]{1,0:T(8,128)(2,1)S(1)} collective-permute-done((bf16[64,1024]{1,0:T(8,128)(2,1)S(1)}, bf16[64,1024]{1,0:T(8,128)(2,1)S(1)}, u32[]{:S(2)}, u32[]{:S(2)}) %collective-permute-start.69) | collective-permute-done | bytes 131104 | tf_op jit(solution)/shard_map/ppermute | solution.py:143
  281.3 2.1 collective-permute-done.59
  283.4 1.9 collective-permute-start.70
  288.3 6.2 %collective-permute-done.70 = bf16[64,1024]{1,0:T(8,128)(2,1)S(1)} collective-permute-done((bf16[64,1024]{1,0:T(8,128)(2,1)S(1)}, bf16[64,1024]{1,0:T(8,128)(2,1)S(1)}, u32[]{:S(2)}, u32[]{:S(2)}) %collective-permute-start.70) | collective-permute-done | bytes 131104 | tf_op jit(solution)/shard_map/ppermute | solution.py:143
  298.9 1.8 collective-permute-done.79
  316.3 2.1 multiply_subtract_fusion.3
  321.7 1.8 collective-permute-done.66
  (428 shorter events, 95.7 us)
Async XLA Ops:
  1.7 28.6 %collective-permute-start.9 = (bf16[64,1024]{1,0:T(8,128)(2,1)S(1)}, bf16[64,1024]{1,0:T(8,128)(2,1)S(1)}, u32[]{:S(2)}, u32[]{:S(2)}) collective-permute-start(bf16[64,1024]{1,0:T(8,128)(2,1)S(1)} %convert_element_type.351), channel_id=1, source_target_pairs={{0,0},{1,4},{2,8},{3,12},{4,16},{5,20},{6,24},{7,28},{8,1},{9,5},{... | collective-permute-start | bytes 393224 | tf_op jit(solution)/shard_map/ppermute | solution.py:474
  4.4 12.4 %collective-permute-start.2 = (bf16[32,1152]{1,0:T(8,128)(2,1)S(1)}, bf16[32,1152]{1,0:T(8,128)(2,1)S(1)}, u32[]{:S(2)}, u32[]{:S(2)}) collective-permute-start(bf16[32,1152]{1,0:T(8,128)(2,1)S(1)} %get-tuple-element.222), channel_id=1, source_target_pairs={{0,1},{1,0},{2,3},{3,2},{4,5},{5,4},{6,7},{7,6},{8,9},{9,8},{10,11... | collective-permute-start | bytes 221192 | tf_op jit(solution)/shard_map/ppermute | solution.py:169
  18.5 12.1 %collective-permute-start.3 = (bf16[128,512]{1,0:T(8,128)(2,1)S(1)}, bf16[128,512]{1,0:T(8,128)(2,1)S(1)}, u32[]{:S(2)}, u32[]{:S(2)}) collective-permute-start(bf16[128,512]{1,0:T(8,128)(2,1)S(1)} %pad_maximum_fusion.10), channel_id=1, source_target_pairs={{0,8},{4,12},{8,16},{12,20},{16,24},{20,28},{24,0},{28,4},{1,9},{5... | collective-permute-start | bytes 393224 | tf_op jit(solution)/shard_map/ppermute | solution.py:95
  24.8 15.0 %collective-permute-start.12 = (bf16[96,1024]{1,0:T(8,128)(2,1)S(1)}, bf16[96,1024]{1,0:T(8,128)(2,1)S(1)}, u32[]{:S(2)}, u32[]{:S(2)}) collective-permute-start(bf16[96,1024]{1,0:T(8,128)(2,1)S(1)} %convert_element_type.352), channel_id=1, source_target_pairs={{0,0},{1,4},{2,8},{3,12},{4,16},{5,20},{6,24},{7,28},{8,1},{9,5},{... | collective-permute-start | bytes 589832 | tf_op jit(solution)/shard_map/ppermute | solution.py:476
  27.3 20.0 %collective-permute-start.19 = (bf16[128,768]{1,0:T(8,128)(2,1)S(1)}, bf16[128,768]{1,0:T(8,128)(2,1)S(1)}, u32[]{:S(2)}, u32[]{:S(2)}) collective-permute-start(bf16[128,768]{1,0:T(8,128)(2,1)S(1)} %get-tuple-element.189), channel_id=1, source_target_pairs={{0,4},{4,0},{8,12},{12,8},{16,20},{20,16},{24,28},{28,24},{1,5},{5... | collective-permute-start | bytes 589832 | tf_op jit(solution)/shard_map/ppermute | solution.py:95
  30.6 16.7 %collective-permute-start.14 = (bf16[128,512]{1,0:T(8,128)(2,1)S(1)}, bf16[128,512]{1,0:T(8,128)(2,1)S(1)}, u32[]{:S(2)}, u32[]{:S(2)}) collective-permute-start(bf16[128,512]{1,0:T(8,128)(2,1)S(1)} %collective-permute-done.3), channel_id=1, source_target_pairs={{0,8},{4,12},{8,16},{12,20},{16,24},{20,28},{24,0},{28,4},{1,9},{5... | collective-permute-start | bytes 393224 | tf_op jit(solution)/shard_map/ppermute | solution.py:95
  33.3 21.8 %collective-permute-start.5 = (bf16[144,1024]{1,0:T(8,128)(2,1)S(1)}, bf16[144,1024]{1,0:T(8,128)(2,1)S(1)}, u32[]{:S(2)}, u32[]{:S(2)}) collective-permute-start(bf16[144,1024]{1,0:T(8,128)(2,1)S(1)} %fusion.38.tok0), channel_id=1, source_target_pairs={{0,2},{1,3},{2,0},{3,1},{4,6},{5,7},{6,4},{7,5},{8,10},{9,11},{10,... | collective-permute-start | bytes 884744 | tf_op jit(solution)/shard_map/ppermute | solution.py:46
  37.5 30.2 %collective-permute-start.4 = (bf16[144,1024]{1,0:T(8,128)(2,1)S(1)}, bf16[144,1024]{1,0:T(8,128)(2,1)S(1)}, u32[]{:S(2)}, u32[]{:S(2)}) collective-permute-start(bf16[144,1024]{1,0:T(8,128)(2,1)S(1)} %fusion.38.tok0), channel_id=1, source_target_pairs={{0,1},{1,0},{2,3},{3,2},{4,5},{5,4},{6,7},{7,6},{8,9},{9,8},{10,11... | collective-permute-start | bytes 884744 | tf_op jit(solution)/shard_map/ppermute | solution.py:45
  39.8 12.8 %collective-permute-start.13 = (bf16[96,1024]{1,0:T(8,128)(2,1)S(1)}, bf16[96,1024]{1,0:T(8,128)(2,1)S(1)}, u32[]{:S(2)}, u32[]{:S(2)}) collective-permute-start(bf16[96,1024]{1,0:T(8,128)(2,1)S(1)} %collective-permute-done.12), channel_id=1, source_target_pairs={{0,8},{4,12},{8,16},{12,20},{16,24},{20,28},{24,0},{28,4},{1,9},{5... | collective-permute-start | bytes 589832 | tf_op jit(solution)/shard_map/ppermute | solution.py:95
  47.4 17.9 %collective-permute-start.8 = (bf16[256,640]{1,0:T(8,128)(2,1)S(1)}, bf16[256,640]{1,0:T(8,128)(2,1)S(1)}, u32[]{:S(2)}, u32[]{:S(2)}) collective-permute-start(bf16[256,640]{1,0:T(8,128)(2,1)S(1)} %maximum_select_fusion.1), channel_id=1, source_target_pairs={{0,8},{4,12},{8,16},{12,20},{16,24},{20,28},{24,0},{28,4},{1,9},{5... | collective-permute-start | bytes 983048 | tf_op jit(solution)/shard_map/ppermute | solution.py:95
  52.6 12.7 %collective-permute-start.21 = (bf16[64,1024]{1,0:T(8,128)(2,1)S(1)}, bf16[64,1024]{1,0:T(8,128)(2,1)S(1)}, u32[]{:S(2)}, u32[]{:S(2)}) collective-permute-start(bf16[64,1024]{1,0:T(8,128)(2,1)S(1)} %collective-permute-done.10), channel_id=1, source_target_pairs={{0,8},{4,12},{8,16},{12,20},{16,24},{20,28},{24,0},{28,4},{1,9},{5... | collective-permute-start | bytes 393224 | tf_op jit(solution)/shard_map/ppermute | solution.py:95
  55.1 14.4 %collective-permute-start.25 = (bf16[96,1024]{1,0:T(8,128)(2,1)S(1)}, bf16[96,1024]{1,0:T(8,128)(2,1)S(1)}, u32[]{:S(2)}, u32[]{:S(2)}) collective-permute-start(bf16[96,1024]{1,0:T(8,128)(2,1)S(1)} %collective-permute-done.13), channel_id=1, source_target_pairs={{0,8},{4,12},{8,16},{12,20},{16,24},{20,28},{24,0},{28,4},{1,9},{5... | collective-permute-start | bytes 589832 | tf_op jit(solution)/shard_map/ppermute | solution.py:95
  55.5 19.5 %collective-permute-start.6 = (bf16[144,1024]{1,0:T(8,128)(2,1)S(1)}, bf16[144,1024]{1,0:T(8,128)(2,1)S(1)}, u32[]{:S(2)}, u32[]{:S(2)}) collective-permute-start(bf16[144,1024]{1,0:T(8,128)(2,1)S(1)} %collective-permute-done.5.tok2), channel_id=1, source_target_pairs={{0,1},{1,0},{2,3},{3,2},{4,5},{5,4},{6,7},{7,6},{8,9},{9,8},{10,11... | collective-permute-start | bytes 884744 | tf_op jit(solution)/shard_map/ppermute | solution.py:47
  67.8 12.4 %collective-permute-start.11 = (bf16[256,640]{1,0:T(8,128)(2,1)S(1)}, bf16[256,640]{1,0:T(8,128)(2,1)S(1)}, u32[]{:S(2)}, u32[]{:S(2)}) collective-permute-start(bf16[256,640]{1,0:T(8,128)(2,1)S(1)} %collective-permute-done.8), channel_id=1, source_target_pairs={{0,8},{4,12},{8,16},{12,20},{16,24},{20,28},{24,0},{28,4},{1,9},{5... | collective-permute-start | bytes 983048 | tf_op jit(solution)/shard_map/ppermute | solution.py:95
  67.9 14.3 %collective-permute-start.22 = (bf16[512,512]{1,0:T(8,128)(2,1)S(1)}, bf16[512,512]{1,0:T(8,128)(2,1)S(1)}, u32[]{:S(2)}, u32[]{:S(2)}) collective-permute-start(bf16[512,512]{1,0:T(8,128)(2,1)S(1)} %constant_dynamic-slice_fusion.8), channel_id=1, source_target_pairs={{0,4},{4,0},{8,12},{12,8},{16,20},{20,16},{24,28},{28,24},{1,5},{5... | collective-permute-start | bytes 1572872 | tf_op jit(solution)/shard_map/ppermute | solution.py:95
  72.3 34.0 %collective-permute-start.28 = (bf16[256,768]{1,0:T(8,128)(2,1)S(1)}, bf16[256,768]{1,0:T(8,128)(2,1)}, u32[]{:S(2)}, u32[]{:S(2)}) collective-permute-start(bf16[256,768]{1,0:T(8,128)(2,1)S(1)} %maximum_select_fusion), channel_id=1, source_target_pairs={{0,8},{4,12},{8,16},{12,20},{16,24},{20,28},{24,0},{28,4},{1,9},{5... | collective-permute-start | bytes 1179656 | tf_op jit(solution)/shard_map/ppermute | solution.py:95
  80.2 26.1 %collective-permute-start.15 = (bf16[256,640]{1,0:T(8,128)(2,1)S(1)}, bf16[256,640]{1,0:T(8,128)(2,1)S(1)}, u32[]{:S(2)}, u32[]{:S(2)}) collective-permute-start(bf16[256,640]{1,0:T(8,128)(2,1)S(1)} %collective-permute-done.11), channel_id=1, source_target_pairs={{0,8},{4,12},{8,16},{12,20},{16,24},{20,28},{24,0},{28,4},{1,9},{5... | collective-permute-start | bytes 983048 | tf_op jit(solution)/shard_map/ppermute | solution.py:95
  81.7 24.5 %collective-permute-start.26 = (bf16[128,768]{1,0:T(8,128)(2,1)S(1)}, bf16[128,768]{1,0:T(8,128)(2,1)}, u32[]{:S(2)}, u32[]{:S(2)}) collective-permute-start(bf16[128,768]{1,0:T(8,128)(2,1)S(1)} %copy-done.48), channel_id=1, source_target_pairs={{0,8},{4,12},{8,16},{12,20},{16,24},{20,28},{24,0},{28,4},{1,9},{5... | collective-permute-start | bytes 589832 | tf_op jit(solution)/shard_map/ppermute | solution.py:95
  81.8 22.3 %collective-permute-start.31 = (bf16[96,1024]{1,0:T(8,128)(2,1)S(1)}, bf16[96,1024]{1,0:T(8,128)(2,1)S(1)}, u32[]{:S(2)}, u32[]{:S(2)}) collective-permute-start(bf16[96,1024]{1,0:T(8,128)(2,1)S(1)} %collective-permute-done.25), channel_id=1, source_target_pairs={{0,8},{4,12},{8,16},{12,20},{16,24},{20,28},{24,0},{28,4},{1,9},{5... | collective-permute-start | bytes 589832 | tf_op jit(solution)/shard_map/ppermute | solution.py:95
  82.2 27.6 %collective-permute-start.24 = (bf16[256,1024]{1,0:T(8,128)(2,1)S(1)}, bf16[256,1024]{1,0:T(8,128)(2,1)}, u32[]{:S(2)}, u32[]{:S(2)}) collective-permute-start(bf16[256,1024]{1,0:T(8,128)(2,1)S(1)} %constant_dynamic-slice_fusion.7), channel_id=1, source_target_pairs={{0,4},{4,0},{8,12},{12,8},{16,20},{20,16},{24,28},{28,24},{1,5},{5... | collective-permute-start | bytes 1572872 | tf_op jit(solution)/shard_map/ppermute | solution.py:95
  107.4 23.3 %collective-permute-start.33 = (bf16[256,768]{1,0:T(8,128)(2,1)}, bf16[256,768]{1,0:T(8,128)(2,1)}, u32[]{:S(2)}, u32[]{:S(2)}) collective-permute-start(bf16[256,768]{1,0:T(8,128)(2,1)} %collective-permute-done.28), channel_id=1, source_target_pairs={{0,8},{4,12},{8,16},{12,20},{16,24},{20,28},{24,0},{28,4},{1,9},{5... | collective-permute-start | bytes 1179656 | tf_op jit(solution)/shard_map/ppermute | solution.py:95
  107.5 43.4 %collective-permute-start.42 = (bf16[384,1024]{1,0:T(8,128)(2,1)}, bf16[384,1024]{1,0:T(8,128)(2,1)}, u32[]{:S(2)}, u32[]{:S(2)}) collective-permute-start(bf16[384,1024]{1,0:T(8,128)(2,1)} %constant_dynamic-slice_fusion.4), channel_id=1, source_target_pairs={{0,4},{4,0},{8,12},{12,8},{16,20},{20,16},{24,28},{28,24},{1,5},{5... | collective-permute-start | bytes 2359304 | tf_op jit(solution)/shard_map/ppermute | solution.py:95
  116.2 15.0 %collective-permute-start.32 = (bf16[128,768]{1,0:T(8,128)(2,1)}, bf16[128,768]{1,0:T(8,128)(2,1)S(1)}, u32[]{:S(2)}, u32[]{:S(2)}) collective-permute-start(bf16[128,768]{1,0:T(8,128)(2,1)} %collective-permute-done.27), channel_id=1, source_target_pairs={{0,8},{4,12},{8,16},{12,20},{16,24},{20,28},{24,0},{28,4},{1,9},{5... | collective-permute-start | bytes 589832 | tf_op jit(solution)/shard_map/ppermute | solution.py:95
  130.6 31.4 %collective-permute-start.37 = (bf16[128,1024]{1,0:T(8,128)(2,1)S(1)}, bf16[128,1024]{1,0:T(8,128)(2,1)S(1)}, u32[]{:S(2)}, u32[]{:S(2)}) collective-permute-start(bf16[128,1024]{1,0:T(8,128)(2,1)S(1)} %copy-done.1), channel_id=1, source_target_pairs={{0,1},{1,0},{2,3},{3,2},{4,5},{5,4},{6,7},{7,6},{8,9},{9,8},{10,11... | collective-permute-start | bytes 786440 | tf_op jit(solution)/shard_map/ppermute | solution.py:45
  131.2 13.6 %collective-permute-start.41 = (bf16[256,768]{1,0:T(8,128)(2,1)}, bf16[256,768]{1,0:T(8,128)(2,1)S(1)}, u32[]{:S(2)}, u32[]{:S(2)}) collective-permute-start(bf16[256,768]{1,0:T(8,128)(2,1)} %collective-permute-done.33), channel_id=1, source_target_pairs={{0,8},{4,12},{8,16},{12,20},{16,24},{20,28},{24,0},{28,4},{1,9},{5... | collective-permute-start | bytes 1179656 | tf_op jit(solution)/shard_map/ppermute | solution.py:95
  138.1 22.4 %collective-permute-start.40 = (bf16[512,768]{1,0:T(8,128)(2,1)S(1)}, bf16[512,768]{1,0:T(8,128)(2,1)S(1)}, u32[]{:S(2)}, u32[]{:S(2)}) collective-permute-start(bf16[512,768]{1,0:T(8,128)(2,1)S(1)} %constant_dynamic-slice_fusion.6), channel_id=1, source_target_pairs={{0,4},{4,0},{8,12},{12,8},{16,20},{20,16},{24,28},{28,24},{1,5},{5... | collective-permute-start | bytes 2359304 | tf_op jit(solution)/shard_map/ppermute | solution.py:95
  138.1 23.9 %collective-permute-start.39 = (bf16[128,1024]{1,0:T(8,128)(2,1)S(1)}, bf16[128,1024]{1,0:T(8,128)(2,1)S(1)}, u32[]{:S(2)}, u32[]{:S(2)}) collective-permute-start(bf16[128,1024]{1,0:T(8,128)(2,1)S(1)} %collective-permute-done.38.cot2), channel_id=1, source_target_pairs={{0,1},{1,0},{2,3},{3,2},{4,5},{5,4},{6,7},{7,6},{8,9},{9,8},{10,11... | collective-permute-start | bytes 786440 | tf_op jit(solution)/shard_map/ppermute | solution.py:47
  174.6 13.8 %collective-permute-start.49 = (bf16[2,96,1024]{2,1,0:T(8,128)(2,1)S(1)}, bf16[2,96,1024]{2,1,0:T(8,128)(2,1)S(1)}, u32[]{:S(2)}, u32[]{:S(2)}) collective-permute-start(bf16[2,96,1024]{2,1,0:T(8,128)(2,1)S(1)} %fusion.33), channel_id=1, source_target_pairs={{0,8},{4,12},{8,16},{12,20},{16,24},{20,28},{24,0},{28,4},{1,9},{5... | collective-permute-start | bytes 1179656 | tf_op jit(solution)/shard_map/ppermute | solution.py:143
  175.8 24.1 %collective-permute-start.48 = (bf16[4,128,768]{2,1,0:T(8,128)(2,1)S(1)}, bf16[4,128,768]{2,1,0:T(8,128)(2,1)S(1)}, u32[]{:S(2)}, u32[]{:S(2)}) collective-permute-start(bf16[4,128,768]{2,1,0:T(8,128)(2,1)S(1)} %fusion), channel_id=1, source_target_pairs={{0,4},{4,0},{8,12},{12,8},{16,20},{20,16},{24,28},{28,24},{1,5},{5... | collective-permute-start | bytes 2359304 | tf_op jit(solution)/shard_map/ppermute | solution.py:150
  179.3 17.6 %collective-permute-start.51 = (bf16[2,128,768]{2,1,0:T(8,128)(2,1)S(1)}, bf16[2,128,768]{2,1,0:T(8,128)(2,1)S(1)}, u32[]{:S(2)}, u32[]{:S(2)}) collective-permute-start(bf16[2,128,768]{2,1,0:T(8,128)(2,1)S(1)} %fusion.34), channel_id=1, source_target_pairs={{0,8},{4,12},{8,16},{12,20},{16,24},{20,28},{24,0},{28,4},{1,9},{5... | collective-permute-start | bytes 1179656 | tf_op jit(solution)/shard_map/ppermute | solution.py:143
  181.2 15.8 %collective-permute-start.44 = (bf16[128,1024]{1,0:T(8,128)(2,1)S(1)}, bf16[128,1024]{1,0:T(8,128)(2,1)S(1)}, u32[]{:S(2)}, u32[]{:S(2)}) collective-permute-start(bf16[128,1024]{1,0:T(8,128)(2,1)S(1)} %fusion.41), channel_id=1, source_target_pairs={{0,2},{1,3},{2,0},{3,1},{4,6},{5,7},{6,4},{7,5},{8,10},{9,11},{10,... | collective-permute-start | bytes 786440 | tf_op jit(solution)/shard_map/ppermute | solution.py:52
  188.5 16.7 %collective-permute-start.50 = (bf16[2,96,1024]{2,1,0:T(8,128)(2,1)S(1)}, bf16[2,96,1024]{2,1,0:T(8,128)(2,1)S(1)}, u32[]{:S(2)}, u32[]{:S(2)}) collective-permute-start(bf16[2,96,1024]{2,1,0:T(8,128)(2,1)S(1)} %fusion.4), channel_id=1, source_target_pairs={{0,8},{4,12},{8,16},{12,20},{16,24},{20,28},{24,0},{28,4},{1,9},{5... | collective-permute-start | bytes 1179656 | tf_op jit(solution)/shard_map/ppermute | solution.py:143
  196.9 15.8 %collective-permute-start.52 = (bf16[2,128,768]{2,1,0:T(8,128)(2,1)S(1)}, bf16[2,128,768]{2,1,0:T(8,128)(2,1)S(1)}, u32[]{:S(2)}, u32[]{:S(2)}) collective-permute-start(bf16[2,128,768]{2,1,0:T(8,128)(2,1)S(1)} %fusion.3), channel_id=1, source_target_pairs={{0,8},{4,12},{8,16},{12,20},{16,24},{20,28},{24,0},{28,4},{1,9},{5... | collective-permute-start | bytes 1179656 | tf_op jit(solution)/shard_map/ppermute | solution.py:143
  199.8 13.7 %collective-permute-start.45 = (bf16[128,1024]{1,0:T(8,128)(2,1)S(1)}, bf16[128,1024]{1,0:T(8,128)(2,1)S(1)}, u32[]{:S(2)}, u32[]{:S(2)}) collective-permute-start(bf16[128,1024]{1,0:T(8,128)(2,1)S(1)} %get-tuple-element.162), channel_id=1, source_target_pairs={{0,1},{1,0},{2,3},{3,2},{4,5},{5,4},{6,7},{7,6},{8,9},{9,8},{10,11... | collective-permute-start | bytes 786440 | tf_op jit(solution)/shard_map/ppermute | solution.py:45
  215.3 49.6 %collective-permute-start.68 = (bf16[4,64,1024]{2,1,0:T(8,128)(2,1)}, bf16[4,64,1024]{2,1,0:T(8,128)(2,1)}, u32[]{:S(2)}, u32[]{:S(2)}) collective-permute-start(bf16[4,64,1024]{2,1,0:T(8,128)(2,1)} %fusion.27), channel_id=1, source_target_pairs={{0,4},{4,0},{8,12},{12,8},{16,20},{20,16},{24,28},{28,24},{1,5},{5... | collective-permute-start | bytes 1572872 | tf_op jit(solution)/shard_map/ppermute | solution.py:150
  217.7 37.5 %collective-permute-start.81 = (bf16[2,96,1024]{2,1,0:T(8,128)(2,1)}, bf16[2,96,1024]{2,1,0:T(8,128)(2,1)}, u32[]{:S(2)}, u32[]{:S(2)}) collective-permute-start(bf16[2,96,1024]{2,1,0:T(8,128)(2,1)} %fusion.1), channel_id=1, source_target_pairs={{0,8},{4,12},{8,16},{12,20},{16,24},{20,28},{24,0},{28,4},{1,9},{5... | collective-permute-start | bytes 1179656 | tf_op jit(solution)/shard_map/ppermute | solution.py:143
  217.7 26.3 %collective-permute-start.73 = (bf16[128,768]{1,0:T(8,128)(2,1)}, bf16[128,768]{1,0:T(8,128)(2,1)}, u32[]{:S(2)}, u32[]{:S(2)}) collective-permute-start(bf16[128,768]{1,0:T(8,128)(2,1)} %fusion.48), channel_id=1, source_target_pairs={{0,8},{4,12},{8,16},{12,20},{16,24},{20,28},{24,0},{28,4},{1,9},{5... | collective-permute-start | bytes 589832 | tf_op jit(solution)/shard_map/ppermute | solution.py:143
  236.5 20.2 %collective-permute-start.76 = (bf16[2,128,768]{2,1,0:T(8,128)(2,1)}, bf16[2,128,768]{2,1,0:T(8,128)(2,1)S(1)}, u32[]{:S(2)}, u32[]{:S(2)}) collective-permute-start(bf16[2,128,768]{2,1,0:T(8,128)(2,1)} %fusion.2), channel_id=1, source_target_pairs={{0,8},{4,12},{8,16},{12,20},{16,24},{20,28},{24,0},{28,4},{1,9},{5... | collective-permute-start | bytes 1179656 | tf_op jit(solution)/shard_map/ppermute | solution.py:143
  238.8 16.0 %collective-permute-start.53 = (bf16[2,144,512]{2,1,0:T(8,128)(2,1)S(1)}, bf16[2,144,512]{2,1,0:T(8,128)(2,1)S(1)}, u32[]{:S(2)}, u32[]{:S(2)}) collective-permute-start(bf16[2,144,512]{2,1,0:T(8,128)(2,1)S(1)} %fusion.39), channel_id=1, source_target_pairs={{0,8},{4,12},{8,16},{12,20},{16,24},{20,28},{24,0},{28,4},{1,9},{5... | collective-permute-start | bytes 884744 | tf_op jit(solution)/shard_map/ppermute | solution.py:143
  244.2 24.3 %collective-permute-start.56 = (bf16[2,128,1024]{2,1,0:T(8,128)(2,1)S(1)}, bf16[2,128,1024]{2,1,0:T(8,128)(2,1)S(1)}, u32[]{:S(2)}, u32[]{:S(2)}) collective-permute-start(bf16[2,128,1024]{2,1,0:T(8,128)(2,1)S(1)} %copy-done.8), channel_id=1, source_target_pairs={{0,1},{1,0},{2,3},{3,2},{4,5},{5,4},{6,7},{7,6},{8,9},{9,8},{10,11... | collective-permute-start | bytes 1572872 | tf_op jit(solution)/shard_map/ppermute | solution.py:51
  254.8 13.1 %collective-permute-start.58 = (bf16[4,128,512]{2,1,0:T(8,128)(2,1)S(1)}, bf16[4,128,512]{2,1,0:T(8,128)(2,1)S(1)}, u32[]{:S(2)}, u32[]{:S(2)}) collective-permute-start(bf16[4,128,512]{2,1,0:T(8,128)(2,1)S(1)} %fusion.26), channel_id=1, source_target_pairs={{0,4},{4,0},{8,12},{12,8},{16,20},{20,16},{24,28},{28,24},{1,5},{5... | collective-permute-start | bytes 1572872 | tf_op jit(solution)/shard_map/ppermute | solution.py:150
  256.7 17.0 %collective-permute-start.62 = (bf16[2,144,512]{2,1,0:T(8,128)(2,1)S(1)}, bf16[2,144,512]{2,1,0:T(8,128)(2,1)S(1)}, u32[]{:S(2)}, u32[]{:S(2)}) collective-permute-start(bf16[2,144,512]{2,1,0:T(8,128)(2,1)S(1)} %fusion.8), channel_id=1, source_target_pairs={{0,8},{4,12},{8,16},{12,20},{16,24},{20,28},{24,0},{28,4},{1,9},{5... | collective-permute-start | bytes 884744 | tf_op jit(solution)/shard_map/ppermute | solution.py:143
  264.9 39.5 %collective-permute-start.54 = (bf16[2,128,1024]{2,1,0:T(8,128)(2,1)S(1)}, bf16[2,128,1024]{2,1,0:T(8,128)(2,1)S(1)}, u32[]{:S(2)}, u32[]{:S(2)}) collective-permute-start(bf16[2,128,1024]{2,1,0:T(8,128)(2,1)S(1)} %copy-done.39), channel_id=1, source_target_pairs={{0,1},{1,0},{2,3},{3,2},{4,5},{5,4},{6,7},{7,6},{8,9},{9,8},{10,11... | collective-permute-start | bytes 1572872 | tf_op jit(solution)/shard_map/ppermute | solution.py:51
  268.5 16.8 %collective-permute-start.75 = (bf16[128,768]{1,0:T(8,128)(2,1)S(1)}, bf16[128,768]{1,0:T(8,128)(2,1)S(1)}, u32[]{:S(2)}, u32[]{:S(2)}) collective-permute-start(bf16[128,768]{1,0:T(8,128)(2,1)S(1)} %fusion.37), channel_id=1, source_target_pairs={{0,8},{4,12},{8,16},{12,20},{16,24},{20,28},{24,0},{28,4},{1,9},{5... | collective-permute-start | bytes 589832 | tf_op jit(solution)/shard_map/ppermute | solution.py:143
  272.7 14.1 %collective-permute-start.57 = (bf16[128,1024]{1,0:T(8,128)(2,1)S(1)}, bf16[128,1024]{1,0:T(8,128)(2,1)S(1)}, u32[]{:S(2)}, u32[]{:S(2)}) collective-permute-start(bf16[128,1024]{1,0:T(8,128)(2,1)S(1)} %fusion.42), channel_id=1, source_target_pairs={{0,2},{1,3},{2,0},{3,1},{4,6},{5,7},{6,4},{7,5},{8,10},{9,11},{10,... | collective-permute-start | bytes 786440 | tf_op jit(solution)/shard_map/ppermute | solution.py:52
  280.5 22.3 %collective-permute-start.83 = (bf16[96,1024]{1,0:T(8,128)(2,1)S(1)}, bf16[96,1024]{1,0:T(8,128)(2,1)S(1)}, u32[]{:S(2)}, u32[]{:S(2)}) collective-permute-start(bf16[96,1024]{1,0:T(8,128)(2,1)S(1)} %fusion.35), channel_id=1, source_target_pairs={{0,0},{4,1},{8,2},{12,3},{16,4},{20,5},{24,6},{28,7},{1,8},{5,9},{... | collective-permute-start | bytes 589832 | tf_op jit(solution)/shard_map/ppermute | solution.py:568
  300.7 12.3 %collective-permute-start.61 = (bf16[128,512]{1,0:T(8,128)(2,1)S(1)}, bf16[128,512]{1,0:T(8,128)(2,1)S(1)}, u32[]{:S(2)}, u32[]{:S(2)}) collective-permute-start(bf16[128,512]{1,0:T(8,128)(2,1)S(1)} %fusion.47), channel_id=1, source_target_pairs={{0,8},{4,12},{8,16},{12,20},{16,24},{20,28},{24,0},{28,4},{1,9},{5... | collective-permute-start | bytes 393224 | tf_op jit(solution)/shard_map/ppermute | solution.py:143
  305.8 12.6 %collective-permute-start.55 = (bf16[128,1024]{1,0:T(8,128)(2,1)}, bf16[128,1024]{1,0:T(8,128)(2,1)}, u32[]{:S(2)}, u32[]{:S(2)}) collective-permute-start(bf16[128,1024]{1,0:T(8,128)(2,1)} %fusion.28), channel_id=1, source_target_pairs={{0,2},{1,3},{2,0},{3,1},{4,6},{5,7},{6,4},{7,5},{8,10},{9,11},{10,... | collective-permute-start | bytes 786440 | tf_op jit(solution)/shard_map/ppermute | solution.py:52
  (92 other events, 822.9 us)

commit v3 on v2

--- a/solution.py
+++ b/solution.py
@@ -1,3 +1,4 @@
+import functools
 import math
 
 import jax
@@ -75,9 +76,25 @@
 WINDOW = 6
 
 
+def finish_ring(held, z, rows, *ahead):
+    return in_order(held[:-1] + [after(held[-1], *ahead)], z, rows)
+
+
+def finish_pair(value, got, even, rows, *ahead):
+    got = after(got, *ahead)
+    columns = value.shape[1]
+    value, got = value.reshape(4, rows, columns), got.reshape(4, rows, columns)
+    both = [jnp.where(even, value, got), jnp.where(even, got, value)]
+    return jnp.stack(both, axis=1).reshape(8 * rows, columns)
+
+
+def gathered(whole, *ahead):
+    return lax.all_gather(whole, "rep", axis=0, tiled=True)
+
+
 def gather_rep(blocks):
     if lax.axis_size("rep") != 8:
-        return {n: lax.all_gather(x, "rep", axis=0, tiled=True) for n, x in blocks.items()}, {}
+        return {n: functools.partial(gathered, x) for n, x in blocks.items()}, {}
     place = lax.axis_index("rep")
     z, even = place // 2, place % 2 == 0
     chain = {name: [block] for name, block in blocks.items()}
@@ -91,18 +108,16 @@
             value = in_order(held, z, rows) if len(held) == 4 else held[0]
             pairs = xor_perm(8, 1)
         if index >= WINDOW:
-            value = after(value, *steps[max(0, index - WINDOW - 2) : index - WINDOW + 1])
+            value = after(value, *steps[max(0, index - WINDOW - 3) : index - WINDOW + 1])
         got = lax.ppermute(value, "rep", pairs)
         steps.append(got)
         named[name, kind, len(held)] = got
         if kind == "z":
             held.append(got)
             if len(held) == 4 and held[0].shape[0] == 2 * rows:
-                result[name] = in_order(held, z, 2 * rows)
+                result[name] = functools.partial(finish_ring, held, z, 2 * rows)
         elif len(held) == 4:
-            value, got = value.reshape(4, rows, columns), got.reshape(4, rows, columns)
-            both = [jnp.where(even, value, got), jnp.where(even, got, value)]
-            result[name] = jnp.stack(both, axis=1).reshape(8 * rows, columns)
+            result[name] = functools.partial(finish_pair, value, got, even, rows)
         else:
             chain[name] = [
                 jnp.where(even, jnp.concatenate([value, got]), jnp.concatenate([got, value]))
@@ -131,23 +146,28 @@
     def entry(self, back):
         return lax.dynamic_index_in_dim(self.held, (self.z + 4 - back) % 4, axis=0, keepdims=False)
 
+    def pending(self):
+        if self.whole:
+            return self.total
+        if self.kinds[self.count] == "y":
+            return as_bf(lax.dynamic_index_in_dim(self.held, 1 - self.y, axis=self.axis, keepdims=False))
+        back = self.kinds[: self.count].count("z") + 1
+        value = self.entry(back)
+        return as_bf(value if back == 1 else value + self.got.astype(jnp.float32))
+
     def step(self, *ahead):
         if self.whole:
             return self.total
-        kind = self.kinds[self.count]
+        kind, value = self.kinds[self.count], self.pending()
         if kind == "z":
             back = self.kinds[: self.count].count("z") + 1
-            value = self.entry(back)
-            if back > 1:
-                value = value + self.got.astype(jnp.float32)
-            self.got = lax.ppermute(after(as_bf(value), *ahead), "rep", RING)
+            self.got = lax.ppermute(after(value, *ahead), "rep", RING)
             came = self.got
             if back == 3:
                 self.held = self.entry(0) + self.got.astype(jnp.float32)
                 self.axis = 0
         else:
-            value = lax.dynamic_index_in_dim(self.held, 1 - self.y, axis=self.axis, keepdims=False)
-            came = lax.ppermute(after(as_bf(value), *ahead), "rep", xor_perm(8, 1))
+            came = lax.ppermute(after(value, *ahead), "rep", xor_perm(8, 1))
             kept = lax.dynamic_index_in_dim(self.held, self.y, axis=self.axis, keepdims=False)
             self.held = kept + came.astype(jnp.float32)
         self.count += 1
@@ -294,8 +314,8 @@
 def probabilities(q_rot, k_rot, allowed):
     scores = jnp.where(allowed, dot_t(q_rot, k_rot), -1e30)
     peak = jnp.max(scores, axis=-1, keepdims=True)
-    log_total = peak + jnp.log(jnp.sum(jnp.exp(scores - peak), axis=-1, keepdims=True))
-    return jnp.exp(scores - log_total)
+    weights = jnp.exp(scores - peak)
+    return weights * (1.0 / jnp.sum(weights, axis=-1, keepdims=True))
 
 
 def block_rows(index, length):
@@ -363,9 +383,9 @@
                 probs = probabilities(q_rot, k_rot, allowed)
                 probs_bf = as_bf(probs)
                 d_att = datt_ref[rows, head_columns(head)]
-                attended = dot(probs_bf, v_bf)
-                delta = jnp.sum(d_att.astype(jnp.float32) * attended, axis=-1, keepdims=True)
-                d_scores = as_bf(probs * (dot_t(d_att, v_bf) - delta))
+                d_probs = dot_t(d_att, v_bf)
+                delta = jnp.sum(probs_bf.astype(jnp.float32) * d_probs, axis=-1, keepdims=True)
+                d_scores = as_bf(probs * (d_probs - delta))
                 d_values = d_values + t_dot(probs_bf, d_att)
                 d_krot = d_krot + t_dot(d_scores, q_rot)
                 upstream = dot(d_scores, k_rot) * SCALE
@@ -485,8 +505,7 @@
             "d": turned_down,
         }
     )
-    w_query, output, gate, up, down = (whole[n] for n in "qogud")
-    w_keys = whole["k"]
+    w_query, w_keys, output = (whole[n]() for n in "qko")
     gains = w_keys.reshape(-1, w_qkv.shape[0], w_keys.shape[1])
     gains = gains[:, 0, w_keys.shape[1] - 128 : w_keys.shape[1] - 128 + own]
     gains = gains.reshape(1, -1).astype(jnp.float32)
@@ -515,28 +534,31 @@
     cot_group = group_gather(after(out_cot, send))
     x_mid = x_float + group_sum(send, partial[1])
     mid_float, inv_mlp = rms_forward(x_mid, mlp_gain)
+    mid_bf = after(mid_float.astype(bf), *seen(("g", "z", 3), ("u", "z", 2)))
+    gate, up, down = (whole[n](mid_bf) for n in "gud")
     mid_normed, cot_all, hidden, d_gate, d_up, *partial = run_kernel(
         ffn_kernel,
         [((flat, D), bf), ((flat, D), bf)] + [((flat, half), bf)] * 3 + sent,
-        *group_gather(after(mid_float.astype(bf), *seen(("g", "z", 3), ("u", "z", 2)))),
+        *group_gather(mid_bf),
         *cot_group, gate, up, down,
     )
     rep_down = RepSum(dot(hidden.T, cot_all), True)
-    rep_up = RepSum(dot(mid_normed.T, d_up), True)
+    rep_up = RepSum(dot(mid_normed.T, d_up), False)
     rep_gate = RepSum(dot(mid_normed.T, d_gate), False)
     first = rep_down.step(), rep_gate.step(), rep_up.step()
     d_mid_norm = group_sum(*partial)
     d_mid_part, d_mlp_gain = rms_backward(x_mid, inv_mlp, mlp_gain, d_mid_norm)
     d_mid = out_cot.astype(jnp.float32) + d_mid_part
-    second = rep_down.step(), rep_up.step()
+    second = rep_down.step(), rep_gate.step()
     d_mid_bf = jnp.concatenate(group_gather(d_mid.astype(bf)))
     rep_out = RepSum(dot(attended_bf.T, d_mid_bf), False)
-    rep_down.step(d_mid_bf), rep_up.step(d_mid_bf), rep_gate.step(d_mid_bf), rep_out.step()
+    leaving = rep_down.pending(), rep_gate.pending(), rep_up.pending(), rep_out.pending()
+    rep_out.step(), rep_down.step(d_mid_bf), rep_gate.step(d_mid_bf), rep_up.step(d_mid_bf)
     d_query, d_keys, d_head_gains, d_attn_gain, *partial = run_kernel(
         attention_back_kernel,
         [((flat, wide), bf), ((flat, kv_width), bf), ((2, HEAD_SIZE), jnp.float32), ((1, D), jnp.float32)]
         + sent,
-        after(d_mid_bf, first[1], *second),
+        after(d_mid_bf, *leaving),
         *group, segment_group, gains, cosine, sine, queries, keys_values, w_query, w_keys, output,
         scratch=[pltpu.VMEM((flat, wide), bf)],
     )
@@ -547,10 +569,10 @@
     grad_keys = dot(normed.T, d_keys).reshape(gain_grads.shape[0], -1, kv_width)
     rep_keys = RepSum(jnp.concatenate([grad_keys, gain_grads], axis=1).reshape(-1, kv_width), True)
     rep_query = RepSum(dot(normed.T, d_query), False)
-    begun = rep_keys.step(), rep_query.step()
+    begun = rep_keys.step(rep_query.pending()), rep_query.step()
     for _ in range(3):
         rep_keys.step(), rep_query.step()
-    for ready in (rep_gate, rep_gate, rep_out, rep_up, rep_down, rep_out, rep_out):
+    for ready in (rep_gate, rep_up, rep_up, rep_out, rep_down, rep_out, rep_out):
         ready.step(begun[0])
     sum_keys, sum_query = rep_keys.total, rep_query.total
     group_rows = grad_keys.shape[1]

time: 328 us -> 323 us (0.985)
  starting transfers between devices: 78.3 us -> 74.9 us
    ppermute x24, waiting for transfers between devices: 62.4 us -> 70.9 us  [the longest x18 47.7 us: step(): self.got = lax.ppermute(after(value, *ahead), 'rep', RING)]
    ppermute x4, waiting for transfers between devices: 5.78 us -> 1.83 us  [group_gather(): far = lax.ppermute(part, 'shard', xor_perm(4, 2))]
    ppermute x4, waiting for transfers between devices: 0.43 us -> 4.35 us  [group_sum(): lax.ppermute(as_bf(keep[1] + near[0].astype(jnp.float32)), 'shard', xor_p...]
    ppermute x24, waiting for transfers between devices: 57.3 us -> 54 us  [gather_rep(): got = lax.ppermute(value, 'rep', pairs)]
    unnamed x166 -> x164, local copies, waits for them, and re-layouts: 12.9 us -> 10.2 us
  transfers between devices with their start and end apart: 84 -> 84, of which waited for: 38 -> 36; matrix products, arithmetic and copies ran while one was open for 16% -> 16% of each run, Pallas kernels for 9% -> 8%
where the time goes in v3:
time: 323 us; the launch traced here: 320 us
  waiting for transfers between devices  147 us (46%)
  starting transfers between devices  74.9 us (23%)
  Pallas kernels  33.7 us (10%)
  other arithmetic  30.9 us (10%)
  local copies, waits for them, and re-layouts  21.2 us (7%)
  matrix products  8.62 us (3%)
  between operations  3.51 us (1%)
    ppermute x24, waiting for transfers between devices, gather_rep(): got = lax.ppermute(value, 'rep', pairs)  54 us
    ppermute x18, waiting for transfers between devices, step(): self.got = lax.ppermute(after(value, *ahead), 'rep', RING)  47.7 us
    pallas_call x3, Pallas kernels, run_kernel(): pl.pallas_call(kernel, out_shape=[jax.ShapeDtypeStruct(shape, dtype) for...  33.7 us
    ppermute x24, starting transfers between devices, gather_rep(): got = lax.ppermute(value, 'rep', pairs)  24.4 us
    ppermute x6, waiting for transfers between devices, step(): came = lax.ppermute(after(value, *ahead), 'rep', xor_perm(8, 1))  23.2 us
    ppermute x12, waiting for transfers between devices, trade(): lax.ppermute(pieces(k), 'shard', xor_perm(4, k))  16.2 us
    ppermute x18, starting transfers between devices, step(): self.got = lax.ppermute(after(value, *ahead), 'rep', RING)  13.5 us
    ppermute x12, starting transfers between devices, trade(): lax.ppermute(pieces(k), 'shard', xor_perm(4, k))  11.9 us
  transfers between devices with their start and end apart: 84, of which 36 were waited for; matrix products, arithmetic and copies ran while one was open for 16% of the time, Pallas kernels for 8%

profile of v3, /device:TPU:0, one launch (start us, length us, event | category | flops | bytes accessed | tf_op | source)
XLA Modules:
  0.0 320.3 jit_solution(4142392588730628086)
XLA Ops:
  4.4 4.4 %collective-permute-start.2 = (bf16[32,1152]{1,0:T(8,128)(2,1)S(1)}, bf16[32,1152]{1,0:T(8,128)(2,1)S(1)}, u32[]{:S(2)}, u32[]{:S(2)}) collective-permute-start(bf16[32,1152]{1,0:T(8,128)(2,1)S(1)} %get-tuple-element.230), channel_id=1, source_target_pairs={{0,1},{1,0},{2,3},{3,2},{4,5},{5,4},{6,7},{7,6},{8,9},{9,8},{10,11... | collective-permute-start | bytes 221192 | tf_op jit(solution)/shard_map/ppermute | solution.py:189
  8.8 2.2 collective-permute-start
  11.6 5.2 %collective-permute-done = bf16[32,1152]{1,0:T(8,128)(2,1)S(1)} collective-permute-done((bf16[32,1152]{1,0:T(8,128)(2,1)S(1)}, bf16[32,1152]{1,0:T(8,128)(2,1)S(1)}, u32[]{:S(2)}, u32[]{:S(2)}) %collective-permute-start) | collective-permute-done | bytes 73760 | tf_op jit(solution)/shard_map/ppermute | solution.py:189
  18.7 2.5 collective-permute-start.13
  21.3 3.5 %collective-permute-done.13 = bf16[32,1536]{1,0:T(8,128)(2,1)S(1)} collective-permute-done((bf16[32,1536]{1,0:T(8,128)(2,1)S(1)}, bf16[32,1536]{1,0:T(8,128)(2,1)S(1)}, u32[]{:S(2)}, u32[]{:S(2)}) %collective-permute-start.13) | collective-permute-done | bytes 98336 | tf_op jit(solution)/shard_map/ppermute | solution.py:189
  27.3 3.0 collective-permute-start.15
  30.6 2.7 collective-permute-start.18
  33.3 2.8 collective-permute-start.5
  37.7 2.1 collective-permute-start.4
  39.8 7.5 %collective-permute-start.17 = (bf16[96,1024]{1,0:T(8,128)(2,1)S(1)}, bf16[96,1024]{1,0:T(8,128)(2,1)S(1)}, u32[]{:S(2)}, u32[]{:S(2)}) collective-permute-start(bf16[96,1024]{1,0:T(8,128)(2,1)S(1)} %collective-permute-done.16), channel_id=1, source_target_pairs={{0,8},{4,12},{8,16},{12,20},{16,24},{20,28},{24,0},{28,4},{1,9},{5... | collective-permute-start | bytes 589832 | tf_op jit(solution)/shard_map/ppermute | solution.py:112
  48.3 4.2 %collective-permute-done.17 = bf16[96,1024]{1,0:T(8,128)(2,1)S(1)} collective-permute-done((bf16[96,1024]{1,0:T(8,128)(2,1)S(1)}, bf16[96,1024]{1,0:T(8,128)(2,1)S(1)}, u32[]{:S(2)}, u32[]{:S(2)}) %collective-permute-start.17) | collective-permute-done | bytes 196640 | tf_op jit(solution)/shard_map/ppermute | solution.py:112
  52.6 2.5 collective-permute-start.21
  55.5 2.9 collective-permute-start.6
  58.4 6.9 %collective-permute-done.21 = bf16[64,1024]{1,0:T(8,128)(2,1)S(1)} collective-permute-done((bf16[64,1024]{1,0:T(8,128)(2,1)S(1)}, bf16[64,1024]{1,0:T(8,128)(2,1)S(1)}, u32[]{:S(2)}, u32[]{:S(2)}) %collective-permute-start.21) | collective-permute-done | bytes 131104 | tf_op jit(solution)/shard_map/ppermute | solution.py:112
  65.3 2.4 collective-permute-start.23
  67.9 4.3 %collective-permute-done.23 = bf16[64,1024]{1,0:T(8,128)(2,1)S(1)} collective-permute-done((bf16[64,1024]{1,0:T(8,128)(2,1)S(1)}, bf16[64,1024]{1,0:T(8,128)(2,1)S(1)}, u32[]{:S(2)}, u32[]{:S(2)}) %collective-permute-start.23) | collective-permute-done | bytes 131104 | tf_op jit(solution)/shard_map/ppermute | solution.py:112
  72.5 7.7 %collective-permute-done.11 = bf16[256,640]{1,0:T(8,128)(2,1)S(1)} collective-permute-done((bf16[256,640]{1,0:T(8,128)(2,1)S(1)}, bf16[256,640]{1,0:T(8,128)(2,1)S(1)}, u32[]{:S(2)}, u32[]{:S(2)}) %collective-permute-start.11) | collective-permute-done | bytes 327712 | tf_op jit(solution)/shard_map/ppermute | solution.py:112
  81.4 3.8 %collective-permute-start.28 = (bf16[256,768]{1,0:T(8,128)(2,1)}, bf16[256,768]{1,0:T(8,128)(2,1)}, u32[]{:S(2)}, u32[]{:S(2)}) collective-permute-start(bf16[256,768]{1,0:T(8,128)(2,1)} %maximum_select_fusion), channel_id=1, source_target_pairs={{0,8},{4,12},{8,16},{12,20},{16,24},{20,28},{24,0},{28,4},{1,9},{5... | collective-permute-start | bytes 1179656 | tf_op jit(solution)/shard_map/ppermute | solution.py:112
  86.5 7.5 %collective-permute-done.31 = bf16[96,1024]{1,0:T(8,128)(2,1)S(1)} collective-permute-done((bf16[96,1024]{1,0:T(8,128)(2,1)S(1)}, bf16[96,1024]{1,0:T(8,128)(2,1)S(1)}, u32[]{:S(2)}, u32[]{:S(2)}) %collective-permute-start.31) | collective-permute-done | bytes 196640 | tf_op jit(solution)/shard_map/ppermute | solution.py:112
  95.1 5.9 %collective-permute-done.19 = bf16[256,640]{1,0:T(8,128)(2,1)S(1)} collective-permute-done((bf16[256,640]{1,0:T(8,128)(2,1)S(1)}, bf16[256,640]{1,0:T(8,128)(2,1)S(1)}, u32[]{:S(2)}, u32[]{:S(2)}) %collective-permute-start.19) | collective-permute-done | bytes 327712 | tf_op jit(solution)/shard_map/ppermute | solution.py:112
  103.3 6.2 %collective-permute-done.28 = bf16[256,768]{1,0:T(8,128)(2,1)} collective-permute-done((bf16[256,768]{1,0:T(8,128)(2,1)}, bf16[256,768]{1,0:T(8,128)(2,1)}, u32[]{:S(2)}, u32[]{:S(2)}) %collective-permute-start.28) | collective-permute-done | bytes 393248 | tf_op jit(solution)/shard_map/ppermute | solution.py:112
  109.6 3.8 %collective-permute-done.27 = bf16[128,768]{1,0:T(8,128)(2,1)} collective-permute-done((bf16[128,768]{1,0:T(8,128)(2,1)}, bf16[128,768]{1,0:T(8,128)(2,1)}, u32[]{:S(2)}, u32[]{:S(2)}) %collective-permute-start.27) | collective-permute-done | bytes 196640 | tf_op jit(solution)/shard_map/ppermute | solution.py:112
  115.6 11.8 %shard_map.372 = (bf16[512,1024]{1,0:T(8,128)(2,1)S(1)}, f32[512,512]{1,0:T(8,128)S(1)}, f32[512,512]{1,0:T(8,128)S(1)}, bf16[512,512]{1,0:T(8,128)(2,1)S(1)}, b...) custom-call(bf16[144,1024]{1,0:T(8,128)(2,1)S(1)} %fusion.38.tok0, ...), custom_call_target="tpu_custom_call" | custom-call | tf_op jit(solution)/shard_map/pallas_call | solution.py:446
  130.1 2.0 collective-permute-start.30
  134.8 1.8 collective-permute-done.38.cot2
  136.6 4.3 %collective-permute-done.30 = bf16[128,1024]{1,0:T(8,128)(2,1)S(1)} collective-permute-done((bf16[128,1024]{1,0:T(8,128)(2,1)S(1)}, bf16[128,1024]{1,0:T(8,128)(2,1)S(1)}, u32[]{:S(2)}, u32[]{:S(2)}) %collective-permute-start.30) | collective-permute-done | bytes 262176 | tf_op jit(solution)/shard_map/ppermute | solution.py:53
  141.3 6.2 %collective-permute-done.41 = bf16[256,768]{1,0:T(8,128)(2,1)S(1)} collective-permute-done((bf16[256,768]{1,0:T(8,128)(2,1)S(1)}, bf16[256,768]{1,0:T(8,128)(2,1)S(1)}, u32[]{:S(2)}, u32[]{:S(2)}) %collective-permute-start.41) | collective-permute-done | bytes 393248 | tf_op jit(solution)/shard_map/ppermute | solution.py:112
  158.7 8.6 %shard_map.373 = (bf16[512,1024]{1,0:T(8,128)(2,1)S(1)}, bf16[512,1024]{1,0:T(8,128)(2,1)}, bf16[512,768]{1,0:T(8,128)(2,1)S(1)}, bf16[512,768]{1,0:T(8,128)(2,1...) custom-call(bf16[128,1024]{1,0:T(8,128)(2,1)S(1)} %multiply_convert_fusion.mn0, ...), custom_call_target="tpu_custom_call" | custom-call | tf_op jit(solution)/shard_map/pallas_call | solution.py:446
  167.3 2.3 fusion.98
  176.5 7.6 %collective-permute-done.48 = bf16[2,96,1024]{2,1,0:T(8,128)(2,1)S(1)} collective-permute-done((bf16[2,96,1024]{2,1,0:T(8,128)(2,1)S(1)}, bf16[2,96,1024]{2,1,0:T(8,128)(2,1)S(1)}, u32[]{:S(2)}, u32[]{:S(2)}) %collective-permute-start.48) | collective-permute-done | bytes 393248 | tf_op jit(solution)/shard_map/ppermute | solution.py:164
  185.9 6.5 %collective-permute-done.50 = bf16[4,128,768]{2,1,0:T(8,128)(2,1)S(1)} collective-permute-done((bf16[4,128,768]{2,1,0:T(8,128)(2,1)S(1)}, bf16[4,128,768]{2,1,0:T(8,128)(2,1)S(1)}, u32[]{:S(2)}, u32[]{:S(2)}) %collective-permute-start.50) | collective-permute-done | bytes 786464 | tf_op jit(solution)/shard_map/ppermute | solution.py:170
  193.1 15.7 %collective-permute-done.52 = bf16[4,128,768]{2,1,0:T(8,128)(2,1)S(1)} collective-permute-done((bf16[4,128,768]{2,1,0:T(8,128)(2,1)S(1)}, bf16[4,128,768]{2,1,0:T(8,128)(2,1)S(1)}, u32[]{:S(2)}, u32[]{:S(2)}) %collective-permute-start.52) | collective-permute-done | bytes 786464 | tf_op jit(solution)/shard_map/ppermute | solution.py:170
  214.0 2.5 collective-permute-start.73
  216.4 13.4 %shard_map.374 = (bf16[512,512]{1,0:T(8,128)(2,1)S(1)}, bf16[512,512]{1,0:T(8,128)(2,1)S(1)}, f32[2,128]{1,0:T(2,128)S(1)}, f32[1,1024]{1,0:T(1,128)S(1)}, bf16[...) custom-call(bf16[512,1024]{1,0:T(8,128)(2,1)S(1)} %pad_maximum_fusion.4.dmid_ref, ...), custom_call_target="tpu_custom_call" | custom-call | tf_op jit(solution)/shard_map/pallas_call | solution.py:446
  232.3 2.1 collective-permute-start.75
  234.5 1.8 fusion.102
  240.8 7.7 %collective-permute-done.53 = bf16[2,144,512]{2,1,0:T(8,128)(2,1)S(1)} collective-permute-done((bf16[2,144,512]{2,1,0:T(8,128)(2,1)S(1)}, bf16[2,144,512]{2,1,0:T(8,128)(2,1)S(1)}, u32[]{:S(2)}, u32[]{:S(2)}) %collective-permute-start.53) | collective-permute-done | bytes 294944 | tf_op jit(solution)/shard_map/ppermute | solution.py:164
  250.3 9.2 %collective-permute-done.76 = bf16[128,768]{1,0:T(8,128)(2,1)S(1)} collective-permute-done((bf16[128,768]{1,0:T(8,128)(2,1)S(1)}, bf16[128,768]{1,0:T(8,128)(2,1)S(1)}, u32[]{:S(2)}, u32[]{:S(2)}) %collective-permute-start.76) | collective-permute-done | bytes 196640 | tf_op jit(solution)/shard_map/ppermute | solution.py:164
  262.9 6.6 %collective-permute-done.62 = bf16[2,144,512]{2,1,0:T(8,128)(2,1)S(1)} collective-permute-done((bf16[2,144,512]{2,1,0:T(8,128)(2,1)S(1)}, bf16[2,144,512]{2,1,0:T(8,128)(2,1)S(1)}, u32[]{:S(2)}, u32[]{:S(2)}) %collective-permute-start.62) | collective-permute-done | bytes 294944 | tf_op jit(solution)/shard_map/ppermute | solution.py:164
  269.8 6.6 %collective-permute-done.69 = bf16[64,1024]{1,0:T(8,128)(2,1)S(1)} collective-permute-done((bf16[64,1024]{1,0:T(8,128)(2,1)S(1)}, bf16[64,1024]{1,0:T(8,128)(2,1)S(1)}, u32[]{:S(2)}, u32[]{:S(2)}) %collective-permute-start.69) | collective-permute-done | bytes 131104 | tf_op jit(solution)/shard_map/ppermute | solution.py:164
  277.9 2.4 collective-permute-start.70
  283.5 5.3 %collective-permute-done.70 = bf16[64,1024]{1,0:T(8,128)(2,1)S(1)} collective-permute-done((bf16[64,1024]{1,0:T(8,128)(2,1)S(1)}, bf16[64,1024]{1,0:T(8,128)(2,1)S(1)}, u32[]{:S(2)}, u32[]{:S(2)}) %collective-permute-start.70) | collective-permute-done | bytes 131104 | tf_op jit(solution)/shard_map/ppermute | solution.py:164
  290.3 1.8 collective-permute-start.63
  296.1 1.8 multiply_subtract_fusion
  300.8 1.8 collective-permute-start.55
  310.9 2.1 multiply_subtract_fusion.3
  312.9 1.8 fusion.30
  316.2 1.7 collective-permute-done.66
  (426 shorter events, 87.3 us)
Async XLA Ops:
  1.7 28.6 %collective-permute-start.9 = (bf16[64,1024]{1,0:T(8,128)(2,1)S(1)}, bf16[64,1024]{1,0:T(8,128)(2,1)S(1)}, u32[]{:S(2)}, u32[]{:S(2)}) collective-permute-start(bf16[64,1024]{1,0:T(8,128)(2,1)S(1)} %convert_element_type.358), channel_id=1, source_target_pairs={{0,0},{1,4},{2,8},{3,12},{4,16},{5,20},{6,24},{7,28},{8,1},{9,5},{... | collective-permute-start | bytes 393224 | tf_op jit(solution)/shard_map/ppermute | solution.py:494
  4.4 12.4 %collective-permute-start.2 = (bf16[32,1152]{1,0:T(8,128)(2,1)S(1)}, bf16[32,1152]{1,0:T(8,128)(2,1)S(1)}, u32[]{:S(2)}, u32[]{:S(2)}) collective-permute-start(bf16[32,1152]{1,0:T(8,128)(2,1)S(1)} %get-tuple-element.230), channel_id=1, source_target_pairs={{0,1},{1,0},{2,3},{3,2},{4,5},{5,4},{6,7},{7,6},{8,9},{9,8},{10,11... | collective-permute-start | bytes 221192 | tf_op jit(solution)/shard_map/ppermute | solution.py:189
  18.5 12.1 %collective-permute-start.3 = (bf16[128,512]{1,0:T(8,128)(2,1)S(1)}, bf16[128,512]{1,0:T(8,128)(2,1)S(1)}, u32[]{:S(2)}, u32[]{:S(2)}) collective-permute-start(bf16[128,512]{1,0:T(8,128)(2,1)S(1)} %pad_maximum_fusion.10), channel_id=1, source_target_pairs={{0,8},{4,12},{8,16},{12,20},{16,24},{20,28},{24,0},{28,4},{1,9},{5... | collective-permute-start | bytes 393224 | tf_op jit(solution)/shard_map/ppermute | solution.py:112
  21.2 12.0 %collective-permute-start.7 = (bf16[128,640]{1,0:T(8,128)(2,1)S(1)}, bf16[128,640]{1,0:T(8,128)(2,1)S(1)}, u32[]{:S(2)}, u32[]{:S(2)}) collective-permute-start(bf16[128,640]{1,0:T(8,128)(2,1)S(1)} %pad_maximum_fusion.7), channel_id=1, source_target_pairs={{0,4},{4,0},{8,12},{12,8},{16,20},{20,16},{24,28},{28,24},{1,5},{5... | collective-permute-start | bytes 491528 | tf_op jit(solution)/shard_map/ppermute | solution.py:112
  24.8 15.0 %collective-permute-start.16 = (bf16[96,1024]{1,0:T(8,128)(2,1)S(1)}, bf16[96,1024]{1,0:T(8,128)(2,1)S(1)}, u32[]{:S(2)}, u32[]{:S(2)}) collective-permute-start(bf16[96,1024]{1,0:T(8,128)(2,1)S(1)} %convert_element_type.360), channel_id=1, source_target_pairs={{0,0},{1,4},{2,8},{3,12},{4,16},{5,20},{6,24},{7,28},{8,1},{9,5},{... | collective-permute-start | bytes 589832 | tf_op jit(solution)/shard_map/ppermute | solution.py:496
  27.3 20.0 %collective-permute-start.15 = (bf16[128,768]{1,0:T(8,128)(2,1)S(1)}, bf16[128,768]{1,0:T(8,128)(2,1)S(1)}, u32[]{:S(2)}, u32[]{:S(2)}) collective-permute-start(bf16[128,768]{1,0:T(8,128)(2,1)S(1)} %get-tuple-element.197), channel_id=1, source_target_pairs={{0,4},{4,0},{8,12},{12,8},{16,20},{20,16},{24,28},{28,24},{1,5},{5... | collective-permute-start | bytes 589832 | tf_op jit(solution)/shard_map/ppermute | solution.py:112
  30.6 16.7 %collective-permute-start.18 = (bf16[128,512]{1,0:T(8,128)(2,1)S(1)}, bf16[128,512]{1,0:T(8,128)(2,1)S(1)}, u32[]{:S(2)}, u32[]{:S(2)}) collective-permute-start(bf16[128,512]{1,0:T(8,128)(2,1)S(1)} %collective-permute-done.3), channel_id=1, source_target_pairs={{0,8},{4,12},{8,16},{12,20},{16,24},{20,28},{24,0},{28,4},{1,9},{5... | collective-permute-start | bytes 393224 | tf_op jit(solution)/shard_map/ppermute | solution.py:112
  33.3 21.8 %collective-permute-start.5 = (bf16[144,1024]{1,0:T(8,128)(2,1)S(1)}, bf16[144,1024]{1,0:T(8,128)(2,1)S(1)}, u32[]{:S(2)}, u32[]{:S(2)}) collective-permute-start(bf16[144,1024]{1,0:T(8,128)(2,1)S(1)} %fusion.38.tok0), channel_id=1, source_target_pairs={{0,2},{1,3},{2,0},{3,1},{4,6},{5,7},{6,4},{7,5},{8,10},{9,11},{10,... | collective-permute-start | bytes 884744 | tf_op jit(solution)/shard_map/ppermute | solution.py:47
  37.7 30.0 %collective-permute-start.4 = (bf16[144,1024]{1,0:T(8,128)(2,1)S(1)}, bf16[144,1024]{1,0:T(8,128)(2,1)S(1)}, u32[]{:S(2)}, u32[]{:S(2)}) collective-permute-start(bf16[144,1024]{1,0:T(8,128)(2,1)S(1)} %fusion.38.tok0), channel_id=1, source_target_pairs={{0,1},{1,0},{2,3},{3,2},{4,5},{5,4},{6,7},{7,6},{8,9},{9,8},{10,11... | collective-permute-start | bytes 884744 | tf_op jit(solution)/shard_map/ppermute | solution.py:46
  39.8 12.8 %collective-permute-start.17 = (bf16[96,1024]{1,0:T(8,128)(2,1)S(1)}, bf16[96,1024]{1,0:T(8,128)(2,1)S(1)}, u32[]{:S(2)}, u32[]{:S(2)}) collective-permute-start(bf16[96,1024]{1,0:T(8,128)(2,1)S(1)} %collective-permute-done.16), channel_id=1, source_target_pairs={{0,8},{4,12},{8,16},{12,20},{16,24},{20,28},{24,0},{28,4},{1,9},{5... | collective-permute-start | bytes 589832 | tf_op jit(solution)/shard_map/ppermute | solution.py:112
  47.4 17.9 %collective-permute-start.8 = (bf16[256,640]{1,0:T(8,128)(2,1)S(1)}, bf16[256,640]{1,0:T(8,128)(2,1)S(1)}, u32[]{:S(2)}, u32[]{:S(2)}) collective-permute-start(bf16[256,640]{1,0:T(8,128)(2,1)S(1)} %maximum_select_fusion.1), channel_id=1, source_target_pairs={{0,8},{4,12},{8,16},{12,20},{16,24},{20,28},{24,0},{28,4},{1,9},{5... | collective-permute-start | bytes 983048 | tf_op jit(solution)/shard_map/ppermute | solution.py:112
  52.6 12.7 %collective-permute-start.21 = (bf16[64,1024]{1,0:T(8,128)(2,1)S(1)}, bf16[64,1024]{1,0:T(8,128)(2,1)S(1)}, u32[]{:S(2)}, u32[]{:S(2)}) collective-permute-start(bf16[64,1024]{1,0:T(8,128)(2,1)S(1)} %collective-permute-done.10), channel_id=1, source_target_pairs={{0,8},{4,12},{8,16},{12,20},{16,24},{20,28},{24,0},{28,4},{1,9},{5... | collective-permute-start | bytes 393224 | tf_op jit(solution)/shard_map/ppermute | solution.py:112
  55.1 25.2 %collective-permute-start.25 = (bf16[96,1024]{1,0:T(8,128)(2,1)S(1)}, bf16[96,1024]{1,0:T(8,128)(2,1)S(1)}, u32[]{:S(2)}, u32[]{:S(2)}) collective-permute-start(bf16[96,1024]{1,0:T(8,128)(2,1)S(1)} %collective-permute-done.17), channel_id=1, source_target_pairs={{0,8},{4,12},{8,16},{12,20},{16,24},{20,28},{24,0},{28,4},{1,9},{5... | collective-permute-start | bytes 589832 | tf_op jit(solution)/shard_map/ppermute | solution.py:112
  55.5 17.0 %collective-permute-start.6 = (bf16[144,1024]{1,0:T(8,128)(2,1)S(1)}, bf16[144,1024]{1,0:T(8,128)(2,1)S(1)}, u32[]{:S(2)}, u32[]{:S(2)}) collective-permute-start(bf16[144,1024]{1,0:T(8,128)(2,1)S(1)} %collective-permute-done.5.tok2), channel_id=1, source_target_pairs={{0,1},{1,0},{2,3},{3,2},{4,5},{5,4},{6,7},{7,6},{8,9},{9,8},{10,11... | collective-permute-start | bytes 884744 | tf_op jit(solution)/shard_map/ppermute | solution.py:48
  67.8 12.4 %collective-permute-start.11 = (bf16[256,640]{1,0:T(8,128)(2,1)S(1)}, bf16[256,640]{1,0:T(8,128)(2,1)S(1)}, u32[]{:S(2)}, u32[]{:S(2)}) collective-permute-start(bf16[256,640]{1,0:T(8,128)(2,1)S(1)} %collective-permute-done.8), channel_id=1, source_target_pairs={{0,8},{4,12},{8,16},{12,20},{16,24},{20,28},{24,0},{28,4},{1,9},{5... | collective-permute-start | bytes 983048 | tf_op jit(solution)/shard_map/ppermute | solution.py:112
  67.9 17.3 %collective-permute-start.22 = (bf16[512,512]{1,0:T(8,128)(2,1)S(1)}, bf16[512,512]{1,0:T(8,128)(2,1)S(1)}, u32[]{:S(2)}, u32[]{:S(2)}) collective-permute-start(bf16[512,512]{1,0:T(8,128)(2,1)S(1)} %constant_dynamic-slice_fusion.8), channel_id=1, source_target_pairs={{0,4},{4,0},{8,12},{12,8},{16,20},{20,16},{24,28},{28,24},{1,5},{5... | collective-permute-start | bytes 1572872 | tf_op jit(solution)/shard_map/ppermute | solution.py:112
  80.2 14.9 %collective-permute-start.26 = (bf16[128,768]{1,0:T(8,128)(2,1)S(1)}, bf16[128,768]{1,0:T(8,128)(2,1)}, u32[]{:S(2)}, u32[]{:S(2)}) collective-permute-start(bf16[128,768]{1,0:T(8,128)(2,1)S(1)} %copy-done.47), channel_id=1, source_target_pairs={{0,8},{4,12},{8,16},{12,20},{16,24},{20,28},{24,0},{28,4},{1,9},{5... | collective-permute-start | bytes 589832 | tf_op jit(solution)/shard_map/ppermute | solution.py:112
  81.3 12.7 %collective-permute-start.31 = (bf16[96,1024]{1,0:T(8,128)(2,1)S(1)}, bf16[96,1024]{1,0:T(8,128)(2,1)S(1)}, u32[]{:S(2)}, u32[]{:S(2)}) collective-permute-start(bf16[96,1024]{1,0:T(8,128)(2,1)S(1)} %collective-permute-done.25), channel_id=1, source_target_pairs={{0,8},{4,12},{8,16},{12,20},{16,24},{20,28},{24,0},{28,4},{1,9},{5... | collective-permute-start | bytes 589832 | tf_op jit(solution)/shard_map/ppermute | solution.py:112
  81.4 19.7 %collective-permute-start.19 = (bf16[256,640]{1,0:T(8,128)(2,1)S(1)}, bf16[256,640]{1,0:T(8,128)(2,1)S(1)}, u32[]{:S(2)}, u32[]{:S(2)}) collective-permute-start(bf16[256,640]{1,0:T(8,128)(2,1)S(1)} %collective-permute-done.11), channel_id=1, source_target_pairs={{0,8},{4,12},{8,16},{12,20},{16,24},{20,28},{24,0},{28,4},{1,9},{5... | collective-permute-start | bytes 983048 | tf_op jit(solution)/shard_map/ppermute | solution.py:112
  81.4 28.1 %collective-permute-start.28 = (bf16[256,768]{1,0:T(8,128)(2,1)}, bf16[256,768]{1,0:T(8,128)(2,1)}, u32[]{:S(2)}, u32[]{:S(2)}) collective-permute-start(bf16[256,768]{1,0:T(8,128)(2,1)} %maximum_select_fusion), channel_id=1, source_target_pairs={{0,8},{4,12},{8,16},{12,20},{16,24},{20,28},{24,0},{28,4},{1,9},{5... | collective-permute-start | bytes 1179656 | tf_op jit(solution)/shard_map/ppermute | solution.py:112
  85.2 24.4 %collective-permute-start.24 = (bf16[256,1024]{1,0:T(8,128)(2,1)S(1)}, bf16[256,1024]{1,0:T(8,128)(2,1)}, u32[]{:S(2)}, u32[]{:S(2)}) collective-permute-start(bf16[256,1024]{1,0:T(8,128)(2,1)S(1)} %constant_dynamic-slice_fusion.7), channel_id=1, source_target_pairs={{0,4},{4,0},{8,12},{12,8},{16,20},{20,16},{24,28},{28,24},{1,5},{5... | collective-permute-start | bytes 1572872 | tf_op jit(solution)/shard_map/ppermute | solution.py:112
  101.0 12.3 %collective-permute-start.27 = (bf16[128,768]{1,0:T(8,128)(2,1)}, bf16[128,768]{1,0:T(8,128)(2,1)}, u32[]{:S(2)}, u32[]{:S(2)}) collective-permute-start(bf16[128,768]{1,0:T(8,128)(2,1)} %collective-permute-done.26), channel_id=1, source_target_pairs={{0,8},{4,12},{8,16},{12,20},{16,24},{20,28},{24,0},{28,4},{1,9},{5... | collective-permute-start | bytes 589832 | tf_op jit(solution)/shard_map/ppermute | solution.py:112
  101.0 50.4 %collective-permute-start.42 = (bf16[384,1024]{1,0:T(8,128)(2,1)}, bf16[384,1024]{1,0:T(8,128)(2,1)}, u32[]{:S(2)}, u32[]{:S(2)}) collective-permute-start(bf16[384,1024]{1,0:T(8,128)(2,1)} %constant_dynamic-slice_fusion.4), channel_id=1, source_target_pairs={{0,4},{4,0},{8,12},{12,8},{16,20},{20,16},{24,28},{28,24},{1,5},{5... | collective-permute-start | bytes 2359304 | tf_op jit(solution)/shard_map/ppermute | solution.py:112
  109.6 24.5 %collective-permute-start.33 = (bf16[256,768]{1,0:T(8,128)(2,1)}, bf16[256,768]{1,0:T(8,128)(2,1)S(1)}, u32[]{:S(2)}, u32[]{:S(2)}) collective-permute-start(bf16[256,768]{1,0:T(8,128)(2,1)} %collective-permute-done.28), channel_id=1, source_target_pairs={{0,8},{4,12},{8,16},{12,20},{16,24},{20,28},{24,0},{28,4},{1,9},{5... | collective-permute-start | bytes 1179656 | tf_op jit(solution)/shard_map/ppermute | solution.py:112
  113.4 14.1 %collective-permute-start.32 = (bf16[128,768]{1,0:T(8,128)(2,1)}, bf16[128,768]{1,0:T(8,128)(2,1)S(1)}, u32[]{:S(2)}, u32[]{:S(2)}) collective-permute-start(bf16[128,768]{1,0:T(8,128)(2,1)} %collective-permute-done.27), channel_id=1, source_target_pairs={{0,8},{4,12},{8,16},{12,20},{16,24},{20,28},{24,0},{28,4},{1,9},{5... | collective-permute-start | bytes 589832 | tf_op jit(solution)/shard_map/ppermute | solution.py:112
  127.4 31.2 %collective-permute-start.37 = (bf16[128,1024]{1,0:T(8,128)(2,1)S(1)}, bf16[128,1024]{1,0:T(8,128)(2,1)S(1)}, u32[]{:S(2)}, u32[]{:S(2)}) collective-permute-start(bf16[128,1024]{1,0:T(8,128)(2,1)S(1)} %copy-done.1), channel_id=1, source_target_pairs={{0,1},{1,0},{2,3},{3,2},{4,5},{5,4},{6,7},{7,6},{8,9},{9,8},{10,11... | collective-permute-start | bytes 786440 | tf_op jit(solution)/shard_map/ppermute | solution.py:46
  134.0 22.6 %collective-permute-start.40 = (bf16[512,768]{1,0:T(8,128)(2,1)S(1)}, bf16[512,768]{1,0:T(8,128)(2,1)S(1)}, u32[]{:S(2)}, u32[]{:S(2)}) collective-permute-start(bf16[512,768]{1,0:T(8,128)(2,1)S(1)} %constant_dynamic-slice_fusion.6), channel_id=1, source_target_pairs={{0,4},{4,0},{8,12},{12,8},{16,20},{20,16},{24,28},{28,24},{1,5},{5... | collective-permute-start | bytes 2359304 | tf_op jit(solution)/shard_map/ppermute | solution.py:112
  140.9 17.7 %collective-permute-start.39 = (bf16[128,1024]{1,0:T(8,128)(2,1)S(1)}, bf16[128,1024]{1,0:T(8,128)(2,1)S(1)}, u32[]{:S(2)}, u32[]{:S(2)}) collective-permute-start(bf16[128,1024]{1,0:T(8,128)(2,1)S(1)} %collective-permute-done.38.cot2), channel_id=1, source_target_pairs={{0,1},{1,0},{2,3},{3,2},{4,5},{5,4},{6,7},{7,6},{8,9},{9,8},{10,11... | collective-permute-start | bytes 786440 | tf_op jit(solution)/shard_map/ppermute | solution.py:48
  170.7 13.4 %collective-permute-start.48 = (bf16[2,96,1024]{2,1,0:T(8,128)(2,1)S(1)}, bf16[2,96,1024]{2,1,0:T(8,128)(2,1)S(1)}, u32[]{:S(2)}, u32[]{:S(2)}) collective-permute-start(bf16[2,96,1024]{2,1,0:T(8,128)(2,1)S(1)} %fusion.32), channel_id=1, source_target_pairs={{0,8},{4,12},{8,16},{12,20},{16,24},{20,28},{24,0},{28,4},{1,9},{5... | collective-permute-start | bytes 1179656 | tf_op jit(solution)/shard_map/ppermute | solution.py:164
  171.9 20.5 %collective-permute-start.50 = (bf16[4,128,768]{2,1,0:T(8,128)(2,1)S(1)}, bf16[4,128,768]{2,1,0:T(8,128)(2,1)S(1)}, u32[]{:S(2)}, u32[]{:S(2)}) collective-permute-start(bf16[4,128,768]{2,1,0:T(8,128)(2,1)S(1)} %fusion), channel_id=1, source_target_pairs={{0,4},{4,0},{8,12},{12,8},{16,20},{20,16},{24,28},{28,24},{1,5},{5... | collective-permute-start | bytes 2359304 | tf_op jit(solution)/shard_map/ppermute | solution.py:170
  173.6 35.1 %collective-permute-start.52 = (bf16[4,128,768]{2,1,0:T(8,128)(2,1)S(1)}, bf16[4,128,768]{2,1,0:T(8,128)(2,1)S(1)}, u32[]{:S(2)}, u32[]{:S(2)}) collective-permute-start(bf16[4,128,768]{2,1,0:T(8,128)(2,1)S(1)} %fusion.1), channel_id=1, source_target_pairs={{0,4},{4,0},{8,12},{12,8},{16,20},{20,16},{24,28},{28,24},{1,5},{5... | collective-permute-start | bytes 2359304 | tf_op jit(solution)/shard_map/ppermute | solution.py:170
  184.2 24.7 %collective-permute-start.49 = (bf16[2,96,1024]{2,1,0:T(8,128)(2,1)S(1)}, bf16[2,96,1024]{2,1,0:T(8,128)(2,1)S(1)}, u32[]{:S(2)}, u32[]{:S(2)}) collective-permute-start(bf16[2,96,1024]{2,1,0:T(8,128)(2,1)S(1)} %fusion.2), channel_id=1, source_target_pairs={{0,8},{4,12},{8,16},{12,20},{16,24},{20,28},{24,0},{28,4},{1,9},{5... | collective-permute-start | bytes 1179656 | tf_op jit(solution)/shard_map/ppermute | solution.py:164
  185.6 24.4 %collective-permute-start.46 = (bf16[128,1024]{1,0:T(8,128)(2,1)S(1)}, bf16[128,1024]{1,0:T(8,128)(2,1)S(1)}, u32[]{:S(2)}, u32[]{:S(2)}) collective-permute-start(bf16[128,1024]{1,0:T(8,128)(2,1)S(1)} %get-tuple-element.170), channel_id=1, source_target_pairs={{0,2},{1,3},{2,0},{3,1},{4,6},{5,7},{6,4},{7,5},{8,10},{9,11},{10,... | collective-permute-start | bytes 786440 | tf_op jit(solution)/shard_map/ppermute | solution.py:47
  185.9 25.5 %collective-permute-start.45 = (bf16[128,1024]{1,0:T(8,128)(2,1)S(1)}, bf16[128,1024]{1,0:T(8,128)(2,1)S(1)}, u32[]{:S(2)}, u32[]{:S(2)}) collective-permute-start(bf16[128,1024]{1,0:T(8,128)(2,1)S(1)} %get-tuple-element.170), channel_id=1, source_target_pairs={{0,1},{1,0},{2,3},{3,2},{4,5},{5,4},{6,7},{7,6},{8,9},{9,8},{10,11... | collective-permute-start | bytes 786440 | tf_op jit(solution)/shard_map/ppermute | solution.py:46
  192.7 18.0 %collective-permute-start.51 = (bf16[128,768]{1,0:T(8,128)(2,1)S(1)}, bf16[128,768]{1,0:T(8,128)(2,1)S(1)}, u32[]{:S(2)}, u32[]{:S(2)}) collective-permute-start(bf16[128,768]{1,0:T(8,128)(2,1)S(1)} %fusion.48), channel_id=1, source_target_pairs={{0,8},{4,12},{8,16},{12,20},{16,24},{20,28},{24,0},{28,4},{1,9},{5... | collective-permute-start | bytes 589832 | tf_op jit(solution)/shard_map/ppermute | solution.py:164
  213.2 46.5 %collective-permute-start.68 = (bf16[4,64,1024]{2,1,0:T(8,128)(2,1)}, bf16[4,64,1024]{2,1,0:T(8,128)(2,1)}, u32[]{:S(2)}, u32[]{:S(2)}) collective-permute-start(bf16[4,64,1024]{2,1,0:T(8,128)(2,1)} %fusion.25), channel_id=1, source_target_pairs={{0,4},{4,0},{8,12},{12,8},{16,20},{20,16},{24,28},{28,24},{1,5},{5... | collective-permute-start | bytes 1572872 | tf_op jit(solution)/shard_map/ppermute | solution.py:170
  213.8 34.8 %collective-permute-start.81 = (bf16[2,96,1024]{2,1,0:T(8,128)(2,1)}, bf16[2,96,1024]{2,1,0:T(8,128)(2,1)}, u32[]{:S(2)}, u32[]{:S(2)}) collective-permute-start(bf16[2,96,1024]{2,1,0:T(8,128)(2,1)} %fusion.3), channel_id=1, source_target_pairs={{0,8},{4,12},{8,16},{12,20},{16,24},{20,28},{24,0},{28,4},{1,9},{5... | collective-permute-start | bytes 1179656 | tf_op jit(solution)/shard_map/ppermute | solution.py:164
  214.0 24.8 %collective-permute-start.73 = (bf16[128,768]{1,0:T(8,128)(2,1)}, bf16[128,768]{1,0:T(8,128)(2,1)}, u32[]{:S(2)}, u32[]{:S(2)}) collective-permute-start(bf16[128,768]{1,0:T(8,128)(2,1)} %fusion.37), channel_id=1, source_target_pairs={{0,8},{4,12},{8,16},{12,20},{16,24},{20,28},{24,0},{28,4},{1,9},{5... | collective-permute-start | bytes 589832 | tf_op jit(solution)/shard_map/ppermute | solution.py:164
  237.1 24.6 %collective-permute-start.58 = (bf16[4,128,512]{2,1,0:T(8,128)(2,1)S(1)}, bf16[4,128,512]{2,1,0:T(8,128)(2,1)S(1)}, u32[]{:S(2)}, u32[]{:S(2)}) collective-permute-start(bf16[4,128,512]{2,1,0:T(8,128)(2,1)S(1)} %fusion.26), channel_id=1, source_target_pairs={{0,4},{4,0},{8,12},{12,8},{16,20},{20,16},{24,28},{28,24},{1,5},{5... | collective-permute-start | bytes 1572872 | tf_op jit(solution)/shard_map/ppermute | solution.py:170
  240.7 20.8 %collective-permute-start.56 = (bf16[2,128,1024]{2,1,0:T(8,128)(2,1)S(1)}, bf16[2,128,1024]{2,1,0:T(8,128)(2,1)S(1)}, u32[]{:S(2)}, u32[]{:S(2)}) collective-permute-start(bf16[2,128,1024]{2,1,0:T(8,128)(2,1)S(1)} %copy-done.8), channel_id=1, source_target_pairs={{0,1},{1,0},{2,3},{3,2},{4,5},{5,4},{6,7},{7,6},{8,9},{9,8},{10,11... | collective-permute-start | bytes 1572872 | tf_op jit(solution)/shard_map/ppermute | solution.py:52
  259.6 39.9 %collective-permute-start.54 = (bf16[2,128,1024]{2,1,0:T(8,128)(2,1)S(1)}, bf16[2,128,1024]{2,1,0:T(8,128)(2,1)S(1)}, u32[]{:S(2)}, u32[]{:S(2)}) collective-permute-start(bf16[2,128,1024]{2,1,0:T(8,128)(2,1)S(1)} %copy-done.38), channel_id=1, source_target_pairs={{0,1},{1,0},{2,3},{3,2},{4,5},{5,4},{6,7},{7,6},{8,9},{9,8},{10,11... | collective-permute-start | bytes 1572872 | tf_op jit(solution)/shard_map/ppermute | solution.py:52
  261.5 18.7 %collective-permute-start.77 = (bf16[128,768]{1,0:T(8,128)(2,1)S(1)}, bf16[128,768]{1,0:T(8,128)(2,1)S(1)}, u32[]{:S(2)}, u32[]{:S(2)}) collective-permute-start(bf16[128,768]{1,0:T(8,128)(2,1)S(1)} %fusion.35), channel_id=1, source_target_pairs={{0,8},{4,12},{8,16},{12,20},{16,24},{20,28},{24,0},{28,4},{1,9},{5... | collective-permute-start | bytes 589832 | tf_op jit(solution)/shard_map/ppermute | solution.py:164
  261.7 20.4 %collective-permute-start.57 = (bf16[128,1024]{1,0:T(8,128)(2,1)S(1)}, bf16[128,1024]{1,0:T(8,128)(2,1)S(1)}, u32[]{:S(2)}, u32[]{:S(2)}) collective-permute-start(bf16[128,1024]{1,0:T(8,128)(2,1)S(1)} %fusion.42), channel_id=1, source_target_pairs={{0,2},{1,3},{2,0},{3,1},{4,6},{5,7},{6,4},{7,5},{8,10},{9,11},{10,... | collective-permute-start | bytes 786440 | tf_op jit(solution)/shard_map/ppermute | solution.py:53
  276.5 21.4 %collective-permute-start.83 = (bf16[96,1024]{1,0:T(8,128)(2,1)S(1)}, bf16[96,1024]{1,0:T(8,128)(2,1)S(1)}, u32[]{:S(2)}, u32[]{:S(2)}) collective-permute-start(bf16[96,1024]{1,0:T(8,128)(2,1)S(1)} %fusion.33), channel_id=1, source_target_pairs={{0,0},{4,1},{8,2},{12,3},{16,4},{20,5},{24,6},{28,7},{1,8},{5,9},{... | collective-permute-start | bytes 589832 | tf_op jit(solution)/shard_map/ppermute | solution.py:590
  290.3 12.4 %collective-permute-start.63 = (bf16[2,144,512]{2,1,0:T(8,128)(2,1)S(1)}, bf16[2,144,512]{2,1,0:T(8,128)(2,1)S(1)}, u32[]{:S(2)}, u32[]{:S(2)}) collective-permute-start(bf16[2,144,512]{2,1,0:T(8,128)(2,1)S(1)} %fusion.16), channel_id=1, source_target_pairs={{0,8},{4,12},{8,16},{12,20},{16,24},{20,28},{24,0},{28,4},{1,9},{5... | collective-permute-start | bytes 884744 | tf_op jit(solution)/shard_map/ppermute | solution.py:164
  292.9 12.0 %collective-permute-start.71 = (bf16[64,1024]{1,0:T(8,128)(2,1)S(1)}, bf16[64,1024]{1,0:T(8,128)(2,1)S(1)}, u32[]{:S(2)}, u32[]{:S(2)}) collective-permute-start(bf16[64,1024]{1,0:T(8,128)(2,1)S(1)} %fusion.44), channel_id=1, source_target_pairs={{0,8},{4,12},{8,16},{12,20},{16,24},{20,28},{24,0},{28,4},{1,9},{5... | collective-permute-start | bytes 393224 | tf_op jit(solution)/shard_map/ppermute | solution.py:164
  295.0 12.3 %collective-permute-start.61 = (bf16[128,512]{1,0:T(8,128)(2,1)S(1)}, bf16[128,512]{1,0:T(8,128)(2,1)S(1)}, u32[]{:S(2)}, u32[]{:S(2)}) collective-permute-start(bf16[128,512]{1,0:T(8,128)(2,1)S(1)} %fusion.47), channel_id=1, source_target_pairs={{0,8},{4,12},{8,16},{12,20},{16,24},{20,28},{24,0},{28,4},{1,9},{5... | collective-permute-start | bytes 393224 | tf_op jit(solution)/shard_map/ppermute | solution.py:164
  300.8 12.1 %collective-permute-start.55 = (bf16[128,1024]{1,0:T(8,128)(2,1)}, bf16[128,1024]{1,0:T(8,128)(2,1)}, u32[]{:S(2)}, u32[]{:S(2)}) collective-permute-start(bf16[128,1024]{1,0:T(8,128)(2,1)} %fusion.27), channel_id=1, source_target_pairs={{0,2},{1,3},{2,0},{3,1},{4,6},{5,7},{6,4},{7,5},{8,10},{9,11},{10,... | collective-permute-start | bytes 786440 | tf_op jit(solution)/shard_map/ppermute | solution.py:53
  (91 other events, 756.0 us)
